TPU v7x, 256 devices: a whole 4x4x8 slice. The times are simulated.
256 devices in a mesh: ctx: 32 (over y, z_lo, core), tp: 8 (over z_hi, x).
Axes of the slice: x: 4, y: 4, z: 8 (z_hi: 2, z_lo: 4; z = z_hi * 4 + z_lo), core: 2. Of those that a mesh axis runs over, the one named last changes fastest.
Arguments:
- query_self: bfloat16 [4096, 8192], P('ctx', 'tp'), may hold values from -120 to 120
- key_self: bfloat16 [4096, 1024], P('ctx', 'tp'), may hold values from -6 to 6
- value_self: bfloat16 [4096, 1024], P('ctx', 'tp'), may hold values from -6 to 6
- grad_self: bfloat16 [4096, 8192], P('ctx', 'tp'), may hold values from -6 to 6
- document_id: int32 [4096], replicated, may hold values from 0 to 15, never falling along the last dimension, each value on 1 to 2176 neighbouring positions
- query_cross: bfloat16 [4096, 8192], P('ctx', 'tp'), may hold values from -120 to 120
- image_keys: bfloat16 [2048, 1024], P('ctx', 'tp'), may hold values from -6 to 6
- image_values: bfloat16 [2048, 1024], P('ctx', 'tp'), may hold values from -6 to 6
- grad_cross: bfloat16 [4096, 8192], P('ctx', 'tp'), may hold values from -6 to 6
- image_block: int32 [4096], P('ctx'), may hold values from 0 to 3, never falling along the last dimension, each value on 1 to 2048 neighbouring positions
- gate: float32 [1], replicated, may hold values from 0.2 to 1.2
- w_key: bfloat16 [8192, 1024], P(None, 'tp'), may hold values from -0.0625 to 0.0625
- w_value: bfloat16 [8192, 1024], P(None, 'tp'), may hold values from -0.0625 to 0.0625
Outputs:
- query_grad: bfloat16 [4096, 8192], P('ctx', 'tp')
- key_grad: bfloat16 [4096, 1024], P('ctx', 'tp')
- value_grad: bfloat16 [4096, 1024], P('ctx', 'tp')
- input_grad: bfloat16 [4096, 8192], P('ctx', 'tp')
- cross_query_grad: bfloat16 [4096, 8192], P('ctx', 'tp')
- image_key_grad: bfloat16 [2048, 1024], P('ctx', 'tp')
- image_value_grad: bfloat16 [2048, 1024], P('ctx', 'tp')
- gate_grad: float32 [1], replicated
Inputs may be any that keep to these rules, and one draw needn't show every extreme that they name: document_id never falls along the sequence, every document holds at most 2176 tokens, and one holds exactly that many.
All inputs are finite; a program needn't handle non-finite values.
Results may differ from a plain program's by a relative error of at most 0.013.
Values may be sent and summed in bfloat16 or wider, within the bound.
No kernel may reach another device: no remote copies, remote signals or barrier semaphores. Data moves between devices by JAX's collectives and lax.ppermute only.
A program may use at most 128 MiB of HBM per device.

v0:
```python
import math

import jax
import jax.numpy as jnp
from jax import lax
from jax.sharding import PartitionSpec as P

DH = 128
GROUP = 8
NIMG = 4


NEG_FILL = -1e30


def local(
    query_self,
    key_self,
    value_self,
    grad_self,
    document_id,
    query_cross,
    image_keys,
    image_values,
    grad_cross,
    image_block,
    gate,
    w_key,
    w_value,
):
    local_rows = query_self.shape[0]
    ctx_count = lax.axis_size("ctx")
    seq_len = local_rows * ctx_count
    score_scale = DH ** (-0.5)
    first_row = lax.axis_index("ctx") * local_rows
    last_row = first_row + local_rows - 1
    tanh_gate = jnp.tanh(gate[0])
    query_heads = query_self.reshape(local_rows, GROUP, DH)
    grad_heads = grad_self.reshape(local_rows, GROUP, DH)
    query_pos = first_row + jnp.arange(local_rows, dtype=jnp.int32)
    query_doc = lax.dynamic_slice_in_dim(document_id, first_row, local_rows, 0)
    first_doc = query_doc[0]

    def masked_scores(key_rows, value_rows, key_start):
        width_keys = key_rows.shape[0]
        key_pos = key_start + jnp.arange(width_keys, dtype=jnp.int32)
        key_doc = lax.dynamic_slice_in_dim(document_id, key_start, width_keys, 0)
        allowed = (
            (key_pos[None, :] <= query_pos[:, None]) & (key_doc[None, :] == query_doc[:, None])
        )[None]
        scores = (
            jnp.einsum("qhd,kd->hqk", query_heads, key_rows, preferred_element_type=jnp.float32)
            * score_scale
        )
        scores = jnp.where(allowed, scores, NEG_FILL)
        dprob = jnp.einsum(
            "qhd,kd->hqk", grad_heads, value_rows, preferred_element_type=jnp.float32
        )
        return (allowed, scores, dprob)

    def run_blocks(block_fn, state, key_all, value_all):
        width_keys = key_all.shape[0]
        key_block = math.gcd(width_keys, 1024)

        def one_block(block_index, inner):
            local_start = block_index * key_block
            key_rows = lax.dynamic_slice_in_dim(key_all, local_start, key_block, 0)
            value_rows = lax.dynamic_slice_in_dim(value_all, local_start, key_block, 0)
            doc_last = lax.dynamic_index_in_dim(
                document_id, local_start + key_block - 1, 0, keepdims=False
            )
            live = (local_start <= last_row) & (doc_last >= first_doc)
            return lax.cond(
                live,
                lambda held: block_fn(held, key_rows, value_rows, local_start),
                lambda held: held,
                inner,
            )

        return lax.fori_loop(0, width_keys // key_block, one_block, state)

    def forward_block(state, key_rows, value_rows, key_start):
        row_peak, row_total, row_dot = state
        allowed, scores, dprob = masked_scores(key_rows, value_rows, key_start)
        new_peak = jnp.maximum(row_peak, jnp.max(scores, axis=-1))
        factor = jnp.exp(row_peak - new_peak)
        weights = jnp.where(allowed, jnp.exp(scores - new_peak[..., None]), 0.0)
        return (
            new_peak,
            row_total * factor + jnp.sum(weights, axis=-1),
            row_dot * factor + jnp.sum(weights * dprob, axis=-1),
        )

    zero_stats = jnp.zeros((GROUP, local_rows), jnp.float32)
    stat_init = (jnp.full((GROUP, local_rows), NEG_FILL, jnp.float32), zero_stats, zero_stats)
    shard_pair = (
        lax.all_gather(key_self, "ctx", axis=0, tiled=True),
        lax.all_gather(value_self, "ctx", axis=0, tiled=True),
    )
    row_peak, row_total, row_dot = run_blocks(
        forward_block, stat_init, shard_pair[0], shard_pair[1]
    )
    log_sum = row_peak + jnp.log(row_total)
    row_delta = row_dot / row_total

    def backward_block(state, key_rows, value_rows, key_start):
        query_acc, key_acc, value_acc = state
        allowed, scores, dprob = masked_scores(key_rows, value_rows, key_start)
        prob = jnp.where(allowed, jnp.exp(scores - log_sum[..., None]), 0.0)
        prob_half = prob.astype(jnp.bfloat16)
        dscore = (prob * (dprob - row_delta[..., None])).astype(jnp.bfloat16)
        query_acc = query_acc + jnp.einsum(
            "hqk,kd->qhd", dscore, key_rows, preferred_element_type=jnp.float32
        )
        key_part = jnp.einsum(
            "hqk,qhd->kd", dscore, query_heads, preferred_element_type=jnp.float32
        )
        value_part = jnp.einsum(
            "hqk,qhd->kd", prob_half, grad_heads, preferred_element_type=jnp.float32
        )
        width_keys = key_rows.shape[0]
        key_old = lax.dynamic_slice_in_dim(key_acc, key_start, width_keys, 0)
        value_old = lax.dynamic_slice_in_dim(value_acc, key_start, width_keys, 0)
        key_acc = lax.dynamic_update_slice_in_dim(key_acc, key_old + key_part, key_start, 0)
        value_acc = lax.dynamic_update_slice_in_dim(value_acc, value_old + value_part, key_start, 0)
        return (query_acc, key_acc, value_acc)

    zero_keys = jnp.zeros((seq_len, DH), jnp.float32)
    grad_init = (jnp.zeros((local_rows, GROUP, DH), jnp.float32), zero_keys, zero_keys)
    shard_pair = (
        lax.all_gather(key_self, "ctx", axis=0, tiled=True),
        lax.all_gather(value_self, "ctx", axis=0, tiled=True),
    )
    query_acc, key_acc, value_acc = run_blocks(
        backward_block, grad_init, shard_pair[0], shard_pair[1]
    )
    key_sum = lax.psum_scatter(key_acc, "ctx", scatter_dimension=0, tiled=True)
    value_sum = lax.psum_scatter(value_acc, "ctx", scatter_dimension=0, tiled=True)
    key_grad = (key_sum * score_scale).astype(jnp.bfloat16)
    value_grad = value_sum.astype(jnp.bfloat16)
    query_grad = (query_acc * score_scale).astype(jnp.bfloat16).reshape(local_rows, GROUP * DH)
    input_part = jnp.einsum("sn,dn->sd", key_grad, w_key, preferred_element_type=jnp.float32)
    input_part = input_part + jnp.einsum(
        "sn,dn->sd", value_grad, w_value, preferred_element_type=jnp.float32
    )
    input_grad = lax.psum_scatter(
        input_part.astype(jnp.bfloat16), "tp", scatter_dimension=1, tiled=True
    )
    self_out = (query_grad, key_grad, value_grad, input_grad)
    image_key_all = lax.all_gather(image_keys, "ctx", axis=0, tiled=True)
    image_value_all = lax.all_gather(image_values, "ctx", axis=0, tiled=True)
    image_total = image_key_all.shape[0]
    image_of_key = jnp.arange(image_total, dtype=jnp.int32) // (image_total // NIMG)
    cross_heads = query_cross.reshape(local_rows, GROUP, DH)
    cross_grad_heads = grad_cross.reshape(local_rows, GROUP, DH)
    allowed = (image_of_key[None, :] <= image_block[:, None])[None]
    scores = (
        jnp.einsum("qhd,kd->hqk", cross_heads, image_key_all, preferred_element_type=jnp.float32)
        * score_scale
    )
    scores = jnp.where(allowed, scores, NEG_FILL)
    row_peak = jnp.max(scores, axis=-1)
    weights = jnp.where(allowed, jnp.exp(scores - row_peak[..., None]), 0.0)
    prob = weights / jnp.sum(weights, axis=-1)[..., None]
    dprob = jnp.einsum(
        "qhd,kd->hqk", cross_grad_heads, image_value_all, preferred_element_type=jnp.float32
    )
    row_dot = jnp.sum(prob * dprob, axis=-1)
    dscore = (prob * (tanh_gate * (dprob - row_dot[..., None]))).astype(jnp.bfloat16)
    prob_half = prob.astype(jnp.bfloat16)
    cross_query = (
        jnp.einsum("hqk,kd->qhd", dscore, image_key_all, preferred_element_type=jnp.float32)
        * score_scale
    )
    cross_query_grad = cross_query.astype(jnp.bfloat16).reshape(local_rows, GROUP * DH)
    key_part = jnp.einsum("hqk,qhd->kd", dscore, cross_heads, preferred_element_type=jnp.float32)
    value_part = jnp.einsum(
        "hqk,qhd->kd", prob_half, cross_grad_heads, preferred_element_type=jnp.float32
    )
    key_own = lax.psum_scatter(key_part, "ctx", scatter_dimension=0, tiled=True)
    value_own = lax.psum_scatter(value_part, "ctx", scatter_dimension=0, tiled=True)
    gate_total = lax.psum(jnp.sum(row_dot), ("ctx", "tp"))
    image_key_grad = (key_own * score_scale).astype(jnp.bfloat16)
    image_value_grad = (value_own * tanh_gate).astype(jnp.bfloat16)
    gate_grad = ((1.0 - tanh_gate * tanh_gate) * gate_total).reshape(1)
    cross_out = (cross_query_grad, image_key_grad, image_value_grad, gate_grad)
    return self_out + cross_out


def solution(mesh):
    in_specs = (
        P("ctx", "tp"),
        P("ctx", "tp"),
        P("ctx", "tp"),
        P("ctx", "tp"),
        P(),
        P("ctx", "tp"),
        P("ctx", "tp"),
        P("ctx", "tp"),
        P("ctx", "tp"),
        P("ctx"),
        P(),
        P(None, "tp"),
        P(None, "tp"),
    )
    out_specs = (
        P("ctx", "tp"),
        P("ctx", "tp"),
        P("ctx", "tp"),
        P("ctx", "tp"),
        P("ctx", "tp"),
        P("ctx", "tp"),
        P("ctx", "tp"),
        P(),
    )
    return jax.shard_map(local, mesh=mesh, in_specs=in_specs, out_specs=out_specs, check_vma=False)
```

profile of v0, /device:TPU:8, one launch (start us, length us, event | category | flops | bytes accessed | tf_op | source)
XLA Modules:
  0.0 896.9 jit_solution(14027753186955597932)
XLA Ops:
  12.1 59.1 %all-gather.3.cloned.1.call-done = bf16[4096,128]{1,0:T(8,128)(2,1)} async-done(((bf16[128,128]{1,0:T(8,128)(2,1)}), bf16[4096,128]{1,0:T(8,128)(2,1)}) %all-gather.3.cloned.1.call-update) | async-done | bytes 1048592 | tf_op jit(solution)/shard_map/all_gather | solution.py:131
  71.2 59.5 %all-gather.5.cloned.1.call-done = bf16[4096,128]{1,0:T(8,128)(2,1)} async-done(((bf16[128,128]{1,0:T(8,128)(2,1)}), bf16[4096,128]{1,0:T(8,128)(2,1)}) %all-gather.5.cloned.1.call-update) | async-done | bytes 1048592 | tf_op jit(solution)/shard_map/all_gather | solution.py:132
  130.7 20.3 %while.44 = (s32[]{:T(128)}, f32[8,128]{1,0:T(8,128)S(1)}, f32[8,128]{1,0:T(8,128)S(1)}, f32[8,128]{1,0:T(8,128)S(1)}, s32[]{:T(128)}, /*index=5*/s32[4096]{0:T(...) while((s32[]{:T(128)}, f32[8,128]{1,0:T(8,128)S(1)}, ...), condition=%wide.region_6.7_spmd.clone, body=%wide.region_0.6_spmd.clone.sunk | while | flops 551948416 | bytes 14253011 | solution.py:80
  130.7 1.3 dynamic_slice.139
  132.6 6.2 conditional.6
  133.7 1.7 fusion.5
  136.4 2.3 fusion.4
  138.8 1.3 dynamic_slice.139
  140.8 6.2 conditional.6
  141.8 1.7 fusion.5
  144.6 2.3 fusion.4
  147.0 1.3 dynamic_slice.139
  149.0 1.3 dynamic_slice.139
  151.0 1.5 broadcast_in_dim.102
  152.4 1.4 broadcast_in_dim.102.clone
  153.9 32.8 %while.45 = (s32[]{:T(128)}, f32[128,8,128]{2,0,1:T(8,128)S(1)}, f32[4096,128]{1,0:T(8,128)}, f32[4096,128]{1,0:T(8,128)}, s32[]{:T(128)}, /*index=5*/s32[4096]{...) while((s32[]{:T(128)}, f32[128,8,128]{2,0,1:T(8,128)S(1)}, ...), condition=%wide.region_10.11_spmd.clone, body=%wide.region_7.10_spmd.clone.sunk | while | flops 1355547776 | bytes 24284160 | solution.py:80
  153.9 1.3 dynamic_slice.140
  155.9 12.4 %conditional.7 = ((f32[128,8,128]{2,0,1:T(8,128)S(1)}, f32[4096,128]{1,0:T(8,128)}, f32[4096,128]{1,0:T(8,128)})) conditional(s32[]{:T(128)} %convert_element_type.110, (f32[128,8,128]{2,0,1:T(8,128)S(1)}, f32[4096,128]{1,0:T(8,128)}, f32[4096,128]{1,0:T(8,128)}) %tuple.148, (s32[]{:T(128)}, s32[]{:T(128)}, s32[4096]{0:T(1024)}, s32[128]{0:T(128)S(1)}, ...), branch_computations={%region_8.8_spmd, %region_9.9_spmd} | conditional | flops 1355547776 | bytes 24283234 | solution.py:73
  157.0 1.7 fusion.37
  158.6 2.5 fusion.15
  161.1 2.6 fusion.34
  163.7 1.7 fusion.26
  165.4 2.9 fusion.30
  168.3 1.3 dynamic_slice.140
  170.3 12.5 %conditional.7 = ((f32[128,8,128]{2,0,1:T(8,128)S(1)}, f32[4096,128]{1,0:T(8,128)}, f32[4096,128]{1,0:T(8,128)})) conditional(s32[]{:T(128)} %convert_element_type.110, (f32[128,8,128]{2,0,1:T(8,128)S(1)}, f32[4096,128]{1,0:T(8,128)}, f32[4096,128]{1,0:T(8,128)}) %tuple.148, (s32[]{:T(128)}, s32[]{:T(128)}, s32[4096]{0:T(1024)}, s32[128]{0:T(128)S(1)}, ...), branch_computations={%region_8.8_spmd, %region_9.9_spmd} | conditional | flops 1355547776 | bytes 24283234 | solution.py:73
  171.3 1.7 fusion.37
  173.0 2.5 fusion.15
  175.5 2.6 fusion.34
  178.1 1.7 fusion.26
  179.8 2.9 fusion.30
  182.7 1.3 dynamic_slice.140
  184.7 1.3 dynamic_slice.140
  188.1 50.5 %all_gather.16 = bf16[2048,128]{1,0:T(8,128)(2,1)S(1)} all-gather(bf16[64,128]{1,0:T(8,128)(2,1)S(1)} %copy-done.4), channel_id=1, replica_groups=mesh['ctx'=32,'tp'=8] {'ctx'}, dimensions={0}, use_global_device_ids=true | all-gather | bytes 540672 | tf_op jit(solution)/shard_map/all_gather | solution.py:150
  238.6 43.4 %all_gather.17 = bf16[2048,128]{1,0:T(8,128)(2,1)} all-gather(bf16[64,128]{1,0:T(8,128)(2,1)S(1)} %copy-done.5), channel_id=1, replica_groups=mesh['ctx'=32,'tp'=8] {'ctx'}, dimensions={0}, use_global_device_ids=true | all-gather | bytes 540672 | tf_op jit(solution)/shard_map/all_gather | solution.py:151
  282.3 7.5 fusion.99
  289.8 9.8 %fusion.96 = (f32[]{:T(128)}, f32[2048,128,8]{1,0,2:T(8,128)}) fusion(f32[8,128,2048]{1,2,0:T(8,128)} %get-tuple-element.1403, f32[8,128]{1,0:T(8,128)S(1)} %get-tuple-element.1402, bf16[2048,128]{1,0:T(8,128)(2,1)} %all_gather.17, bf16[128,1024]{1,0:T(8,128)(2,1)} %param.29), kind=kOutput, calls=%fused_computation.111 | convolution fusion | flops 543162368 | bytes 17567748 | tf_op jit(solution)/shard_map/qhd,kd->hqk/dot_general | solution.py:165
  299.6 14.0 %convolution_bitcast_fusion.2 = f32[2048,128]{1,0:T(8,128)} fusion(f32[2048,128,8]{1,0,2:T(8,128)} %get-tuple-element.1405, f32[]{:T(128)} %bitcast.16, f32[8,128,2048]{1,2,0:T(8,128)} %get-tuple-element.1403, f32[8,128]{1,0:T(8,128)S(1)} %get-tuple-element.1402, bf16[128,1024]{1,0:T(8,128)(2,1)S(1)} %copy-done.7), kind=kOutput, calls=%fused_computation.74 | convolution fusion | flops 551554048 | bytes 18092036 | tf_op jit(solution)/shard_map/hqk,qhd->kd/dot_general | solution.py:176
  313.6 5.7 fusion.60
  319.4 14.3 %reduce-scatter.8.cloned.1.call-done = f32[128,128]{1,0:T(8,128)} async-done(((f32[4096,128]{1,0:T(8,128)}), f32[128,128]{1,0:T(8,128)}) %reduce-scatter.8.cloned.1.call-update) | async-done | bytes 65552 | tf_op jit(solution)/shard_map/reduce_scatter | solution.py:138
  334.6 146.9 %reduce-scatter.6.cloned.1.call-done = f32[128,128]{1,0:T(8,128)} async-done(((f32[4096,128]{1,0:T(8,128)}), f32[128,128]{1,0:T(8,128)}) %reduce-scatter.6.cloned.1.call-update) | async-done | bytes 65552 | tf_op jit(solution)/shard_map/reduce_scatter | solution.py:137
  483.3 2.1 fusion.50
  485.3 95.1 %psum.7 = f32[]{:T(128)} all-reduce(f32[]{:T(128)} %get-tuple-element.1404), channel_id=1, replica_groups=mesh['ctx'=32,'tp'=8] {'ctx','tp'}, use_global_device_ids=true, to_apply=%region_20.21 | all-reduce | flops 1 | bytes 8 | tf_op jit(solution)/shard_map/psum | solution.py:182
  580.5 13.0 %fusion.63 = bf16[8,128,128]{1,2,0:T(8,128)(2,1)S(1)} fusion(bf16[2048,128]{1,0:T(8,128)(2,1)S(1)} %all_gather.16, f32[2048,128,8]{1,0,2:T(8,128)} %get-tuple-element.1405, f32[]{:T(128)} %bitcast.16, f32[8,128,2048]{1,2,0:T(8,128)} %get-tuple-element.1403, f32[8,128]{1,0:T(8,128)S(1)} %get-tuple-element.1402), kind=kOutput, calls=%fused_computation.76 | convolution fusion | flops 551816192 | bytes 17567748 | tf_op jit(solution)/shard_map/hqk,kd->qhd/dot_general | solution.py:172
  595.8 32.1 %reduce-scatter.12.cloned.1.call-done = f32[64,128]{1,0:T(8,128)} async-done(((f32[2048,128]{1,0:T(8,128)}), f32[64,128]{1,0:T(8,128)}) %reduce-scatter.12.cloned.1.call-update) | async-done | bytes 32784 | tf_op jit(solution)/shard_map/reduce_scatter | solution.py:180
  627.8 1.4 multiply_convert_fusion.3
  629.2 143.9 %reduce-scatter.14.cloned.1.call-done = f32[64,128]{1,0:T(8,128)} async-done(((f32[2048,128]{1,0:T(8,128)}), f32[64,128]{1,0:T(8,128)}) %reduce-scatter.14.cloned.1.call-update) | async-done | bytes 32784 | tf_op jit(solution)/shard_map/reduce_scatter | solution.py:181
  773.1 1.4 multiply_convert_fusion.2
  774.5 114.5 %reduce-scatter.10.cloned.1.call-done = bf16[128,1024]{1,0:T(8,128)(2,1)} async-done(((bf16[128,8192]{1,0:T(8,128)(2,1)}), bf16[128,1024]{1,0:T(8,128)(2,1)}) %reduce-scatter.10.cloned.1.call-update) | async-done | bytes 262160 | tf_op jit(solution)/shard_map/reduce_scatter | solution.py:146
  (83 shorter events, 16.5 us)
Async XLA Ops:
  7.2 475.4 %copy-start = (bf16[8192,128]{1,0:T(8,128)(2,1)S(1)}, bf16[8192,128]{1,0:T(8,128)(2,1)}, u32[]{:S(2)}) copy-start(bf16[8192,128]{1,0:T(8,128)(2,1)} %param.32) | copy-start | bytes 6291460
  7.2 64.0 %all-gather.3.cloned.1.call-start = ((), (), s32[]{:S(2)}) async-start(), calls=%async_computation.5 | async-start | bytes 1081344 | tf_op jit(solution)/shard_map/all_gather | solution.py:131
  7.9 122.7 %all-gather.5.cloned.1.call-start = ((), (), s32[]{:S(2)}) async-start(), calls=%async_computation.6 | async-start | bytes 1081344 | tf_op jit(solution)/shard_map/all_gather | solution.py:132
  8.7 325.1 %reduce-scatter.8.cloned.1.call-start = ((), (), s32[]{:S(2)}) async-start(), calls=%async_computation.8 | async-start | bytes 2162688 | tf_op jit(solution)/shard_map/reduce_scatter | solution.py:138
  186.7 1.4 copy-start.4
  186.7 51.8 %copy-start.5 = (bf16[64,128]{1,0:T(8,128)(2,1)S(1)}, bf16[64,128]{1,0:T(8,128)(2,1)}, u32[]{:S(2)}) copy-start(bf16[64,128]{1,0:T(8,128)(2,1)} %param.28) | copy-start | bytes 49156
  186.7 95.2 %copy-start.6 = (s32[128]{0:T(128)S(1)}, s32[128]{0:T(128)}, u32[]{:S(2)}) copy-start(s32[128]{0:T(128)} %param.30) | copy-start | bytes 1540
  186.8 294.7 %reduce-scatter.6.cloned.1.call-start = ((), (), s32[]{:S(2)}) async-start(), calls=%async_computation.7 | async-start | bytes 2162688 | tf_op jit(solution)/shard_map/reduce_scatter | solution.py:137
  187.4 440.5 %reduce-scatter.12.cloned.1.call-start = ((), (), s32[]{:S(2)}) async-start(), calls=%async_computation.10 | async-start | bytes 1081344 | tf_op jit(solution)/shard_map/reduce_scatter | solution.py:180
  289.8 9.8 %copy-start.7 = (bf16[128,1024]{1,0:T(8,128)(2,1)S(1)}, bf16[128,1024]{1,0:T(8,128)(2,1)}, u32[]{:S(2)}) copy-start(bf16[128,1024]{1,0:T(8,128)(2,1)} %param.26) | copy-start | bytes 786436
  313.6 459.5 %reduce-scatter.14.cloned.1.call-start = ((), (), s32[]{:S(2)}) async-start(), calls=%async_computation.11 | async-start | bytes 1081344 | tf_op jit(solution)/shard_map/reduce_scatter | solution.py:181
  319.3 569.6 %reduce-scatter.10.cloned.1.call-start = ((), (), s32[]{:S(2)}) async-start(), calls=%async_computation.9 | async-start | bytes 2359296 | tf_op jit(solution)/shard_map/reduce_scatter | solution.py:146
  334.6 150.7 %copy-start.2 = (bf16[128,128]{1,0:T(8,128)(2,1)}, bf16[128,128]{1,0:T(8,128)(2,1)S(1)}, u32[]{:S(2)}) copy-start(bf16[128,128]{1,0:T(8,128)(2,1)S(1)} %convert_element_type.70) | copy-start | bytes 98308
  481.5 1.7 copy-start.1
  482.5 2.8 copy-start.3
Sparse Core Ops, SparseCore 0:
  9.8 61.2 all-gather.2
  73.0 57.5 all-gather.4
  186.9 146.7 reduce-scatter.7
  336.1 145.3 reduce-scatter.5
  483.9 143.9 reduce-scatter.11
  630.2 142.8 reduce-scatter.13
  777.8 111.1 reduce-scatter.9
where the time goes:
time: 899 us; the launch traced here: 897 us
  waiting for transfers between devices  572 us (64%)
  blocking collectives  189 us (21%)
  matrix products  83.5 us (9%)
  local copies, waits for them, and re-layouts  20.2 us (2%)
  between operations  16.8 us (2%)
  other arithmetic  9.11 us (1%)
    reduce_scatter x1, waiting for transfers between devices, local(): key_sum = lax.psum_scatter(key_acc, 'ctx', scatter_dimension=0, tiled=True)  147 us
    reduce_scatter x1, waiting for transfers between devices, local(): lax.psum_scatter(value_part, 'ctx', scatter_dimension=0, tiled=True)  144 us
    reduce_scatter x1, waiting for transfers between devices, local(): lax.psum_scatter(input_part.astype(jnp.bfloat16), 'tp', scatter_dimension...  114 us
    psum x1, blocking collectives, local(): gate_total = lax.psum(jnp.sum(row_dot), ('ctx', 'tp'))  95.1 us
    all_gather x1, waiting for transfers between devices, local(): lax.all_gather(value_self, 'ctx', axis=0, tiled=True)  59.5 us
    all_gather x1, waiting for transfers between devices, local(): lax.all_gather(key_self, 'ctx', axis=0, tiled=True)  59.1 us
    all_gather x1, blocking collectives, local(): image_key_all = lax.all_gather(image_keys, 'ctx', axis=0, tiled=True)  50.5 us
    all_gather x1, blocking collectives, local(): image_value_all = lax.all_gather(image_values, 'ctx', axis=0, tiled=True)  43.4 us
  transfers between devices with their start and end apart: 7, of which 7 were waited for; matrix products, arithmetic and copies ran while one was open for 7% of the time, Pallas kernels for 0%

commit v1 on v0

v1 whole, which is shorter than its diff:
```python
import functools
import math

import jax
import jax.numpy as jnp
from jax import lax
from jax.experimental import pallas as pl
from jax.experimental.pallas import tpu as pltpu
from jax.sharding import PartitionSpec as P

DH = 128
GROUP = 8
NIMG = 4
DOC_MAX = 2176

NEG_FILL = -1e30
SCALE = DH ** (-0.5)
LOG2E = math.log2(math.e)
KB = 256
PAIR = 256


def dot(a, b):
    return lax.dot_general(a, b, (((1,), (0,)), ((), ())), preferred_element_type=jnp.float32)


def attn_kernel(
    bounds_ref,
    gain_ref,
    low_ref,
    high_ref,
    q_ref,
    g_ref,
    k_ref,
    v_ref,
    dq_ref,
    dk_ref,
    dv_ref,
    dot_ref,
    e_s,
    d_s,
    peak_s,
    kt_s,
    qt_s,
    gt_s,
    qr_s,
    gr_s,
    dk_s,
    dv_s,
):
    first, clear0, clear1, last = bounds_ref[0], bounds_ref[1], bounds_ref[2], bounds_ref[3]
    gain = gain_ref[0]
    low = low_ref[...]
    high = high_ref[...]
    tok = q_ref.shape[0]
    for h in range(GROUP):
        p, o = (h * tok) // PAIR, (h * tok) % PAIR
        qh = q_ref[:, h * DH : (h + 1) * DH]
        gh = g_ref[:, h * DH : (h + 1) * DH]
        qr_s[p, o : o + tok, :] = qh
        gr_s[p, o : o + tok, :] = gh
        qt_s[p, :, o : o + tok] = qh.T
        gt_s[p, :, o : o + tok] = gh.T

    def prepare(b, carry):
        start = pl.multiple_of(b * KB, KB)
        kt_s[b - first] = k_ref[pl.ds(start, KB), :].T
        where = pl.multiple_of((b - first) * KB, KB)
        dk_s[pl.ds(where, KB), :] = jnp.zeros((KB, DH), jnp.float32)
        dv_s[pl.ds(where, KB), :] = jnp.zeros((KB, DH), jnp.float32)
        return carry

    lax.fori_loop(first, last, prepare, 0)

    def one_pair(p, dot_total):
        qt = qt_s[p]
        gt = gt_s[p]

        def stats(masked, b, carry):
            peak, total, dsum = carry
            start = pl.multiple_of(b * KB, KB)
            where = pl.multiple_of((b - first) * KB, KB)
            s = dot(k_ref[pl.ds(start, KB), :], qt) * (SCALE * LOG2E)
            dp = dot(v_ref[pl.ds(start, KB), :], gt)
            if masked:
                pos = start + lax.broadcasted_iota(jnp.int32, (KB, PAIR), 0)
                allowed = (pos >= low) & (pos <= high)
                s = jnp.where(allowed, s, NEG_FILL)
            new = jnp.maximum(peak, jnp.max(s, axis=0, keepdims=True))
            e = jnp.exp2(s - new)
            if masked:
                e = jnp.where(allowed, e, 0.0)
            factor = jnp.exp2(peak - new)
            e_s[pl.ds(where, KB), :] = e
            d_s[pl.ds(where, KB), :] = dp
            peak_s[b - first] = new
            total = total * factor + jnp.sum(e, axis=0, keepdims=True)
            dsum = dsum * factor + jnp.sum(e * dp, axis=0, keepdims=True)
            return new, total, dsum

        carry = (
            jnp.full((1, PAIR), NEG_FILL, jnp.float32),
            jnp.zeros((1, PAIR), jnp.float32),
            jnp.zeros((1, PAIR), jnp.float32),
        )
        carry = lax.fori_loop(first, clear0, functools.partial(stats, True), carry)
        carry = lax.fori_loop(clear0, clear1, functools.partial(stats, False), carry)
        peak, total, dsum = lax.fori_loop(clear1, last, functools.partial(stats, True), carry)
        inv = 1.0 / total
        delta = dsum * inv

        def grads(b, dqt):
            where = pl.multiple_of((b - first) * KB, KB)
            norm = jnp.exp2(peak_s[b - first] - peak) * inv
            prob = e_s[pl.ds(where, KB), :] * norm
            ds = (prob * (d_s[pl.ds(where, KB), :] - delta)).astype(jnp.bfloat16)
            dv_s[pl.ds(where, KB), :] += dot(prob.astype(jnp.bfloat16), gr_s[p])
            dk_s[pl.ds(where, KB), :] += dot(ds, qr_s[p])
            return dqt + dot(kt_s[b - first], ds)

        dqt = lax.fori_loop(first, last, grads, jnp.zeros((DH, PAIR), jnp.float32))
        dqt = dqt * (SCALE * gain)
        for i in range(PAIR // tok):
            at = pl.multiple_of(p * (PAIR // tok) * DH + i * DH, DH)
            dq_ref[:, pl.ds(at, DH)] = dqt[:, i * tok : (i + 1) * tok].T.astype(jnp.bfloat16)
        return dot_total + delta

    dot_ref[...] = lax.fori_loop(
        0, GROUP * tok // PAIR, one_pair, jnp.zeros((1, PAIR), jnp.float32)
    )
    dk_ref[...] = jnp.zeros(dk_ref.shape, dk_ref.dtype)
    dv_ref[...] = jnp.zeros(dv_ref.shape, dv_ref.dtype)

    def flush(b, carry):
        start = pl.multiple_of(b * KB, KB)
        where = pl.multiple_of((b - first) * KB, KB)
        dk_ref[pl.ds(start, KB), :] = (dk_s[pl.ds(where, KB), :] * (SCALE * gain)).astype(
            jnp.bfloat16
        )
        dv_ref[pl.ds(start, KB), :] = (dv_s[pl.ds(where, KB), :] * gain).astype(jnp.bfloat16)
        return carry

    lax.fori_loop(first, last, flush, 0)


def attention_grads(name, bounds, gain, low, high, q, g, k, v, max_blocks):
    tok = q.shape[0]
    keys = k.shape[0]
    pairs = GROUP * tok // PAIR
    smem = pl.BlockSpec(memory_space=pltpu.SMEM)
    vmem = pl.BlockSpec(memory_space=pltpu.VMEM)
    steps = max_blocks * KB
    flops = 10 * GROUP * tok * steps * DH
    return pl.pallas_call(
        attn_kernel,
        name=name,
        out_shape=(
            jax.ShapeDtypeStruct(q.shape, jnp.bfloat16),
            jax.ShapeDtypeStruct((keys, DH), jnp.bfloat16),
            jax.ShapeDtypeStruct((keys, DH), jnp.bfloat16),
            jax.ShapeDtypeStruct((1, PAIR), jnp.float32),
        ),
        in_specs=[smem, smem, vmem, vmem, vmem, vmem, vmem, vmem],
        out_specs=(vmem, vmem, vmem, vmem),
        scratch_shapes=[
            pltpu.VMEM((steps, PAIR), jnp.float32),
            pltpu.VMEM((steps, PAIR), jnp.float32),
            pltpu.VMEM((max_blocks, 1, PAIR), jnp.float32),
            pltpu.VMEM((max_blocks, DH, KB), jnp.bfloat16),
            pltpu.VMEM((pairs, DH, PAIR), jnp.bfloat16),
            pltpu.VMEM((pairs, DH, PAIR), jnp.bfloat16),
            pltpu.VMEM((pairs, PAIR, DH), jnp.bfloat16),
            pltpu.VMEM((pairs, PAIR, DH), jnp.bfloat16),
            pltpu.VMEM((steps, DH), jnp.float32),
            pltpu.VMEM((steps, DH), jnp.float32),
        ],
        cost_estimate=pl.CostEstimate(
            flops=flops,
            transcendentals=GROUP * tok * steps,
            bytes_accessed=2 * (3 * q.size + 4 * k.size),
        ),
        compiler_params=pltpu.CompilerParams(vmem_limit_bytes=32 * 1024 * 1024),
    )(bounds, gain, low, high, q, g, k, v)


def block_bounds(first_key, clear_from, clear_to, last_key):
    first = first_key // KB
    last = last_key // KB + 1
    clear0 = jnp.clip((clear_from + KB - 1) // KB, first, last)
    clear1 = jnp.clip((clear_to + 1) // KB, clear0, last)
    return jnp.stack([first, clear0, clear1, last]).astype(jnp.int32)


def local(
    query_self,
    key_self,
    value_self,
    grad_self,
    document_id,
    query_cross,
    image_keys,
    image_values,
    grad_cross,
    image_block,
    gate,
    w_key,
    w_value,
):
    rows = query_self.shape[0]
    seq_len = rows * lax.axis_size("ctx")
    first_row = lax.axis_index("ctx") * rows
    row_pos = first_row + jnp.arange(rows, dtype=jnp.int32)
    row_doc = lax.dynamic_slice_in_dim(document_id, first_row, rows, 0)
    low = jnp.sum(document_id[None, :] < row_doc[:, None], axis=1, dtype=jnp.int32)
    repeat = PAIR // rows

    def per_pair(row_values):
        return jnp.tile(row_values, repeat)[None, :]

    pair = lax.all_gather(
        jnp.stack([key_self, value_self]), "ctx", axis=1, tiled=True
    )
    image_pair = lax.all_gather(
        jnp.stack([image_keys, image_values]), "ctx", axis=1, tiled=True
    )
    one = jnp.ones((1,), jnp.float32)
    max_blocks = min((DOC_MAX - 1 + rows + KB - 2) // KB + 1, seq_len // KB)
    query_grad, key_part, value_part, _ = attention_grads(
        "self_attention",
        block_bounds(low[0], low[-1], first_row, first_row + rows - 1),
        one,
        per_pair(low),
        per_pair(row_pos),
        query_self,
        grad_self,
        pair[0],
        pair[1],
        max_blocks,
    )
    part = lax.psum_scatter(
        jnp.stack([key_part, value_part]), "ctx", scatter_dimension=1, tiled=True
    )
    key_grad, value_grad = part[0], part[1]

    tanh_gate = jnp.tanh(gate)
    image_total = image_pair.shape[1]
    image_len = image_total // NIMG
    limit = (image_block + 1) * image_len - 1
    cross_query_grad, image_key_part, image_value_part, row_dots = attention_grads(
        "cross_attention",
        block_bounds(jnp.int32(0), jnp.int32(0), limit[0], limit[-1]),
        tanh_gate,
        jnp.zeros((1, PAIR), jnp.int32),
        per_pair(limit),
        query_cross,
        grad_cross,
        image_pair[0],
        image_pair[1],
        image_total // KB,
    )
    input_part = dot(key_grad, w_key.T) + dot(value_grad, w_value.T)
    input_grad = lax.psum_scatter(
        input_part.astype(jnp.bfloat16), "tp", scatter_dimension=1, tiled=True
    )
    image_part = lax.psum_scatter(
        jnp.stack([image_key_part, image_value_part]), "ctx", scatter_dimension=1, tiled=True
    )
    gate_total = lax.psum(jnp.sum(row_dots), ("ctx", "tp"))
    gate_grad = (1.0 - tanh_gate * tanh_gate) * gate_total
    return (
        query_grad,
        key_grad,
        value_grad,
        input_grad,
        cross_query_grad,
        image_part[0],
        image_part[1],
        gate_grad,
    )


def solution(mesh):
    in_specs = (
        P("ctx", "tp"),
        P("ctx", "tp"),
        P("ctx", "tp"),
        P("ctx", "tp"),
        P(),
        P("ctx", "tp"),
        P("ctx", "tp"),
        P("ctx", "tp"),
        P("ctx", "tp"),
        P("ctx"),
        P(),
        P(None, "tp"),
        P(None, "tp"),
    )
    out_specs = (
        P("ctx", "tp"),
        P("ctx", "tp"),
        P("ctx", "tp"),
        P("ctx", "tp"),
        P("ctx", "tp"),
        P("ctx", "tp"),
        P("ctx", "tp"),
        P(),
    )
    return jax.shard_map(local, mesh=mesh, in_specs=in_specs, out_specs=out_specs, check_vma=False)
```

time: 899 us -> 534 us (0.59)
  waiting for transfers between devices: 572 us -> 383 us
  blocking collectives: 189 us -> 94.4 us
  matrix products: 83.5 us -> 2.76 us
  Pallas kernels: 0 us -> 13.5 us
  local copies, waits for them, and re-layouts: 20.2 us -> 8.5 us
    reduce_scatter x4 -> x2, waiting for transfers between devices: 337 us -> 168 us  [the longest x1 121 us: local(): lax.psum_scatter(jnp.stack([key_part, value_part]), 'ctx', scatter_dimens...]
    all_gather x2 -> x0, blocking collectives: 93.9 us -> none  [the longest x1 50.5 us: local(): image_key_all = lax.all_gather(image_keys, 'ctx', axis=0, tiled=True)]
    dot_general x20 -> x2, matrix products: 76 us -> 2.76 us  [dot(): lax.dot_general(a, b, (((1,), (0,)), ((), ())), preferred_element_type=jn...]
    all_gather x2, waiting for transfers between devices: 119 us -> 101 us  [the longest x1 56.8 us: local(): lax.all_gather(jnp.stack([key_self, value_self]), 'ctx', axis=1, tiled=True)]
    pallas_call x0 -> x2, Pallas kernels: none -> 13.5 us  [attention_grads(): pl.pallas_call(attn_kernel, name=name, out_shape=(jax.ShapeDtypeStruct(q....]
    dynamic_slice x13 -> x1, local copies, waits for them, and re-layouts: 13.7 us -> 0.76 us  [local(): row_doc = lax.dynamic_slice_in_dim(document_id, first_row, rows, 0)]
  transfers between devices with their start and end apart: 7 -> 5, of which waited for: 7 -> 5; matrix products, arithmetic and copies ran while one was open for 7% -> 3% of each run, Pallas kernels for 0% -> 3%
where the time goes in v1:
time: 534 us; the launch traced here: 533 us
  waiting for transfers between devices  383 us (72%)
  blocking collectives  94.4 us (18%)
  between operations  23 us (4%)
  Pallas kernels  13.5 us (3%)
  local copies, waits for them, and re-layouts  8.5 us (2%)
  other arithmetic  7.33 us (1%)
    reduce_scatter x1, waiting for transfers between devices, local(): lax.psum_scatter(jnp.stack([key_part, value_part]), 'ctx', scatter_dimens...  121 us
    reduce_scatter x1, waiting for transfers between devices, local(): lax.psum_scatter(input_part.astype(jnp.bfloat16), 'tp', scatter_dimension...  114 us
    psum x1, blocking collectives, local(): gate_total = lax.psum(jnp.sum(row_dots), ('ctx', 'tp'))  94.4 us
    all_gather x1, waiting for transfers between devices, local(): lax.all_gather(jnp.stack([key_self, value_self]), 'ctx', axis=1, tiled=True)  56.8 us
    reduce_scatter x1, waiting for transfers between devices, local(): lax.psum_scatter(jnp.stack([image_key_part, image_value_part]), 'ctx', sc...  46.4 us
    all_gather x1, waiting for transfers between devices, local(): lax.all_gather(jnp.stack([image_keys, image_values]), 'ctx', axis=1, tile...  44.5 us
    pallas_call x2, Pallas kernels, attention_grads(): pl.pallas_call(attn_kernel, name=name, out_shape=(jax.ShapeDtypeStruct(q....  13.5 us
  transfers between devices with their start and end apart: 5, of which 5 were waited for; matrix products, arithmetic and copies ran while one was open for 3% of the time, Pallas kernels for 3%

profile of v1, /device:TPU:8, one launch (start us, length us, event | category | flops | bytes accessed | tf_op | source)
XLA Modules:
  0.0 533.0 jit_solution(12985898628573519657)
XLA Ops:
  7.2 0.0 copy-start
  7.2 0.0 all-gather.3.cloned.1.call-start
  7.2 1.6 pad_maximum_fusion.2
  8.8 0.0 all-gather.3.cloned.1.call-update
  8.8 0.0 all-gather.5.cloned.1.call-start
  8.9 1.4 pad_maximum_fusion.3
  10.2 0.0 all-gather.5.cloned.1.call-update
  10.2 0.0 reduce-scatter.4.cloned.1.call-start
  10.3 0.8 dynamic_slice.3
  11.1 1.1 convert_reduce_fusion
  12.1 0.6 fusion.2
  16.0 0.1 pad_add_fusion.bounds_ref
  16.1 0.0 copy-start.1
  16.1 0.0 copy-start.2
  16.1 56.8 %all-gather.3.cloned.1.call-done = bf16[2,4096,128]{2,1,0:T(8,128)(2,1)} async-done(((bf16[2,128,128]{2,1,0:T(8,128)(2,1)}), bf16[2,4096,128]{2,1,0:T(8,128)(2,1)}) %all-gather.3.cloned.1.call-update) | async-done | bytes 2097168 | tf_op jit(solution)/shard_map/all_gather | solution.py:220
  72.9 1.7 slice_bitcast_fusion
  74.6 0.0 copy-done.1
  74.6 0.0 copy-done.2
  74.6 6.9 %self_attention.1 = (bf16[128,1024]{1,0:T(8,128)(2,1)}, bf16[4096,128]{1,0:T(8,128)(2,1)S(1)}, bf16[4096,128]{1,0:T(8,128)(2,1)S(1)}, f32[1,256]{1,0:T(1,128)}) custom-call(s32[4]{0:T(128)S(1)} %pad_add_fusion.bounds_ref, f32[1]{0:T(128)} %constant.107.clone.1.gain_ref, s32[1,256]{1,0:T(1,128)S(1)} %bitcast.47, s32[1,256]{1,0:T(1,128)S(1)} %bitcast.49, ...), custom_call_target="tpu_custom_call" | custom-call | flops 3355443200 | bytes 4980736 | tf_op jit(solution)/shard_map/self_attention/pallas_call | solution.py:154
  81.5 1.5 pad_maximum_fusion
  83.1 0.0 reduce-scatter.4.cloned.1.call-update
  83.1 0.0 reduce-scatter.8.cloned.1.call-start
  83.1 0.6 copy-done.8
  83.7 0.6 fusion.1
  88.3 0.1 pad_add_fusion.1.bounds_ref
  88.3 44.5 %all-gather.5.cloned.1.call-done = bf16[2,2048,128]{2,1,0:T(8,128)(2,1)} async-done(((bf16[2,64,128]{2,1,0:T(8,128)(2,1)}), bf16[2,2048,128]{2,1,0:T(8,128)(2,1)}) %all-gather.5.cloned.1.call-update) | async-done | bytes 1048592 | tf_op jit(solution)/shard_map/all_gather | solution.py:223
  132.9 1.3 slice_bitcast_fusion.2
  134.2 0.0 copy-done.3
  134.2 0.0 copy-done.4
  134.2 6.6 %cross_attention.1 = (bf16[128,1024]{1,0:T(8,128)(2,1)}, bf16[2048,128]{1,0:T(8,128)(2,1)S(1)}, bf16[2048,128]{1,0:T(8,128)(2,1)S(1)}, f32[1,256]{1,0:T(1,128)S(1)}) custom-call(s32[4]{0:T(128)S(1)} %pad_add_fusion.1.bounds_ref, f32[1]{0:T(128)S(6)} %tanh.3.gain_ref, s32[1,256]{1,0:T(1,128)S(1)} %broadcast_in_dim.2.low_ref, s32[1,256]{1,0:T(1,128)S(1)} %bitcast.48, ...), custom_call_target="tpu_custom_call" | custom-call | flops 2684354560 | bytes 2883584 | tf_op jit(solution)/shard_map/cross_attention/pallas_call | solution.py:154
  140.8 1.1 pad_maximum_fusion.1
  141.9 0.0 reduce-scatter.8.cloned.1.call-update
  141.9 0.0 reduce-scatter.6.cloned.1.call-start
  141.9 121.4 %reduce-scatter.4.cloned.1.call-done = bf16[2,128,128]{2,1,0:T(8,128)(2,1)} async-done(((bf16[2,4096,128]{2,1,0:T(8,128)(2,1)}), bf16[2,128,128]{2,1,0:T(8,128)(2,1)}) %reduce-scatter.4.cloned.1.call-update) | async-done | bytes 65552 | tf_op jit(solution)/shard_map/reduce_scatter | solution.py:240
  263.4 0.8 slice_bitcast_fusion.4
  264.1 0.0 copy-done
  264.2 0.0 copy-start.5
  264.2 0.7 fusion.3
  264.9 0.0 copy-done.7
  264.9 0.0 copy-done.6
  264.9 0.9 copy-done.5
  265.8 2.0 fusion
  267.8 0.0 reduce-scatter.6.cloned.1.call-update
  267.9 0.6 reduce_sum.19
  268.5 94.4 %psum.7 = f32[1]{0:T(128)} all-reduce(f32[1]{0:T(128)} %bitcast.30), channel_id=1, replica_groups=mesh['ctx'=32,'tp'=8] {'ctx','tp'}, use_global_device_ids=true, to_apply=%region_5.6 | all-reduce | flops 1 | bytes 8 | tf_op jit(solution)/shard_map/psum | solution.py:268
  363.5 46.4 %reduce-scatter.8.cloned.1.call-done = bf16[2,64,128]{2,1,0:T(8,128)(2,1)} async-done(((bf16[2,2048,128]{2,1,0:T(8,128)(2,1)}), bf16[2,64,128]{2,1,0:T(8,128)(2,1)}) %reduce-scatter.8.cloned.1.call-update) | async-done | bytes 32784 | tf_op jit(solution)/shard_map/reduce_scatter | solution.py:265
  409.9 1.3 slice_bitcast_fusion.6
  411.2 114.1 %reduce-scatter.6.cloned.1.call-done = bf16[128,1024]{1,0:T(8,128)(2,1)} async-done(((bf16[128,8192]{1,0:T(8,128)(2,1)}), bf16[128,1024]{1,0:T(8,128)(2,1)}) %reduce-scatter.6.cloned.1.call-update) | async-done | bytes 262160 | tf_op jit(solution)/shard_map/reduce_scatter | solution.py:262
  (11 shorter events, 0.0 us)
Async XLA Ops:
  7.2 257.0 %copy-start = (bf16[8192,128]{1,0:T(8,128)(2,1)S(1)}, bf16[8192,128]{1,0:T(8,128)(2,1)}, u32[]{:S(2)}) copy-start(bf16[8192,128]{1,0:T(8,128)(2,1)} %param.24) | copy-start | bytes 6291460
  7.2 65.7 %all-gather.3.cloned.1.call-start = ((), (), s32[]{:S(2)}) async-start(), calls=%async_computation.3 | async-start | bytes 2162688 | tf_op jit(solution)/shard_map/all_gather | solution.py:220
  8.8 124.1 %all-gather.5.cloned.1.call-start = ((), (), s32[]{:S(2)}) async-start(), calls=%async_computation.6 | async-start | bytes 1081344 | tf_op jit(solution)/shard_map/all_gather | solution.py:223
  10.2 253.1 %reduce-scatter.4.cloned.1.call-start = ((), (), s32[]{:S(2)}) async-start(), calls=%async_computation.4 | async-start | bytes 2162688 | tf_op jit(solution)/shard_map/reduce_scatter | solution.py:240
  16.1 58.5 %copy-start.1 = (bf16[128,1024]{1,0:T(8,128)(2,1)S(1)}, bf16[128,1024]{1,0:T(8,128)(2,1)}, u32[]{:S(2)}) copy-start(bf16[128,1024]{1,0:T(8,128)(2,1)} %q_ref.2) | copy-start | bytes 786436
  16.1 58.5 %copy-start.2 = (bf16[128,1024]{1,0:T(8,128)(2,1)S(1)}, bf16[128,1024]{1,0:T(8,128)(2,1)}, u32[]{:S(2)}) copy-start(bf16[128,1024]{1,0:T(8,128)(2,1)} %g_ref.2) | copy-start | bytes 786436
  83.0 0.7 copy-start.8
  83.0 51.1 %copy-start.3 = (bf16[128,1024]{1,0:T(8,128)(2,1)S(1)}, bf16[128,1024]{1,0:T(8,128)(2,1)}, u32[]{:S(2)}) copy-start(bf16[128,1024]{1,0:T(8,128)(2,1)} %q_ref.3) | copy-start | bytes 786436
  83.1 51.1 %copy-start.4 = (bf16[128,1024]{1,0:T(8,128)(2,1)S(1)}, bf16[128,1024]{1,0:T(8,128)(2,1)}, u32[]{:S(2)}) copy-start(bf16[128,1024]{1,0:T(8,128)(2,1)} %g_ref.3) | copy-start | bytes 786436
  83.1 326.8 %reduce-scatter.8.cloned.1.call-start = ((), (), s32[]{:S(2)}) async-start(), calls=%async_computation.7 | async-start | bytes 1081344 | tf_op jit(solution)/shard_map/reduce_scatter | solution.py:265
  141.9 383.4 %reduce-scatter.6.cloned.1.call-start = ((), (), s32[]{:S(2)}) async-start(), calls=%async_computation.5 | async-start | bytes 2359296 | tf_op jit(solution)/shard_map/reduce_scatter | solution.py:262
  264.1 0.8 copy-start.7
  264.1 0.8 copy-start.6
  264.2 1.6 copy-start.5
Sparse Core Ops, SparseCore 0:
  10.4 62.4 all-gather.2
  75.4 57.4 all-gather.4
  135.4 127.9 reduce-scatter.3
  265.7 144.1 reduce-scatter.7
  414.4 110.9 reduce-scatter.5

commit v2 on v1

v2 whole, which is shorter than its diff:
```python
import functools
import math

import jax
import jax.numpy as jnp
from jax import lax
from jax.experimental import pallas as pl
from jax.experimental.pallas import tpu as pltpu
from jax.sharding import PartitionSpec as P


DH = 128
GROUP = 8
NIMG = 4
DOCS = 16
DOC_MAX = 2176

NEG_FILL = -1e30
SCALE = DH ** (-0.5)
LOG2E = math.log2(math.e)
KB = 256
PAIR = 256
PAD = 16
NY, NZ, NCORE, NX = 4, 4, 2, 4

SMEM = pl.BlockSpec(memory_space=pltpu.SMEM)
VMEM = pl.BlockSpec(memory_space=pltpu.VMEM)
BF16 = jnp.bfloat16
F32 = jnp.float32


def shaped(shape, dtype):
    return jax.ShapeDtypeStruct(shape, dtype)


def dot(a, b):
    return lax.dot_general(a, b, (((1,), (0,)), ((), ())), preferred_element_type=F32)


def dot_t(a, b):
    return lax.dot_general(a, b, (((1,), (1,)), ((), ())), preferred_element_type=F32)


def ctx_shift(dy, dz, flip):
    def move(c):
        y, z, core = c // 8, (c // 2) % 4, c % 2
        return ((y + dy) % NY) * 8 + ((z + dz) % NZ) * 2 + (core ^ flip)

    return [(c, move(c)) for c in range(NY * NZ * NCORE)]


def send_y(value, k):
    return lax.ppermute(value, "ctx", ctx_shift(k, 0, 0))


def send_z(value, k):
    return lax.ppermute(value, "ctx", ctx_shift(0, k, 0))


def send_core(value):
    return lax.ppermute(value, "ctx", ctx_shift(0, 0, 1))


def send_x(value, k):
    perm = [(t, (t // NX) * NX + (t + k) % NX) for t in range(2 * NX)]
    return lax.ppermute(value, "tp", perm)


def send_zh(value):
    return lax.ppermute(value, "tp", [(t, t ^ NX) for t in range(2 * NX)])


def after(value, *earlier):
    return lax.optimization_barrier((value,) + earlier)[0]


def stack_kernel(k_ref, v_ref, ik_ref, iv_ref, kv_ref, ikv_ref):
    kv_ref[0] = k_ref[...]
    kv_ref[1] = v_ref[...]
    ikv_ref[0] = ik_ref[...]
    ikv_ref[1] = iv_ref[...]


def rows_kernel(
    ctx_ref, gate_ref, doc_ref, block_ref, low_ref, high_ref, limit_ref, gain_ref, bounds_ref
):
    tok = doc_ref.shape[1]
    c = ctx_ref[0]
    docs = doc_ref[...]
    mine = doc_ref[pl.ds(c, 1), :]
    low = jnp.zeros((1, tok), jnp.int32)
    for d in range(1, DOCS):
        before = jnp.sum((docs < d).astype(F32), axis=0, keepdims=True)
        before = jnp.sum(before, axis=1, keepdims=True).astype(jnp.int32)
        low = jnp.where(mine == d, before, low)
    high = c * tok + lax.broadcasted_iota(jnp.int32, (1, tok), 1)
    limit = (block_ref[...] + 1) * (bounds_scale(doc_ref) // NIMG) - 1
    for i in range(PAIR // tok):
        low_ref[:, i * tok : (i + 1) * tok] = low
        high_ref[:, i * tok : (i + 1) * tok] = high
        limit_ref[:, i * tok : (i + 1) * tok] = limit
    gain_ref[...] = jnp.tanh(jnp.full(gain_ref.shape, gate_ref[0], F32))
    shift = KB.bit_length() - 1

    def put(at, first_key, clear_from, clear_to, last_key):
        first = lax.shift_right_logical(first_key, shift)
        last = lax.shift_right_logical(last_key, shift) + 1
        clear0 = lax.shift_right_logical(clear_from + KB - 1, shift)
        clear0 = jnp.minimum(jnp.maximum(clear0, first), last)
        clear1 = lax.shift_right_logical(clear_to + 1, shift)
        clear1 = jnp.minimum(jnp.maximum(clear1, clear0), last)
        for i, value in enumerate((first, clear0, clear1, last)):
            bounds_ref[at + i] = value

    put(0, jnp.min(low), jnp.max(low), c * tok, c * tok + tok - 1)
    put(4, jnp.int32(0), jnp.int32(0), jnp.min(limit), jnp.max(limit))


def bounds_scale(doc_ref):
    return doc_ref.shape[0] * doc_ref.shape[1] // 2


def order_kernel(ctx_ref, *refs):
    out_ref = refs[-1]
    z = lax.shift_right_logical(ctx_ref[0], 1) & (NZ - 1)
    for k in range(NZ):
        out_ref[(z - k) & (NZ - 1)] = refs[k][...]


def weights_kernel(order_ref, wk_ref, wv_ref, *out_refs):
    step = pl.program_id(0)
    for k in range(NX):

        @pl.when(lax.shift_right_logical(step, 1) == k)
        def _():
            out_refs[k][0, 0] = wk_ref[...]
            out_refs[k][0, 1] = wv_ref[...]


def weight_pieces(tp, w_key, w_value):
    rows = w_key.shape[0] // (2 * NX)
    zh, x = tp // NX, tp % NX
    step = jnp.arange(2 * NX, dtype=jnp.int32)
    order = ((zh + (step & 1)) & 1) * NX + ((x + (step >> 1)) & (NX - 1))

    def piece_map(k):
        return lambda g, order: (jnp.clip(g - 2 * k, 0, 1), 0, 0, 0)

    return pl.pallas_call(
        weights_kernel,
        name="weight_pieces",
        grid_spec=pltpu.PrefetchScalarGridSpec(
            num_scalar_prefetch=1,
            grid=(2 * NX,),
            in_specs=[pl.BlockSpec((rows, DH), lambda g, order: (order[g], 0))] * 2,
            out_specs=[pl.BlockSpec((1, 2, rows, DH), piece_map(k)) for k in range(NX)],
        ),
        out_shape=[shaped((2, 2, rows, DH), BF16)] * NX,
    )(order, w_key, w_value)


def split_gate(total):
    hi = total.astype(BF16).astype(F32)
    mid = (total - hi).astype(BF16).astype(F32)
    lo = (total - hi) - mid
    row = lax.broadcasted_iota(jnp.int32, (PAD, DH), 0)
    rows = jnp.where(row == 0, hi, jnp.where(row == 1, mid, jnp.where(row == 2, lo, 0.0)))
    return rows.astype(BF16)


def join_gate(rows):
    return jnp.sum(rows.astype(F32), axis=0, keepdims=True)


def core_sum_kernel(pad, own_ref, other_ref, *out_refs):
    n = out_refs[0].shape[0] - pad
    if pad:
        at = NY * n
        tail = split_gate(join_gate(own_ref[at : at + pad]) + join_gate(other_ref[at : at + pad]))
    for k in range(NY):
        at = k * n
        total = own_ref[at : at + n].astype(F32) + other_ref[at : at + n].astype(F32)
        out_refs[k][0:n] = total.astype(BF16)
        if pad:
            out_refs[k][n : n + pad] = tail


def y_sum_kernel(pad, ctx_ref, s0_ref, s1_ref, s2_ref, s3_ref, *out_refs):
    n = out_refs[0].shape[0] - pad
    z = lax.shift_right_logical(ctx_ref[0], 1) & (NZ - 1)
    ins = (s0_ref, s1_ref, s2_ref, s3_ref)
    if pad:
        tail = split_gate(sum(join_gate(r[NZ * n : NZ * n + pad]) for r in ins))
    for k in range(NZ):
        at = pl.multiple_of(((z + k) & (NZ - 1)) * n, n)
        total = sum(r[pl.ds(at, n)].astype(F32) for r in ins)
        out_refs[k][0:n] = total.astype(BF16)
        if pad:
            out_refs[k][n : n + pad] = tail


def z_sum_kernel(pad, s0_ref, s1_ref, s2_ref, s3_ref, *out_refs):
    ins = (s0_ref, s1_ref, s2_ref, s3_ref)
    n = ins[0].shape[0] - pad
    total = sum(r[0:n].astype(F32) for r in ins).astype(BF16)
    if pad:
        gate = sum(join_gate(r[n : n + pad]) for r in ins)
        out_refs[2][...] = jnp.broadcast_to(gate, out_refs[2].shape)
    else:
        out_refs[2][...] = total
    out_refs[0][...] = total[: n // 2]
    out_refs[1][...] = total[n // 2 :]


def project_kernel(*refs):
    grads, weights, out_ref = refs[:NX], refs[NX : 2 * NX], refs[2 * NX]
    tok = grads[0].shape[0] // 2
    cols = 256
    for j in range(out_ref.shape[1] // cols):
        total = None
        for g, w in zip(grads, weights):
            for i in range(2):
                part = dot_t(g[i * tok : (i + 1) * tok], w[0, i, j * cols : (j + 1) * cols])
                total = part if total is None else total + part
        out_ref[:, j * cols : (j + 1) * cols] = total.astype(out_ref.dtype)


def project(half, grads, weights):
    tok = grads[0].shape[0] // 2
    rows = weights[0].shape[2]
    return pl.pallas_call(
        project_kernel,
        grid=(1,),
        in_specs=[pl.BlockSpec(g.shape, lambda i: (0, 0)) for g in grads]
        + [pl.BlockSpec((1, 2, rows, DH), lambda i: (half, 0, 0, 0))] * NX,
        out_specs=pl.BlockSpec((tok, rows), lambda i: (0, 0)),
        out_shape=shaped((tok, rows), BF16 if half == 1 else F32),
        cost_estimate=pl.CostEstimate(
            flops=4 * NX * tok * rows * DH, transcendentals=0, bytes_accessed=4 * NX * rows * DH
        ),
    )(*grads, *weights)


def add_kernel(a_ref, b_ref, o_ref):
    o_ref[...] = (a_ref[...] + b_ref[...].astype(F32)).astype(o_ref.dtype)


def gate_sum_kernel(g0, g1, g2, g3, o_ref):
    o_ref[...] = g0[...] + g1[...] + g2[...] + g3[...]


def gate_out_kernel(a_ref, b_ref, gain_ref, o_ref):
    t = gain_ref[0:1, 0:DH]
    o_ref[...] = (1.0 - t * t) * (a_ref[0:1] + b_ref[0:1])


def call(kernel, outs, *args, smem=0):
    single = not isinstance(outs, (list, tuple))
    specs = [SMEM] * smem + [VMEM] * (len(args) - smem)
    return pl.pallas_call(
        kernel, out_shape=outs, in_specs=specs, out_specs=VMEM if single else [VMEM] * len(outs)
    )(*args)


def attn_kernel(block_rows, base, pad, *refs):
    ctx_ref, bounds_ref, low_ref, high_ref, gain_ref, q_ref, g_ref = refs[:7]
    mine, others = refs[7 : 7 + NY], refs[7 + NY : 7 + 2 * NY]
    dq_ref, own_ref, oth_ref = refs[7 + 2 * NY : 10 + 2 * NY]
    (k_s, v_s, e_s, d_s, peak_s, kt_s, qt_s, gt_s, qr_s, gr_s, dk_s, dv_s) = refs[10 + 2 * NY :]
    first, clear0, clear1, last = (bounds_ref[base + i] for i in range(4))
    c = ctx_ref[0]
    core, my_y = c & 1, lax.shift_right_logical(c, 3)
    gain = gain_ref[0:1, 0:DH]
    low = low_ref[...]
    high = high_ref[...]
    tok = q_ref.shape[0]

    for h in range(GROUP):
        p, o = (h * tok) // PAIR, (h * tok) % PAIR
        qh = q_ref[:, h * DH : (h + 1) * DH]
        gh = g_ref[:, h * DH : (h + 1) * DH]
        qr_s[p, o : o + tok, :] = qh
        gr_s[p, o : o + tok, :] = gh
        qt_s[p, :, o : o + tok] = qh.T
        gt_s[p, :, o : o + tok] = gh.T
    for k in range(NY):
        for flip, ref in ((0, mine[k]), (1, others[k])):
            for z in range(NZ):
                block = ((my_y - k) & (NY - 1)) * 8 + z * 2 + (core ^ flip)
                at = pl.multiple_of(block * block_rows, block_rows)
                k_s[pl.ds(at, block_rows), :] = ref[z, 0]
                v_s[pl.ds(at, block_rows), :] = ref[z, 1]

    def prepare(b, carry):
        start = pl.multiple_of(b * KB, KB)
        kt_s[b - first] = k_s[pl.ds(start, KB), :].T
        where = pl.multiple_of((b - first) * KB, KB)
        dk_s[pl.ds(where, KB), :] = jnp.zeros((KB, DH), F32)
        dv_s[pl.ds(where, KB), :] = jnp.zeros((KB, DH), F32)
        return carry

    lax.fori_loop(first, last, prepare, 0)

    def one_pair(p, dot_total):
        qt = qt_s[p]
        gt = gt_s[p]

        def stats(masked, b, carry):
            peak, total, dsum = carry
            start = pl.multiple_of(b * KB, KB)
            where = pl.multiple_of((b - first) * KB, KB)
            s = dot(k_s[pl.ds(start, KB), :], qt) * (SCALE * LOG2E)
            dp = dot(v_s[pl.ds(start, KB), :], gt)
            if masked:
                pos = start + lax.broadcasted_iota(jnp.int32, (KB, PAIR), 0)
                allowed = (pos >= low) & (pos <= high)
                s = jnp.where(allowed, s, NEG_FILL)
            new = jnp.maximum(peak, jnp.max(s, axis=0, keepdims=True))
            e = jnp.exp2(s - new)
            if masked:
                e = jnp.where(allowed, e, 0.0)
            factor = jnp.exp2(peak - new)
            e_s[pl.ds(where, KB), :] = e
            d_s[pl.ds(where, KB), :] = dp
            peak_s[b - first] = new
            total = total * factor + jnp.sum(e, axis=0, keepdims=True)
            dsum = dsum * factor + jnp.sum(e * dp, axis=0, keepdims=True)
            return new, total, dsum

        carry = (
            jnp.full((1, PAIR), NEG_FILL, F32),
            jnp.zeros((1, PAIR), F32),
            jnp.zeros((1, PAIR), F32),
        )
        carry = lax.fori_loop(first, clear0, functools.partial(stats, True), carry)
        carry = lax.fori_loop(clear0, clear1, functools.partial(stats, False), carry)
        peak, total, dsum = lax.fori_loop(clear1, last, functools.partial(stats, True), carry)
        inv = 1.0 / total
        delta = dsum * inv

        def grads(b, dqt):
            where = pl.multiple_of((b - first) * KB, KB)
            norm = jnp.exp2(peak_s[b - first] - peak) * inv
            prob = e_s[pl.ds(where, KB), :] * norm
            ds = (prob * (d_s[pl.ds(where, KB), :] - delta)).astype(BF16)
            dv_s[pl.ds(where, KB), :] += dot(prob.astype(BF16), gr_s[p])
            dk_s[pl.ds(where, KB), :] += dot(ds, qr_s[p])
            return dqt + dot(kt_s[b - first], ds)

        dqt = lax.fori_loop(first, last, grads, jnp.zeros((DH, PAIR), F32))
        for i in range(PAIR // tok):
            at = pl.multiple_of(p * (PAIR // tok) * DH + i * DH, DH)
            part = dqt[:, i * tok : (i + 1) * tok] * (gain * SCALE)
            dq_ref[:, pl.ds(at, DH)] = part.T.astype(BF16)
        return dot_total + delta

    dots = lax.fori_loop(0, GROUP * tok // PAIR, one_pair, jnp.zeros((1, PAIR), F32))

    n = NZ * 2 * block_rows
    own_ref[...] = jnp.zeros(own_ref.shape, own_ref.dtype)
    oth_ref[...] = jnp.zeros(oth_ref.shape, oth_ref.dtype)
    per_step = KB // block_rows

    def flush(b, carry):
        for i in range(per_step):
            block = b * per_step + i
            k = (lax.shift_right_logical(block, 3) - my_y) & (NY - 1)
            z = lax.shift_right_logical(block, 1) & (NZ - 1)
            at = pl.multiple_of(k * n + z * 2 * block_rows, block_rows)
            where = pl.multiple_of((b - first) * KB + i * block_rows, block_rows)
            dk = (dk_s[pl.ds(where, block_rows), :] * (gain * SCALE)).astype(BF16)
            dv = (dv_s[pl.ds(where, block_rows), :] * gain).astype(BF16)
            for same, ref in ((True, own_ref), (False, oth_ref)):

                @pl.when((core == (i & 1)) if same else (core != (i & 1)))
                def _():
                    ref[pl.ds(at, block_rows), :] = dk
                    ref[pl.ds(at + block_rows, block_rows), :] = dv

        return carry

    lax.fori_loop(first, last, flush, 0)
    if pad:
        gate = jnp.broadcast_to(jnp.sum(dots, axis=1, keepdims=True), (1, DH))
        own_ref[NY * n : NY * n + pad] = split_gate(gate)
        oth_ref[NY * n : NY * n + pad] = split_gate(gate)


def attention_grads(base, pad, max_blocks, ctx, bounds, low, high, gain, q, g, mine, others):
    tok = q.shape[0]
    block_rows = mine[0].shape[2]
    keys = NY * NZ * NCORE * block_rows
    pairs = GROUP * tok // PAIR
    steps = max_blocks * KB
    half = shaped((keys + pad, DH), BF16)
    return pl.pallas_call(
        functools.partial(attn_kernel, block_rows, base, pad),
        out_shape=(shaped(q.shape, BF16), half, half),
        in_specs=[SMEM, SMEM] + [VMEM] * (5 + 2 * NY),
        out_specs=(VMEM, VMEM, VMEM),
        scratch_shapes=[
            pltpu.VMEM((keys, DH), BF16),
            pltpu.VMEM((keys, DH), BF16),
            pltpu.VMEM((steps, PAIR), F32),
            pltpu.VMEM((steps, PAIR), F32),
            pltpu.VMEM((max_blocks, 1, PAIR), F32),
            pltpu.VMEM((max_blocks, DH, KB), BF16),
            pltpu.VMEM((pairs, DH, PAIR), BF16),
            pltpu.VMEM((pairs, DH, PAIR), BF16),
            pltpu.VMEM((pairs, PAIR, DH), BF16),
            pltpu.VMEM((pairs, PAIR, DH), BF16),
            pltpu.VMEM((steps, DH), F32),
            pltpu.VMEM((steps, DH), F32),
        ],
        cost_estimate=pl.CostEstimate(
            flops=10 * GROUP * tok * steps * DH,
            transcendentals=GROUP * tok * steps,
            bytes_accessed=2 * (3 * q.size + 4 * keys * DH),
        ),
        compiler_params=pltpu.CompilerParams(vmem_limit_bytes=32 * 1024 * 1024),
    )(ctx, bounds, low, high, gain, q, g, *mine, *others)


def local(
    query_self,
    key_self,
    value_self,
    grad_self,
    document_id,
    query_cross,
    image_keys,
    image_values,
    grad_cross,
    image_block,
    gate,
    w_key,
    w_value,
):
    tok = query_self.shape[0]
    img = image_keys.shape[0]
    seq = document_id.shape[0]
    ctx = lax.axis_index("ctx").reshape(1)
    tp = lax.axis_index("tp")

    kv, ikv = call(
        stack_kernel,
        (shaped((2, tok, DH), BF16), shaped((2, img, DH), BF16)),
        key_self,
        value_self,
        image_keys,
        image_values,
    )
    kv_z = [kv] + [send_z(kv, k) for k in range(1, NZ)]
    rows_doc = after(document_id.reshape(seq // tok, tok), kv)
    low, high, limit, gain, bounds = pl.pallas_call(
        rows_kernel,
        name="rows",
        out_shape=(shaped((1, PAIR), jnp.int32),) * 3
        + (shaped((8, DH), F32), shaped((8,), jnp.int32)),
        in_specs=[SMEM, SMEM, VMEM, VMEM],
        out_specs=(VMEM,) * 4 + (SMEM,),
    )(ctx, gate, rows_doc, image_block.reshape(1, tok))
    kv_mine = call(order_kernel, shaped((NZ, 2, tok, DH), BF16), ctx, *kv_z, smem=1)
    pieces = weight_pieces(after(tp, kv_mine), w_key, w_value)
    ikv = after(ikv, kv_mine)
    ikv_z = [ikv] + [send_z(ikv, k) for k in range(1, NZ)]
    mine = [kv_mine] + [send_y(kv_mine, k) for k in range(1, NY)]
    others = [send_core(m) for m in mine]
    weights = [pieces[0]] + [send_x(pieces[k], k) for k in range(1, NX)]
    ikv_mine = call(order_kernel, shaped((NZ, 2, img, DH), BF16), ctx, *ikv_z, smem=1)
    imine = [ikv_mine] + [send_y(ikv_mine, k) for k in range(1, NY)]
    query = after(query_self, ikv_mine)

    ones = jnp.ones((8, DH), F32)
    max_blocks = min((DOC_MAX - 1 + tok + KB - 2) // KB + 1, seq // KB)
    query_grad, own, other = attention_grads(
        0, 0, max_blocks, ctx, bounds, low, high, ones, query, grad_self, mine, others
    )
    got = send_core(other)
    imine = [after(m, own) for m in imine]
    iothers = [send_core(m) for m in imine]
    piece = shaped((NZ * 2 * tok, DH), BF16)
    share = call(functools.partial(core_sum_kernel, 0), [piece] * NY, own, got)
    query = after(query_cross, share[0])
    share = [share[0]] + [send_y(share[k], k) for k in range(1, NY)]
    cross_query_grad, iown, iother = attention_grads(
        4,
        PAD,
        seq // 2 // KB,
        ctx,
        bounds,
        jnp.zeros((1, PAIR), jnp.int32),
        limit,
        gain,
        query,
        grad_cross,
        imine,
        iothers,
    )
    igot = send_core(iother)
    piece = shaped((2 * tok, DH), BF16)
    share[0] = after(share[0], iown, *weights[1:])
    share = call(functools.partial(y_sum_kernel, 0), [piece] * NZ, ctx, *share, smem=1)
    iown = after(iown, share[0])
    share = [share[0]] + [send_z(share[k], k) for k in range(1, NZ)]
    ipiece = shaped((NZ * 2 * img + PAD, DH), BF16)
    ishare = call(functools.partial(core_sum_kernel, PAD), [ipiece] * NY, iown, igot)
    share[0] = after(share[0], ishare[0])
    ishare = [ishare[0]] + [send_y(ishare[k], k) for k in range(1, NY)]
    one = shaped((tok, DH), BF16)
    key_grad, value_grad, both = call(functools.partial(z_sum_kernel, 0), [one, one, piece], *share)
    ishare[0] = after(ishare[0], both)
    both = [both] + [send_x(both, k) for k in range(1, NX)]
    ipiece = shaped((2 * img + PAD, DH), BF16)
    ishare = call(functools.partial(y_sum_kernel, PAD), [ipiece] * NZ, ctx, *ishare, smem=1)
    both[0] = after(both[0], ishare[0])
    ishare = [ishare[0]] + [send_z(ishare[k], k) for k in range(1, NZ)]
    away = project(1, both, weights)
    both[0] = after(both[0], away)
    ishare[0] = after(ishare[0], away)
    away = send_zh(away)
    home = project(0, both, weights)
    one = shaped((img, DH), BF16)
    gates = shaped((8, DH), F32)
    image_key_grad, image_value_grad, total = call(
        functools.partial(z_sum_kernel, PAD), [one, one, gates], *ishare
    )
    total = [total] + [send_x(total, k) for k in range(1, NX)]
    total = call(gate_sum_kernel, gates, *total)
    far = send_zh(total)
    input_grad = call(add_kernel, shaped(home.shape, BF16), home, away)
    gate_grad = call(gate_out_kernel, shaped((1, DH), F32), total, far, gain)
    return (
        query_grad,
        key_grad,
        value_grad,
        input_grad,
        cross_query_grad,
        image_key_grad,
        image_value_grad,
        gate_grad[0, :1],
    )


def solution(mesh):
    two = P("ctx", "tp")
    in_specs = (two,) * 4 + (P(),) + (two,) * 4 + (P("ctx"), P(), P(None, "tp"), P(None, "tp"))
    out_specs = (two,) * 7 + (P(),)


    return jax.shard_map(local, mesh=mesh, in_specs=in_specs, out_specs=out_specs, check_vma=False)
```

time: 534 us -> 219 us (0.41)
  waiting for transfers between devices: 383 us -> 52.1 us
  blocking collectives: 94.4 us -> 0 us
  starting transfers between devices: 0.21 us -> 94.5 us
  Pallas kernels: 13.5 us -> 54 us
  between operations: 23 us -> 1.56 us
  other arithmetic: 7.33 us -> 0.52 us
  local copies, waits for them, and re-layouts: 8.5 us -> 15.2 us
    reduce_scatter x3 -> x0, waiting for transfers between devices: 282 us -> none  [the longest x1 121 us: local(): lax.psum_scatter(jnp.stack([key_part, value_part]), 'ctx', scatter_dimens...]
    all_gather x2 -> x0, waiting for transfers between devices: 101 us -> none  [the longest x1 56.8 us: local(): lax.all_gather(jnp.stack([key_self, value_self]), 'ctx', axis=1, tiled=True)]
    ppermute x0 -> x45, starting transfers between devices: none -> 94.5 us  [the longest x12 50.8 us: send_y(): return lax.ppermute(value, 'ctx', ctx_shift(k, 0, 0))]
    psum x1 -> x0, blocking collectives: 94.4 us -> none  [local(): gate_total = lax.psum(jnp.sum(row_dots), ('ctx', 'tp'))]
    ppermute x0 -> x45, waiting for transfers between devices: none -> 52.1 us  [the longest x12 23.1 us: send_z(): return lax.ppermute(value, 'ctx', ctx_shift(0, k, 0))]
    pallas_call x2 -> x18, Pallas kernels: 13.5 us -> 54 us  [the longest x12 20.3 us: call(): pl.pallas_call(kernel, out_shape=outs, in_specs=specs, out_specs=VMEM if...]
    unnamed x18 -> x96, local copies, waits for them, and re-layouts: 1.48 us -> 15.2 us
    another operation x6 -> x0, other arithmetic: 5.64 us -> none  [the longest x1 1.55 us: local(): jnp.stack([key_self, value_self])]
  transfers between devices with their start and end apart: 5 -> 45, of which waited for: 5 -> 20; matrix products, arithmetic and copies ran while one was open for 3% -> 0% of each run, Pallas kernels for 3% -> 17%
where the time goes in v2:
time: 219 us; the launch traced here: 218 us
  starting transfers between devices  94.5 us (43%)
  Pallas kernels  54 us (25%)
  waiting for transfers between devices  52.1 us (24%)
  local copies, waits for them, and re-layouts  15.2 us (7%)
    ppermute x12, starting transfers between devices, send_y(): return lax.ppermute(value, 'ctx', ctx_shift(k, 0, 0))  50.8 us
    ppermute x12, starting transfers between devices, send_z(): return lax.ppermute(value, 'ctx', ctx_shift(0, k, 0))  23.2 us
    ppermute x12, waiting for transfers between devices, send_z(): return lax.ppermute(value, 'ctx', ctx_shift(0, k, 0))  23.1 us
    pallas_call x12, Pallas kernels, call(): pl.pallas_call(kernel, out_shape=outs, in_specs=specs, out_specs=VMEM if...  20.3 us
    ppermute x12, waiting for transfers between devices, send_y(): return lax.ppermute(value, 'ctx', ctx_shift(k, 0, 0))  19.6 us
    pallas_call x2, Pallas kernels, attention_grads(): pl.pallas_call(functools.partial(attn_kernel, block_rows, base, pad), out...  18.4 us
    unnamed x96, local copies, waits for them, and re-layouts  15.2 us
    ppermute x9, starting transfers between devices, send_x(): return lax.ppermute(value, 'tp', perm)  12.2 us
  transfers between devices with their start and end apart: 45, of which 20 were waited for; matrix products, arithmetic and copies ran while one was open for 0% of the time, Pallas kernels for 17%

profile of v2, /device:TPU:8, one launch (start us, length us, event | category | flops | bytes accessed | tf_op | source)
XLA Modules:
  0.0 217.9 jit_solution(12492801214035484497)
XLA Ops:
  0.6 1.4 shard_map.188
  2.1 4.6 %collective-permute-start.2 = (bf16[2,128,128]{2,1,0:T(8,128)(2,1)}, bf16[2,128,128]{2,1,0:T(8,128)(2,1)S(1)}, u32[]{:S(2)}, u32[]{:S(2)}) collective-permute-start(bf16[2,128,128]{2,1,0:T(8,128)(2,1)} %get-tuple-element.63.refs_0_), channel_id=1, source_target_pairs={{0,48},{8,56},{16,0},{24,8},{32,16},{40,24},{48,32},{56,40},{64,11... | collective-permute-start | bytes 196616 | tf_op jit(solution)/shard_map/ppermute | solution.py:57
  7.4 2.1 collective-permute-done.2.refs_3_
  9.5 3.7 %collective-permute-done.1.refs_2_ = bf16[2,128,128]{2,1,0:T(8,128)(2,1)S(1)} collective-permute-done((bf16[2,128,128]{2,1,0:T(8,128)(2,1)}, bf16[2,128,128]{2,1,0:T(8,128)(2,1)S(1)}, u32[]{:S(2)}, u32[]{:S(2)}) %collective-permute-start.1) | collective-permute-done | bytes 65568 | tf_op jit(solution)/shard_map/ppermute | solution.py:57
  13.8 1.7 shard_map.189.refs_7_
  16.2 2.4 %collective-permute-start.7 = (bf16[4,2,128,128]{3,2,1,0:T(8,128)(2,1)}, bf16[4,2,128,128]{3,2,1,0:T(8,128)(2,1)S(1)}, u32[]{:S(2)}, u32[]{:S(2)}) collective-permute-start(bf16[4,2,128,128]{3,2,1,0:T(8,128)(2,1)} %shard_map.189.refs_7_), channel_id=1, source_target_pairs={{0,128},{8,136},{16,144},{24,152},{32,160},{40,168},{48,176},{56,1... | collective-permute-start | bytes 786440 | tf_op jit(solution)/shard_map/ppermute | solution.py:53
  18.5 1.9 collective-permute-start.6
  20.4 3.4 %collective-permute-done.8.refs_10_ = bf16[4,2,128,128]{3,2,1,0:T(8,128)(2,1)S(1)} collective-permute-done((bf16[4,2,128,128]{3,2,1,0:T(8,128)(2,1)}, bf16[4,2,128,128]{3,2,1,0:T(8,128)(2,1)S(1)}, u32[]{:S(2)}, u32[]{:S(2)}) %collective-permute-start.8) | collective-permute-done | bytes 262176 | tf_op jit(solution)/shard_map/ppermute | solution.py:53
  23.9 5.6 %collective-permute-done.7.refs_9_ = bf16[4,2,128,128]{3,2,1,0:T(8,128)(2,1)S(1)} collective-permute-done((bf16[4,2,128,128]{3,2,1,0:T(8,128)(2,1)}, bf16[4,2,128,128]{3,2,1,0:T(8,128)(2,1)S(1)}, u32[]{:S(2)}, u32[]{:S(2)}) %collective-permute-start.7) | collective-permute-done | bytes 262176 | tf_op jit(solution)/shard_map/ppermute | solution.py:53
  31.3 3.2 %collective-permute-done.5.refs_3_ = bf16[2,64,128]{2,1,0:T(8,128)(2,1)S(1)} collective-permute-done((bf16[2,64,128]{2,1,0:T(8,128)(2,1)}, bf16[2,64,128]{2,1,0:T(8,128)(2,1)S(1)}, u32[]{:S(2)}, u32[]{:S(2)}) %collective-permute-start.5) | collective-permute-done | bytes 32800 | tf_op jit(solution)/shard_map/ppermute | solution.py:57
  34.5 2.5 %collective-permute-start.4 = (bf16[2,64,128]{2,1,0:T(8,128)(2,1)}, bf16[2,64,128]{2,1,0:T(8,128)(2,1)S(1)}, u32[]{:S(2)}, u32[]{:S(2)}) collective-permute-start(bf16[2,64,128]{2,1,0:T(8,128)(2,1)} %get-tuple-element.69.refs_0_), channel_id=1, source_target_pairs={{0,32},{8,40},{16,48},{24,56},{32,0},{40,8},{48,16},{56,24},{64,96... | collective-permute-start | bytes 98312 | tf_op jit(solution)/shard_map/ppermute | solution.py:57
  36.9 2.6 %collective-permute-done.4.refs_2_ = bf16[2,64,128]{2,1,0:T(8,128)(2,1)S(1)} collective-permute-done((bf16[2,64,128]{2,1,0:T(8,128)(2,1)}, bf16[2,64,128]{2,1,0:T(8,128)(2,1)S(1)}, u32[]{:S(2)}, u32[]{:S(2)}) %collective-permute-start.4) | collective-permute-done | bytes 32800 | tf_op jit(solution)/shard_map/ppermute | solution.py:57
  41.3 1.6 rows.1
  42.9 2.5 %collective-permute-done.3.refs_1_ = bf16[2,64,128]{2,1,0:T(8,128)(2,1)S(1)} collective-permute-done((bf16[2,64,128]{2,1,0:T(8,128)(2,1)}, bf16[2,64,128]{2,1,0:T(8,128)(2,1)S(1)}, u32[]{:S(2)}, u32[]{:S(2)}) %collective-permute-start.3) | collective-permute-done | bytes 32800 | tf_op jit(solution)/shard_map/ppermute | solution.py:57
  46.0 1.5 shard_map.190.refs_7_
  52.4 7.0 %shard_map.191 = (bf16[128,1024]{1,0:T(8,128)(2,1)}, bf16[4096,128]{1,0:T(8,128)(2,1)S(1)}, bf16[4096,128]{1,0:T(8,128)(2,1)S(1)}) custom-call(s32[1]{0:T(128)} %bitcast.ctx_ref.refs_0_, s32[8]{0:T(128)S(1)} %copy-done.12, s32[1,256]{1,0:T(1,128)S(1)} %copy-done.10, s32[1,256]{1,0:T(1,128)S(1)} %copy-done.11, f32[8,128]{1,0:T(8,128)S(1)} %broadcast_in_dim.6.refs_4_, ...), custom_call_target="tpu_custom_call" | custom-call | flops 3355443200 | bytes 4980736 | tf_op jit(solution)/shard_map/pallas_call | solution.py:396
  61.6 7.6 %weight_pieces.1 = (bf16[2,2,1024,128]{3,2,1,0:T(8,128)(2,1)}, bf16[2,2,1024,128]{3,2,1,0:T(8,128)(2,1)}, bf16[2,2,1024,128]{3,2,1,0:T(8,128)(2,1)}, bf16[2,2,1024,128]{3,2,1,0:T(8,128)(2,1)}) custom-call(s32[8]{0:T(128)} %and_add_fusion.order_ref, bf16[8192,128]{1,0:T(8,128)(2,1)} %wk_ref.1, bf16[8192,128]{1,0:T(8,128)(2,1)} %wv_ref.1), custom_call_target="tpu_custom_call" | custom-call | tf_op jit(solution)/shard_map/weight_pieces/pallas_call | solution.py:149
  69.2 1.7 collective-permute-start.21
  71.0 2.7 %collective-permute-start.22 = (bf16[2,2,1024,128]{3,2,1,0:T(8,128)(2,1)}, bf16[2,2,1024,128]{3,2,1,0:T(8,128)(2,1)}, u32[]{:S(2)}, u32[]{:S(2)}) collective-permute-start(bf16[2,2,1024,128]{3,2,1,0:T(8,128)(2,1)} %get-tuple-element.85), channel_id=1, source_target_pairs={{0,2},{1,3},{2,0},{3,1},{4,6},{5,7},{6,4},{7,5},{8,10},{9,11},{10,... | collective-permute-start | bytes 3145736 | tf_op jit(solution)/shard_map/ppermute | solution.py:66
  73.7 15.2 %collective-permute-start.15 = (bf16[4,2,64,128]{3,2,1,0:T(8,128)(2,1)S(1)}, bf16[4,2,64,128]{3,2,1,0:T(8,128)(2,1)S(1)}, u32[]{:S(2)}, u32[]{:S(2)}) collective-permute-start(bf16[4,2,64,128]{3,2,1,0:T(8,128)(2,1)S(1)} %copy-done.3), channel_id=1, source_target_pairs={{0,128},{8,136},{16,144},{24,152},{32,160},{40,168},{48,176},{56,1... | collective-permute-start | bytes 393224 | tf_op jit(solution)/shard_map/ppermute | solution.py:53
  88.9 2.6 %collective-permute-start.14 = (bf16[4,2,64,128]{3,2,1,0:T(8,128)(2,1)S(1)}, bf16[4,2,64,128]{3,2,1,0:T(8,128)(2,1)S(1)}, u32[]{:S(2)}, u32[]{:S(2)}) collective-permute-start(bf16[4,2,64,128]{3,2,1,0:T(8,128)(2,1)S(1)} %copy-done.3), channel_id=1, source_target_pairs={{0,64},{8,72},{16,80},{24,88},{32,96},{40,104},{48,112},{56,120},{... | collective-permute-start | bytes 393224 | tf_op jit(solution)/shard_map/ppermute | solution.py:53
  92.5 3.7 %collective-permute-done.14.refs_8_ = bf16[4,2,64,128]{3,2,1,0:T(8,128)(2,1)S(1)} collective-permute-done((bf16[4,2,64,128]{3,2,1,0:T(8,128)(2,1)S(1)}, bf16[4,2,64,128]{3,2,1,0:T(8,128)(2,1)S(1)}, u32[]{:S(2)}, u32[]{:S(2)}) %collective-permute-start.14) | collective-permute-done | bytes 131104 | tf_op jit(solution)/shard_map/ppermute | solution.py:53
  96.2 1.4 collective-permute-start.23
  99.5 2.6 %shard_map.192 = (bf16[1024,128]{1,0:T(8,128)(2,1)}, bf16[1024,128]{1,0:T(8,128)(2,1)}, bf16[1024,128]{1,0:T(8,128)(2,1)}, bf16[1024,128]{1,0:T(8,128)(2,1)}) custom-call(bf16[4096,128]{1,0:T(8,128)(2,1)} %copy-done, bf16[4096,128]{1,0:T(8,128)(2,1)} %collective-permute-done.13.other_ref), custom_call_target="tpu_custom_call" | custom-call | tf_op jit(solution)/shard_map/pallas_call | solution.py:260
  102.2 11.4 %shard_map.193 = (bf16[128,1024]{1,0:T(8,128)(2,1)}, bf16[2064,128]{1,0:T(8,128)(2,1)S(1)}, bf16[2064,128]{1,0:T(8,128)(2,1)S(1)}) custom-call(s32[1]{0:T(128)} %bitcast.ctx_ref.refs_0_, s32[8]{0:T(128)S(1)} %copy-done.13, s32[1,256]{1,0:T(1,128)S(1)} %broadcast_in_dim.7.refs_2_, s32[1,256]{1,0:T(1,128)S(1)} %copy-done.9, f32[8,128]{1,0:T(8,128)S(1)} %copy-done.4, ...), custom_call_target="tpu_custom_call" | custom-call | flops 2684354560 | bytes 2883584 | tf_op jit(solution)/shard_map/pallas_call | solution.py:396
  114.4 5.9 %collective-permute-start.24 = (bf16[1024,128]{1,0:T(8,128)(2,1)S(1)}, bf16[1024,128]{1,0:T(8,128)(2,1)S(1)}, u32[]{:S(2)}, u32[]{:S(2)}) collective-permute-start(bf16[1024,128]{1,0:T(8,128)(2,1)S(1)} %copy-done.44), channel_id=1, source_target_pairs={{0,64},{8,72},{16,80},{24,88},{32,96},{40,104},{48,112},{56,120},{... | collective-permute-start | bytes 786440 | tf_op jit(solution)/shard_map/ppermute | solution.py:53
  121.7 14.5 %collective-permute-start.26 = (bf16[1024,128]{1,0:T(8,128)(2,1)S(1)}, bf16[1024,128]{1,0:T(8,128)(2,1)S(1)}, u32[]{:S(2)}, u32[]{:S(2)}) collective-permute-start(bf16[1024,128]{1,0:T(8,128)(2,1)S(1)} %copy-done.42), channel_id=1, source_target_pairs={{0,192},{8,200},{16,208},{24,216},{32,224},{40,232},{48,240},{56,2... | collective-permute-start | bytes 786440 | tf_op jit(solution)/shard_map/ppermute | solution.py:53
  136.2 5.1 %collective-permute-done.26.s3_ref = bf16[1024,128]{1,0:T(8,128)(2,1)S(1)} collective-permute-done((bf16[1024,128]{1,0:T(8,128)(2,1)S(1)}, bf16[1024,128]{1,0:T(8,128)(2,1)S(1)}, u32[]{:S(2)}, u32[]{:S(2)}) %collective-permute-start.26) | collective-permute-done | bytes 262176 | tf_op jit(solution)/shard_map/ppermute | solution.py:53
  141.9 2.0 shard_map.194
  144.7 2.0 shard_map.195
  147.4 1.6 collective-permute-start.28
  149.1 3.9 %collective-permute-start.32 = (bf16[528,128]{1,0:T(8,128)(2,1)}, bf16[528,128]{1,0:T(8,128)(2,1)S(1)}, u32[]{:S(2)}, u32[]{:S(2)}) collective-permute-start(bf16[528,128]{1,0:T(8,128)(2,1)} %get-tuple-element.104), channel_id=1, source_target_pairs={{0,128},{8,136},{16,144},{24,152},{32,160},{40,168},{48,176},{56,1... | collective-permute-start | bytes 405512 | tf_op jit(solution)/shard_map/ppermute | solution.py:53
  154.1 4.1 %collective-permute-start.29 = (bf16[256,128]{1,0:T(8,128)(2,1)}, bf16[256,128]{1,0:T(8,128)(2,1)S(1)}, u32[]{:S(2)}, u32[]{:S(2)}) collective-permute-start(bf16[256,128]{1,0:T(8,128)(2,1)} %get-tuple-element.97), channel_id=1, source_target_pairs={{0,32},{8,40},{16,48},{24,56},{32,0},{40,8},{48,16},{56,24},{64,96... | collective-permute-start | bytes 196616 | tf_op jit(solution)/shard_map/ppermute | solution.py:57
  158.2 2.9 %collective-permute-start.30 = (bf16[256,128]{1,0:T(8,128)(2,1)}, bf16[256,128]{1,0:T(8,128)(2,1)S(1)}, u32[]{:S(2)}, u32[]{:S(2)}) collective-permute-start(bf16[256,128]{1,0:T(8,128)(2,1)} %get-tuple-element.98), channel_id=1, source_target_pairs={{0,48},{8,56},{16,0},{24,8},{32,16},{40,24},{48,32},{56,40},{64,11... | collective-permute-start | bytes 196616 | tf_op jit(solution)/shard_map/ppermute | solution.py:57
  161.1 2.2 %collective-permute-done.30.s3_ref = bf16[256,128]{1,0:T(8,128)(2,1)S(1)} collective-permute-done((bf16[256,128]{1,0:T(8,128)(2,1)}, bf16[256,128]{1,0:T(8,128)(2,1)S(1)}, u32[]{:S(2)}, u32[]{:S(2)}) %collective-permute-start.30) | collective-permute-done | bytes 65568 | tf_op jit(solution)/shard_map/ppermute | solution.py:57
  164.0 1.6 shard_map.196
  169.1 1.8 shard_map.197
  173.4 3.1 %shard_map.198 = bf16[128,1024]{1,0:T(8,128)(2,1)} custom-call(bf16[256,128]{1,0:T(8,128)(2,1)} %get-tuple-element.109.refs_0_, bf16[256,128]{1,0:T(8,128)(2,1)} %copy-done.18, bf16[256,128]{1,0:T(8,128)(2,1)} %copy-done.17, bf16[256,128]{1,0:T(8,128)(2,1)} %copy-done.16, bf16[2,2,1024,128]{3,2,1,0:T(8,128)(2,1)} %get-tuple-element.108.refs_4_, ...), custom_call_target="tpu_custom_call" | custom-call | flops 268435456 | bytes 2097152 | tf_op jit(solution)/shard_map/pallas_call | solution.py:231
  176.4 5.4 %collective-permute-start.37 = (bf16[128,1024]{1,0:T(8,128)(2,1)}, bf16[128,1024]{1,0:T(8,128)(2,1)S(1)}, u32[]{:S(2)}, u32[]{:S(2)}) collective-permute-start(bf16[128,1024]{1,0:T(8,128)(2,1)} %shard_map.198), channel_id=1, source_target_pairs={{0,4},{1,5},{2,6},{3,7},{4,0},{5,1},{6,2},{7,3},{8,12},{9,13},{10,... | collective-permute-start | bytes 786440 | tf_op jit(solution)/shard_map/ppermute | solution.py:70
  183.2 3.2 %collective-permute-start.39 = (bf16[144,128]{1,0:T(8,128)(2,1)S(1)}, bf16[144,128]{1,0:T(8,128)(2,1)S(1)}, u32[]{:S(2)}, u32[]{:S(2)}) collective-permute-start(bf16[144,128]{1,0:T(8,128)(2,1)S(1)} %copy-done.46), channel_id=1, source_target_pairs={{0,32},{8,40},{16,48},{24,56},{32,0},{40,8},{48,16},{56,24},{64,96... | collective-permute-start | bytes 110600 | tf_op jit(solution)/shard_map/ppermute | solution.py:57
  186.4 5.8 %collective-permute-done.38.s1_ref = bf16[144,128]{1,0:T(8,128)(2,1)S(1)} collective-permute-done((bf16[144,128]{1,0:T(8,128)(2,1)S(1)}, bf16[144,128]{1,0:T(8,128)(2,1)S(1)}, u32[]{:S(2)}, u32[]{:S(2)}) %collective-permute-start.38) | collective-permute-done | bytes 36896 | tf_op jit(solution)/shard_map/ppermute | solution.py:57
  194.5 1.5 shard_map.201
  195.9 1.8 collective-permute-start.43
  200.0 3.1 %collective-permute-done.42.g2 = f32[8,128]{1,0:T(8,128)S(1)} collective-permute-done((f32[8,128]{1,0:T(8,128)}, f32[8,128]{1,0:T(8,128)S(1)}, u32[]{:S(2)}, u32[]{:S(2)}) %collective-permute-start.42) | collective-permute-done | bytes 4128 | tf_op jit(solution)/shard_map/ppermute | solution.py:66
  205.8 2.5 %collective-permute-start.44 = (f32[8,128]{1,0:T(8,128)}, f32[8,128]{1,0:T(8,128)S(1)}, u32[]{:S(2)}, u32[]{:S(2)}) collective-permute-start(f32[8,128]{1,0:T(8,128)} %shard_map.202.a_ref), channel_id=1, source_target_pairs={{0,4},{1,5},{2,6},{3,7},{4,0},{5,1},{6,2},{7,3},{8,12},{9,13},{10,... | collective-permute-start | bytes 12296 | tf_op jit(solution)/shard_map/ppermute | solution.py:70
  208.3 3.1 %shard_map.199.a_ref = f32[128,1024]{1,0:T(8,128)} custom-call(bf16[256,128]{1,0:T(8,128)(2,1)} %get-tuple-element.109.refs_0_, bf16[256,128]{1,0:T(8,128)(2,1)} %copy-done.18, bf16[256,128]{1,0:T(8,128)(2,1)} %copy-done.17, bf16[256,128]{1,0:T(8,128)(2,1)} %copy-done.16, bf16[2,2,1024,128]{3,2,1,0:T(8,128)(2,1)} %get-tuple-element.108.refs_4_, ...), custom_call_target="tpu_custom_call" | custom-call | flops 268435456 | bytes 2097152 | tf_op jit(solution)/shard_map/pallas_call | solution.py:231
  211.4 2.1 collective-permute-done.44.b_ref
  216.0 1.9 shard_map.200
  (159 shorter events, 38.7 us)
Async XLA Ops:
  2.1 7.4 %collective-permute-start.2 = (bf16[2,128,128]{2,1,0:T(8,128)(2,1)}, bf16[2,128,128]{2,1,0:T(8,128)(2,1)S(1)}, u32[]{:S(2)}, u32[]{:S(2)}) collective-permute-start(bf16[2,128,128]{2,1,0:T(8,128)(2,1)} %get-tuple-element.63.refs_0_), channel_id=1, source_target_pairs={{0,48},{8,56},{16,0},{24,8},{32,16},{40,24},{48,32},{56,40},{64,11... | collective-permute-start | bytes 196616 | tf_op jit(solution)/shard_map/ppermute | solution.py:57
  6.7 6.5 %collective-permute-start.1 = (bf16[2,128,128]{2,1,0:T(8,128)(2,1)}, bf16[2,128,128]{2,1,0:T(8,128)(2,1)S(1)}, u32[]{:S(2)}, u32[]{:S(2)}) collective-permute-start(bf16[2,128,128]{2,1,0:T(8,128)(2,1)} %get-tuple-element.63.refs_0_), channel_id=1, source_target_pairs={{0,32},{8,40},{16,48},{24,56},{32,0},{40,8},{48,16},{56,24},{64,96... | collective-permute-start | bytes 196616 | tf_op jit(solution)/shard_map/ppermute | solution.py:57
  6.7 6.5 %collective-permute-start = (bf16[2,128,128]{2,1,0:T(8,128)(2,1)}, bf16[2,128,128]{2,1,0:T(8,128)(2,1)S(1)}, u32[]{:S(2)}, u32[]{:S(2)}) collective-permute-start(bf16[2,128,128]{2,1,0:T(8,128)(2,1)} %get-tuple-element.63.refs_0_), channel_id=1, source_target_pairs={{0,16},{8,24},{16,32},{24,40},{32,48},{40,56},{48,0},{56,8},{64,80... | collective-permute-start | bytes 196616 | tf_op jit(solution)/shard_map/ppermute | solution.py:57
  15.5 8.4 %collective-permute-start.8 = (bf16[4,2,128,128]{3,2,1,0:T(8,128)(2,1)}, bf16[4,2,128,128]{3,2,1,0:T(8,128)(2,1)S(1)}, u32[]{:S(2)}, u32[]{:S(2)}) collective-permute-start(bf16[4,2,128,128]{3,2,1,0:T(8,128)(2,1)} %shard_map.189.refs_7_), channel_id=1, source_target_pairs={{0,192},{8,200},{16,208},{24,216},{32,224},{40,232},{48,240},{56,2... | collective-permute-start | bytes 786440 | tf_op jit(solution)/shard_map/ppermute | solution.py:53
  16.2 13.3 %collective-permute-start.7 = (bf16[4,2,128,128]{3,2,1,0:T(8,128)(2,1)}, bf16[4,2,128,128]{3,2,1,0:T(8,128)(2,1)S(1)}, u32[]{:S(2)}, u32[]{:S(2)}) collective-permute-start(bf16[4,2,128,128]{3,2,1,0:T(8,128)(2,1)} %shard_map.189.refs_7_), channel_id=1, source_target_pairs={{0,128},{8,136},{16,144},{24,152},{32,160},{40,168},{48,176},{56,1... | collective-permute-start | bytes 786440 | tf_op jit(solution)/shard_map/ppermute | solution.py:53
  18.5 11.8 %collective-permute-start.6 = (bf16[4,2,128,128]{3,2,1,0:T(8,128)(2,1)}, bf16[4,2,128,128]{3,2,1,0:T(8,128)(2,1)S(1)}, u32[]{:S(2)}, u32[]{:S(2)}) collective-permute-start(bf16[4,2,128,128]{3,2,1,0:T(8,128)(2,1)} %shard_map.189.refs_7_), channel_id=1, source_target_pairs={{0,64},{8,72},{16,80},{24,88},{32,96},{40,104},{48,112},{56,120},{... | collective-permute-start | bytes 786440 | tf_op jit(solution)/shard_map/ppermute | solution.py:53
  20.4 27.1 %collective-permute-start.9 = (bf16[4,2,128,128]{3,2,1,0:T(8,128)(2,1)}, bf16[4,2,128,128]{3,2,1,0:T(8,128)(2,1)S(1)}, u32[]{:S(2)}, u32[]{:S(2)}) collective-permute-start(bf16[4,2,128,128]{3,2,1,0:T(8,128)(2,1)} %shard_map.189.refs_7_), channel_id=1, source_target_pairs={{0,8},{8,0},{16,24},{24,16},{32,40},{40,32},{48,56},{56,48},{64,72... | collective-permute-start | bytes 786440 | tf_op jit(solution)/shard_map/ppermute | solution.py:61
  23.9 23.6 %collective-permute-start.12 = (bf16[4,2,128,128]{3,2,1,0:T(8,128)(2,1)S(1)}, bf16[4,2,128,128]{3,2,1,0:T(8,128)(2,1)S(1)}, u32[]{:S(2)}, u32[]{:S(2)}) collective-permute-start(bf16[4,2,128,128]{3,2,1,0:T(8,128)(2,1)S(1)} %collective-permute-done.8.refs_10_), channel_id=1, source_target_pairs={{0,8},{8,0},{16,24},{24,16},{32,40},{40,32},{48,56},{56,48},{64,72... | collective-permute-start | bytes 786440 | tf_op jit(solution)/shard_map/ppermute | solution.py:61
  29.5 18.0 %collective-permute-start.11 = (bf16[4,2,128,128]{3,2,1,0:T(8,128)(2,1)S(1)}, bf16[4,2,128,128]{3,2,1,0:T(8,128)(2,1)S(1)}, u32[]{:S(2)}, u32[]{:S(2)}) collective-permute-start(bf16[4,2,128,128]{3,2,1,0:T(8,128)(2,1)S(1)} %collective-permute-done.7.refs_9_), channel_id=1, source_target_pairs={{0,8},{8,0},{16,24},{24,16},{32,40},{40,32},{48,56},{56,48},{64,72... | collective-permute-start | bytes 786440 | tf_op jit(solution)/shard_map/ppermute | solution.py:61
  30.3 17.2 %collective-permute-start.10 = (bf16[4,2,128,128]{3,2,1,0:T(8,128)(2,1)S(1)}, bf16[4,2,128,128]{3,2,1,0:T(8,128)(2,1)S(1)}, u32[]{:S(2)}, u32[]{:S(2)}) collective-permute-start(bf16[4,2,128,128]{3,2,1,0:T(8,128)(2,1)S(1)} %collective-permute-done.6.refs_8_), channel_id=1, source_target_pairs={{0,8},{8,0},{16,24},{24,16},{32,40},{40,32},{48,56},{56,48},{64,72... | collective-permute-start | bytes 786440 | tf_op jit(solution)/shard_map/ppermute | solution.py:61
  30.3 4.1 %collective-permute-start.5 = (bf16[2,64,128]{2,1,0:T(8,128)(2,1)}, bf16[2,64,128]{2,1,0:T(8,128)(2,1)S(1)}, u32[]{:S(2)}, u32[]{:S(2)}) collective-permute-start(bf16[2,64,128]{2,1,0:T(8,128)(2,1)} %get-tuple-element.69.refs_0_), channel_id=1, source_target_pairs={{0,48},{8,56},{16,0},{24,8},{32,16},{40,24},{48,32},{56,40},{64,11... | collective-permute-start | bytes 98312 | tf_op jit(solution)/shard_map/ppermute | solution.py:57
  34.5 5.0 %collective-permute-start.4 = (bf16[2,64,128]{2,1,0:T(8,128)(2,1)}, bf16[2,64,128]{2,1,0:T(8,128)(2,1)S(1)}, u32[]{:S(2)}, u32[]{:S(2)}) collective-permute-start(bf16[2,64,128]{2,1,0:T(8,128)(2,1)} %get-tuple-element.69.refs_0_), channel_id=1, source_target_pairs={{0,32},{8,40},{16,48},{24,56},{32,0},{40,8},{48,16},{56,24},{64,96... | collective-permute-start | bytes 98312 | tf_op jit(solution)/shard_map/ppermute | solution.py:57
  39.5 5.9 %collective-permute-start.3 = (bf16[2,64,128]{2,1,0:T(8,128)(2,1)}, bf16[2,64,128]{2,1,0:T(8,128)(2,1)S(1)}, u32[]{:S(2)}, u32[]{:S(2)}) collective-permute-start(bf16[2,64,128]{2,1,0:T(8,128)(2,1)} %get-tuple-element.69.refs_0_), channel_id=1, source_target_pairs={{0,16},{8,24},{16,32},{24,40},{32,48},{40,56},{48,0},{56,8},{64,80... | collective-permute-start | bytes 98312 | tf_op jit(solution)/shard_map/ppermute | solution.py:57
  60.5 38.6 %collective-permute-start.13 = (bf16[4096,128]{1,0:T(8,128)(2,1)S(1)}, bf16[4096,128]{1,0:T(8,128)(2,1)}, u32[]{:S(2)}, u32[]{:S(2)}) collective-permute-start(bf16[4096,128]{1,0:T(8,128)(2,1)S(1)} %get-tuple-element.73), channel_id=1, source_target_pairs={{0,8},{8,0},{16,24},{24,16},{32,40},{40,32},{48,56},{56,48},{64,72... | collective-permute-start | bytes 3145736 | tf_op jit(solution)/shard_map/ppermute | solution.py:61
  61.1 27.9 %collective-permute-start.16 = (bf16[4,2,64,128]{3,2,1,0:T(8,128)(2,1)S(1)}, bf16[4,2,64,128]{3,2,1,0:T(8,128)(2,1)S(1)}, u32[]{:S(2)}, u32[]{:S(2)}) collective-permute-start(bf16[4,2,64,128]{3,2,1,0:T(8,128)(2,1)S(1)} %copy-done.3), channel_id=1, source_target_pairs={{0,192},{8,200},{16,208},{24,216},{32,224},{40,232},{48,240},{56,2... | collective-permute-start | bytes 393224 | tf_op jit(solution)/shard_map/ppermute | solution.py:53
  69.2 32.9 %copy-start.8 = (bf16[128,1024]{1,0:T(8,128)(2,1)S(1)}, bf16[128,1024]{1,0:T(8,128)(2,1)}, u32[]{:S(2)}) copy-start(bf16[128,1024]{1,0:T(8,128)(2,1)} %refs_6_.3) | copy-start | bytes 786436
  69.2 32.9 %copy-start.9 = (s32[1,256]{1,0:T(1,128)S(1)}, s32[1,256]{1,0:T(1,128)}, u32[]{:S(2)}) copy-start(s32[1,256]{1,0:T(1,128)} %get-tuple-element.75.refs_3_) | copy-start | bytes 3076
  69.2 51.1 %collective-permute-start.21 = (bf16[2,2,1024,128]{3,2,1,0:T(8,128)(2,1)}, bf16[2,2,1024,128]{3,2,1,0:T(8,128)(2,1)S(1)}, u32[]{:S(2)}, u32[]{:S(2)}) collective-permute-start(bf16[2,2,1024,128]{3,2,1,0:T(8,128)(2,1)} %get-tuple-element.84), channel_id=1, source_target_pairs={{0,1},{1,2},{2,3},{3,0},{4,5},{5,6},{6,7},{7,4},{8,9},{9,10},{10,1... | collective-permute-start | bytes 3145736 | tf_op jit(solution)/shard_map/ppermute | solution.py:66
  71.0 50.7 %collective-permute-start.22 = (bf16[2,2,1024,128]{3,2,1,0:T(8,128)(2,1)}, bf16[2,2,1024,128]{3,2,1,0:T(8,128)(2,1)}, u32[]{:S(2)}, u32[]{:S(2)}) collective-permute-start(bf16[2,2,1024,128]{3,2,1,0:T(8,128)(2,1)} %get-tuple-element.85), channel_id=1, source_target_pairs={{0,2},{1,3},{2,0},{3,1},{4,6},{5,7},{6,4},{7,5},{8,10},{9,11},{10,... | collective-permute-start | bytes 3145736 | tf_op jit(solution)/shard_map/ppermute | solution.py:66
  73.7 18.8 %collective-permute-start.15 = (bf16[4,2,64,128]{3,2,1,0:T(8,128)(2,1)S(1)}, bf16[4,2,64,128]{3,2,1,0:T(8,128)(2,1)S(1)}, u32[]{:S(2)}, u32[]{:S(2)}) collective-permute-start(bf16[4,2,64,128]{3,2,1,0:T(8,128)(2,1)S(1)} %copy-done.3), channel_id=1, source_target_pairs={{0,128},{8,136},{16,144},{24,152},{32,160},{40,168},{48,176},{56,1... | collective-permute-start | bytes 393224 | tf_op jit(solution)/shard_map/ppermute | solution.py:53
  88.9 7.3 %collective-permute-start.14 = (bf16[4,2,64,128]{3,2,1,0:T(8,128)(2,1)S(1)}, bf16[4,2,64,128]{3,2,1,0:T(8,128)(2,1)S(1)}, u32[]{:S(2)}, u32[]{:S(2)}) collective-permute-start(bf16[4,2,64,128]{3,2,1,0:T(8,128)(2,1)S(1)} %copy-done.3), channel_id=1, source_target_pairs={{0,64},{8,72},{16,80},{24,88},{32,96},{40,104},{48,112},{56,120},{... | collective-permute-start | bytes 393224 | tf_op jit(solution)/shard_map/ppermute | solution.py:53
  92.5 5.1 %collective-permute-start.17 = (bf16[4,2,64,128]{3,2,1,0:T(8,128)(2,1)S(1)}, bf16[4,2,64,128]{3,2,1,0:T(8,128)(2,1)S(1)}, u32[]{:S(2)}, u32[]{:S(2)}) collective-permute-start(bf16[4,2,64,128]{3,2,1,0:T(8,128)(2,1)S(1)} %copy-done.3), channel_id=1, source_target_pairs={{0,8},{8,0},{16,24},{24,16},{32,40},{40,32},{48,56},{56,48},{64,72... | collective-permute-start | bytes 393224 | tf_op jit(solution)/shard_map/ppermute | solution.py:61
  96.2 39.9 %collective-permute-start.23 = (bf16[2,2,1024,128]{3,2,1,0:T(8,128)(2,1)}, bf16[2,2,1024,128]{3,2,1,0:T(8,128)(2,1)}, u32[]{:S(2)}, u32[]{:S(2)}) collective-permute-start(bf16[2,2,1024,128]{3,2,1,0:T(8,128)(2,1)} %get-tuple-element.86), channel_id=1, source_target_pairs={{0,3},{1,0},{2,1},{3,2},{4,7},{5,4},{6,5},{7,6},{8,11},{9,8},{10,9... | collective-permute-start | bytes 3145736 | tf_op jit(solution)/shard_map/ppermute | solution.py:66
  97.7 1.3 collective-permute-start.18
  99.0 3.1 %collective-permute-start.19 = (bf16[4,2,64,128]{3,2,1,0:T(8,128)(2,1)S(1)}, bf16[4,2,64,128]{3,2,1,0:T(8,128)(2,1)S(1)}, u32[]{:S(2)}, u32[]{:S(2)}) collective-permute-start(bf16[4,2,64,128]{3,2,1,0:T(8,128)(2,1)S(1)} %collective-permute-done.15.refs_9_), channel_id=1, source_target_pairs={{0,8},{8,0},{16,24},{24,16},{32,40},{40,32},{48,56},{56,48},{64,72... | collective-permute-start | bytes 393224 | tf_op jit(solution)/shard_map/ppermute | solution.py:61
  99.2 2.9 %collective-permute-start.20 = (bf16[4,2,64,128]{3,2,1,0:T(8,128)(2,1)S(1)}, bf16[4,2,64,128]{3,2,1,0:T(8,128)(2,1)S(1)}, u32[]{:S(2)}, u32[]{:S(2)}) collective-permute-start(bf16[4,2,64,128]{3,2,1,0:T(8,128)(2,1)S(1)} %collective-permute-done.16.refs_10_), channel_id=1, source_target_pairs={{0,8},{8,0},{16,24},{24,16},{32,40},{40,32},{48,56},{56,48},{64,72... | collective-permute-start | bytes 393224 | tf_op jit(solution)/shard_map/ppermute | solution.py:61
  114.4 29.5 %collective-permute-start.27 = (bf16[2064,128]{1,0:T(8,128)(2,1)S(1)}, bf16[2064,128]{1,0:T(8,128)(2,1)S(1)}, u32[]{:S(2)}, u32[]{:S(2)}) collective-permute-start(bf16[2064,128]{1,0:T(8,128)(2,1)S(1)} %get-tuple-element.93), channel_id=1, source_target_pairs={{0,8},{8,0},{16,24},{24,16},{32,40},{40,32},{48,56},{56,48},{64,72... | collective-permute-start | bytes 1585160 | tf_op jit(solution)/shard_map/ppermute | solution.py:61
  114.4 21.8 %collective-permute-start.24 = (bf16[1024,128]{1,0:T(8,128)(2,1)S(1)}, bf16[1024,128]{1,0:T(8,128)(2,1)S(1)}, u32[]{:S(2)}, u32[]{:S(2)}) collective-permute-start(bf16[1024,128]{1,0:T(8,128)(2,1)S(1)} %copy-done.44), channel_id=1, source_target_pairs={{0,64},{8,72},{16,80},{24,88},{32,96},{40,104},{48,112},{56,120},{... | collective-permute-start | bytes 786440 | tf_op jit(solution)/shard_map/ppermute | solution.py:53
  120.3 52.4 %copy-start.14 = (bf16[2,2,1024,128]{3,2,1,0:T(8,128)(2,1)}, bf16[2,2,1024,128]{3,2,1,0:T(8,128)(2,1)S(1)}, u32[]{:S(2)}) copy-start(bf16[2,2,1024,128]{3,2,1,0:T(8,128)(2,1)S(1)} %collective-permute-done.21.refs_5_) | copy-start | bytes 3145732
  120.3 15.8 %collective-permute-start.25 = (bf16[1024,128]{1,0:T(8,128)(2,1)S(1)}, bf16[1024,128]{1,0:T(8,128)(2,1)S(1)}, u32[]{:S(2)}, u32[]{:S(2)}) collective-permute-start(bf16[1024,128]{1,0:T(8,128)(2,1)S(1)} %copy-done.43), channel_id=1, source_target_pairs={{0,128},{8,136},{16,144},{24,152},{32,160},{40,168},{48,176},{56,1... | collective-permute-start | bytes 786440 | tf_op jit(solution)/shard_map/ppermute | solution.py:53
  121.7 19.6 %collective-permute-start.26 = (bf16[1024,128]{1,0:T(8,128)(2,1)S(1)}, bf16[1024,128]{1,0:T(8,128)(2,1)S(1)}, u32[]{:S(2)}, u32[]{:S(2)}) collective-permute-start(bf16[1024,128]{1,0:T(8,128)(2,1)S(1)} %copy-done.42), channel_id=1, source_target_pairs={{0,192},{8,200},{16,208},{24,216},{32,224},{40,232},{48,240},{56,2... | collective-permute-start | bytes 786440 | tf_op jit(solution)/shard_map/ppermute | solution.py:53
  146.7 19.6 %collective-permute-start.31 = (bf16[528,128]{1,0:T(8,128)(2,1)}, bf16[528,128]{1,0:T(8,128)(2,1)S(1)}, u32[]{:S(2)}, u32[]{:S(2)}) collective-permute-start(bf16[528,128]{1,0:T(8,128)(2,1)} %get-tuple-element.103), channel_id=1, source_target_pairs={{0,64},{8,72},{16,80},{24,88},{32,96},{40,104},{48,112},{56,120},{... | collective-permute-start | bytes 405512 | tf_op jit(solution)/shard_map/ppermute | solution.py:53
  147.4 10.8 %collective-permute-start.28 = (bf16[256,128]{1,0:T(8,128)(2,1)}, bf16[256,128]{1,0:T(8,128)(2,1)S(1)}, u32[]{:S(2)}, u32[]{:S(2)}) collective-permute-start(bf16[256,128]{1,0:T(8,128)(2,1)} %get-tuple-element.96), channel_id=1, source_target_pairs={{0,16},{8,24},{16,32},{24,40},{32,48},{40,56},{48,0},{56,8},{64,80... | collective-permute-start | bytes 196616 | tf_op jit(solution)/shard_map/ppermute | solution.py:57
  149.1 18.7 %collective-permute-start.32 = (bf16[528,128]{1,0:T(8,128)(2,1)}, bf16[528,128]{1,0:T(8,128)(2,1)S(1)}, u32[]{:S(2)}, u32[]{:S(2)}) collective-permute-start(bf16[528,128]{1,0:T(8,128)(2,1)} %get-tuple-element.104), channel_id=1, source_target_pairs={{0,128},{8,136},{16,144},{24,152},{32,160},{40,168},{48,176},{56,1... | collective-permute-start | bytes 405512 | tf_op jit(solution)/shard_map/ppermute | solution.py:53
  152.9 14.9 %collective-permute-start.33 = (bf16[528,128]{1,0:T(8,128)(2,1)}, bf16[528,128]{1,0:T(8,128)(2,1)S(1)}, u32[]{:S(2)}, u32[]{:S(2)}) collective-permute-start(bf16[528,128]{1,0:T(8,128)(2,1)} %get-tuple-element.105), channel_id=1, source_target_pairs={{0,192},{8,200},{16,208},{24,216},{32,224},{40,232},{48,240},{56,2... | collective-permute-start | bytes 405512 | tf_op jit(solution)/shard_map/ppermute | solution.py:53
  154.1 7.0 %collective-permute-start.29 = (bf16[256,128]{1,0:T(8,128)(2,1)}, bf16[256,128]{1,0:T(8,128)(2,1)S(1)}, u32[]{:S(2)}, u32[]{:S(2)}) collective-permute-start(bf16[256,128]{1,0:T(8,128)(2,1)} %get-tuple-element.97), channel_id=1, source_target_pairs={{0,32},{8,40},{16,48},{24,56},{32,0},{40,8},{48,16},{56,24},{64,96... | collective-permute-start | bytes 196616 | tf_op jit(solution)/shard_map/ppermute | solution.py:57
  158.2 5.1 %collective-permute-start.30 = (bf16[256,128]{1,0:T(8,128)(2,1)}, bf16[256,128]{1,0:T(8,128)(2,1)S(1)}, u32[]{:S(2)}, u32[]{:S(2)}) collective-permute-start(bf16[256,128]{1,0:T(8,128)(2,1)} %get-tuple-element.98), channel_id=1, source_target_pairs={{0,48},{8,56},{16,0},{24,8},{32,16},{40,24},{48,32},{56,40},{64,11... | collective-permute-start | bytes 196616 | tf_op jit(solution)/shard_map/ppermute | solution.py:57
  165.6 5.3 %collective-permute-start.36 = (bf16[256,128]{1,0:T(8,128)(2,1)}, bf16[256,128]{1,0:T(8,128)(2,1)S(1)}, u32[]{:S(2)}, u32[]{:S(2)}) collective-permute-start(bf16[256,128]{1,0:T(8,128)(2,1)} %get-tuple-element.109.refs_0_), channel_id=1, source_target_pairs={{0,3},{1,0},{2,1},{3,2},{4,7},{5,4},{6,5},{7,6},{8,11},{9,8},{10,9... | collective-permute-start | bytes 196616 | tf_op jit(solution)/shard_map/ppermute | solution.py:66
  165.6 6.0 %collective-permute-start.35 = (bf16[256,128]{1,0:T(8,128)(2,1)}, bf16[256,128]{1,0:T(8,128)(2,1)S(1)}, u32[]{:S(2)}, u32[]{:S(2)}) collective-permute-start(bf16[256,128]{1,0:T(8,128)(2,1)} %get-tuple-element.109.refs_0_), channel_id=1, source_target_pairs={{0,2},{1,3},{2,0},{3,1},{4,6},{5,7},{6,4},{7,5},{8,10},{9,11},{10,... | collective-permute-start | bytes 196616 | tf_op jit(solution)/shard_map/ppermute | solution.py:66
  166.4 6.4 %collective-permute-start.34 = (bf16[256,128]{1,0:T(8,128)(2,1)}, bf16[256,128]{1,0:T(8,128)(2,1)S(1)}, u32[]{:S(2)}, u32[]{:S(2)}) collective-permute-start(bf16[256,128]{1,0:T(8,128)(2,1)} %get-tuple-element.109.refs_0_), channel_id=1, source_target_pairs={{0,1},{1,2},{2,3},{3,0},{4,5},{5,6},{6,7},{7,4},{8,9},{9,10},{10,1... | collective-permute-start | bytes 196616 | tf_op jit(solution)/shard_map/ppermute | solution.py:66
  176.4 38.9 %collective-permute-start.37 = (bf16[128,1024]{1,0:T(8,128)(2,1)}, bf16[128,1024]{1,0:T(8,128)(2,1)S(1)}, u32[]{:S(2)}, u32[]{:S(2)}) collective-permute-start(bf16[128,1024]{1,0:T(8,128)(2,1)} %shard_map.198), channel_id=1, source_target_pairs={{0,4},{1,5},{2,6},{3,7},{4,0},{5,1},{6,2},{7,3},{8,12},{9,13},{10,... | collective-permute-start | bytes 786440 | tf_op jit(solution)/shard_map/ppermute | solution.py:70
  181.8 10.4 %collective-permute-start.38 = (bf16[144,128]{1,0:T(8,128)(2,1)S(1)}, bf16[144,128]{1,0:T(8,128)(2,1)S(1)}, u32[]{:S(2)}, u32[]{:S(2)}) collective-permute-start(bf16[144,128]{1,0:T(8,128)(2,1)S(1)} %copy-done.47), channel_id=1, source_target_pairs={{0,16},{8,24},{16,32},{24,40},{32,48},{40,56},{48,0},{56,8},{64,80... | collective-permute-start | bytes 110600 | tf_op jit(solution)/shard_map/ppermute | solution.py:57
  183.2 10.1 %collective-permute-start.39 = (bf16[144,128]{1,0:T(8,128)(2,1)S(1)}, bf16[144,128]{1,0:T(8,128)(2,1)S(1)}, u32[]{:S(2)}, u32[]{:S(2)}) collective-permute-start(bf16[144,128]{1,0:T(8,128)(2,1)S(1)} %copy-done.46), channel_id=1, source_target_pairs={{0,32},{8,40},{16,48},{24,56},{32,0},{40,8},{48,16},{56,24},{64,96... | collective-permute-start | bytes 110600 | tf_op jit(solution)/shard_map/ppermute | solution.py:57
  186.4 6.8 %collective-permute-start.40 = (bf16[144,128]{1,0:T(8,128)(2,1)S(1)}, bf16[144,128]{1,0:T(8,128)(2,1)S(1)}, u32[]{:S(2)}, u32[]{:S(2)}) collective-permute-start(bf16[144,128]{1,0:T(8,128)(2,1)S(1)} %copy-done.45), channel_id=1, source_target_pairs={{0,48},{8,56},{16,0},{24,8},{32,16},{40,24},{48,32},{56,40},{64,11... | collective-permute-start | bytes 110600 | tf_op jit(solution)/shard_map/ppermute | solution.py:57
  195.9 4.0 %collective-permute-start.43 = (f32[8,128]{1,0:T(8,128)}, f32[8,128]{1,0:T(8,128)S(1)}, u32[]{:S(2)}, u32[]{:S(2)}) collective-permute-start(f32[8,128]{1,0:T(8,128)} %get-tuple-element.117.g0), channel_id=1, source_target_pairs={{0,3},{1,0},{2,1},{3,2},{4,7},{5,4},{6,5},{7,6},{8,11},{9,8},{10,9... | collective-permute-start | bytes 12296 | tf_op jit(solution)/shard_map/ppermute | solution.py:66
  197.8 5.3 %collective-permute-start.42 = (f32[8,128]{1,0:T(8,128)}, f32[8,128]{1,0:T(8,128)S(1)}, u32[]{:S(2)}, u32[]{:S(2)}) collective-permute-start(f32[8,128]{1,0:T(8,128)} %get-tuple-element.117.g0), channel_id=1, source_target_pairs={{0,2},{1,3},{2,0},{3,1},{4,6},{5,7},{6,4},{7,5},{8,10},{9,11},{10,... | collective-permute-start | bytes 12296 | tf_op jit(solution)/shard_map/ppermute | solution.py:66
  198.9 5.0 %collective-permute-start.41 = (f32[8,128]{1,0:T(8,128)}, f32[8,128]{1,0:T(8,128)S(1)}, u32[]{:S(2)}, u32[]{:S(2)}) collective-permute-start(f32[8,128]{1,0:T(8,128)} %get-tuple-element.117.g0), channel_id=1, source_target_pairs={{0,1},{1,2},{2,3},{3,0},{4,5},{5,6},{6,7},{7,4},{8,9},{9,10},{10,1... | collective-permute-start | bytes 12296 | tf_op jit(solution)/shard_map/ppermute | solution.py:66
  205.8 7.7 %collective-permute-start.44 = (f32[8,128]{1,0:T(8,128)}, f32[8,128]{1,0:T(8,128)S(1)}, u32[]{:S(2)}, u32[]{:S(2)}) collective-permute-start(f32[8,128]{1,0:T(8,128)} %shard_map.202.a_ref), channel_id=1, source_target_pairs={{0,4},{1,5},{2,6},{3,7},{4,0},{5,1},{6,2},{7,3},{8,12},{9,13},{10,... | collective-permute-start | bytes 12296 | tf_op jit(solution)/shard_map/ppermute | solution.py:70
  (45 other events, 252.9 us)

commit v3 on v2

--- a/solution.py
+++ b/solution.py
@@ -19,7 +19,7 @@
 SCALE = DH ** (-0.5)
 LOG2E = math.log2(math.e)
 KB = 256
-PAIR = 256
+PAIR = 1024
 PAD = 16
 NY, NZ, NCORE, NX = 4, 4, 2, 4
 
@@ -28,6 +28,8 @@
 BF16 = jnp.bfloat16
 F32 = jnp.float32
 
+SMALL = pltpu.CompilerParams(vmem_limit_bytes=8 * 1024 * 1024)
+
 
 def shaped(shape, dtype):
     return jax.ShapeDtypeStruct(shape, dtype)
@@ -61,8 +63,8 @@
     return lax.ppermute(value, "ctx", ctx_shift(0, 0, 1))
 
 
-def send_x(value, k):
-    perm = [(t, (t // NX) * NX + (t + k) % NX) for t in range(2 * NX)]
+def send_x(value, k, flip=0):
+    perm = [(t, ((t // NX) ^ flip) * NX + (t + k) % NX) for t in range(2 * NX)]
     return lax.ppermute(value, "tp", perm)
 
 
@@ -127,6 +129,11 @@
         out_ref[(z - k) & (NZ - 1)] = refs[k][...]
 
 
+def merge_kernel(*refs):
+    for k in range(NY):
+        refs[-1][k] = refs[k][...]
+
+
 def weights_kernel(order_ref, wk_ref, wv_ref, *out_refs):
     step = pl.program_id(0)
     for k in range(NX):
@@ -156,6 +163,7 @@
             out_specs=[pl.BlockSpec((1, 2, rows, DH), piece_map(k)) for k in range(NX)],
         ),
         out_shape=[shaped((2, 2, rows, DH), BF16)] * NX,
+        compiler_params=pltpu.CompilerParams(vmem_limit_bytes=16 * 1024 * 1024),
     )(order, w_key, w_value)
 
 
@@ -212,7 +220,7 @@
     out_refs[1][...] = total[n // 2 :]
 
 
-def project_kernel(*refs):
+def project_kernel(half, *refs):
     grads, weights, out_ref = refs[:NX], refs[NX : 2 * NX], refs[2 * NX]
     tok = grads[0].shape[0] // 2
     cols = 256
@@ -220,7 +228,7 @@
         total = None
         for g, w in zip(grads, weights):
             for i in range(2):
-                part = dot_t(g[i * tok : (i + 1) * tok], w[0, i, j * cols : (j + 1) * cols])
+                part = dot_t(g[i * tok : (i + 1) * tok], w[half, i, j * cols : (j + 1) * cols])
                 total = part if total is None else total + part
         out_ref[:, j * cols : (j + 1) * cols] = total.astype(out_ref.dtype)
 
@@ -229,11 +237,10 @@
     tok = grads[0].shape[0] // 2
     rows = weights[0].shape[2]
     return pl.pallas_call(
-        project_kernel,
-        grid=(1,),
-        in_specs=[pl.BlockSpec(g.shape, lambda i: (0, 0)) for g in grads]
-        + [pl.BlockSpec((1, 2, rows, DH), lambda i: (half, 0, 0, 0))] * NX,
-        out_specs=pl.BlockSpec((tok, rows), lambda i: (0, 0)),
+        functools.partial(project_kernel, half),
+        in_specs=[VMEM] * (2 * NX),
+        out_specs=VMEM,
+        compiler_params=pltpu.CompilerParams(vmem_limit_bytes=16 * 1024 * 1024),
         out_shape=shaped((tok, rows), BF16 if half == 1 else F32),
         cost_estimate=pl.CostEstimate(
             flops=4 * NX * tok * rows * DH, transcendentals=0, bytes_accessed=4 * NX * rows * DH
@@ -241,32 +248,38 @@
     )(*grads, *weights)
 
 
-def add_kernel(a_ref, b_ref, o_ref):
-    o_ref[...] = (a_ref[...] + b_ref[...].astype(F32)).astype(o_ref.dtype)
-
-
 def gate_sum_kernel(g0, g1, g2, g3, o_ref):
     o_ref[...] = g0[...] + g1[...] + g2[...] + g3[...]
 
 
-def gate_out_kernel(a_ref, b_ref, gain_ref, o_ref):
+def finish_kernel(gain_ref, near_ref, far_ref, home_ref, away_ref, gate_ref, out_ref):
     t = gain_ref[0:1, 0:DH]
-    o_ref[...] = (1.0 - t * t) * (a_ref[0:1] + b_ref[0:1])
-
-
-def call(kernel, outs, *args, smem=0):
+    gate_ref[...] = (1.0 - t * t) * (near_ref[0:1] + far_ref[0:1])
+    out_ref[...] = (home_ref[...] + away_ref[...].astype(F32)).astype(out_ref.dtype)
+
+
+def call(kernel, outs, *args, smem=0, params=SMALL):
     single = not isinstance(outs, (list, tuple))
     specs = [SMEM] * smem + [VMEM] * (len(args) - smem)
     return pl.pallas_call(
-        kernel, out_shape=outs, in_specs=specs, out_specs=VMEM if single else [VMEM] * len(outs)
+        kernel,
+        out_shape=outs,
+        in_specs=specs,
+        out_specs=VMEM if single else [VMEM] * len(outs),
+        compiler_params=params,
     )(*args)
 
 
-def attn_kernel(block_rows, base, pad, *refs):
+def attn_kernel(block_rows, base, pad, merged, *refs):
     ctx_ref, bounds_ref, low_ref, high_ref, gain_ref, q_ref, g_ref = refs[:7]
-    mine, others = refs[7 : 7 + NY], refs[7 + NY : 7 + 2 * NY]
-    dq_ref, own_ref, oth_ref = refs[7 + 2 * NY : 10 + 2 * NY]
-    (k_s, v_s, e_s, d_s, peak_s, kt_s, qt_s, gt_s, qr_s, gr_s, dk_s, dv_s) = refs[10 + 2 * NY :]
+    if merged:
+        mine, others = ([ref.at[k] for k in range(NY)] for ref in refs[7:9])
+        refs = refs[9:]
+    else:
+        mine, others = refs[7 : 7 + NY], refs[7 + NY : 7 + 2 * NY]
+        refs = refs[7 + 2 * NY :]
+    dq_ref, own_ref, oth_ref = refs[:3]
+    (k_s, v_s, e_s, d_s, peak_s, kt_s, qt_s, gt_s, qr_s, gr_s, dk_s, dv_s) = refs[3:]
     first, clear0, clear1, last = (bounds_ref[base + i] for i in range(4))
     c = ctx_ref[0]
     core, my_y = c & 1, lax.shift_right_logical(c, 3)
@@ -332,9 +345,15 @@
             jnp.zeros((1, PAIR), F32),
             jnp.zeros((1, PAIR), F32),
         )
-        carry = lax.fori_loop(first, clear0, functools.partial(stats, True), carry)
-        carry = lax.fori_loop(clear0, clear1, functools.partial(stats, False), carry)
-        peak, total, dsum = lax.fori_loop(clear1, last, functools.partial(stats, True), carry)
+
+        def edge(i, carry):
+            b = first + i
+            return stats(True, jnp.where(b < clear0, b, b + (clear1 - clear0)), carry)
+
+        carry = lax.fori_loop(0, (last - first) - (clear1 - clear0), edge, carry)
+        peak, total, dsum = lax.fori_loop(
+            clear0, clear1, functools.partial(stats, False), carry
+        )
         inv = 1.0 / total
         delta = dsum * inv
 
@@ -388,15 +407,16 @@
 
 def attention_grads(base, pad, max_blocks, ctx, bounds, low, high, gain, q, g, mine, others):
     tok = q.shape[0]
-    block_rows = mine[0].shape[2]
+    merged = len(mine) == 1
+    block_rows = mine[0].shape[-2]
     keys = NY * NZ * NCORE * block_rows
     pairs = GROUP * tok // PAIR
     steps = max_blocks * KB
     half = shaped((keys + pad, DH), BF16)
     return pl.pallas_call(
-        functools.partial(attn_kernel, block_rows, base, pad),
+        functools.partial(attn_kernel, block_rows, base, pad, merged),
         out_shape=(shaped(q.shape, BF16), half, half),
-        in_specs=[SMEM, SMEM] + [VMEM] * (5 + 2 * NY),
+        in_specs=[SMEM, SMEM] + [VMEM] * (5 + 2 * len(mine)),
         out_specs=(VMEM, VMEM, VMEM),
         scratch_shapes=[
             pltpu.VMEM((keys, DH), BF16),
@@ -449,6 +469,7 @@
         value_self,
         image_keys,
         image_values,
+        params=None,
     )
     kv_z = [kv] + [send_z(kv, k) for k in range(1, NZ)]
     rows_doc = after(document_id.reshape(seq // tok, tok), kv)
@@ -459,15 +480,17 @@
         + (shaped((8, DH), F32), shaped((8,), jnp.int32)),
         in_specs=[SMEM, SMEM, VMEM, VMEM],
         out_specs=(VMEM,) * 4 + (SMEM,),
+        compiler_params=SMALL,
     )(ctx, gate, rows_doc, image_block.reshape(1, tok))
+    pieces = weight_pieces(after(tp, bounds), w_key, w_value)
+    kv_z[0] = after(kv_z[0], pieces[0])
     kv_mine = call(order_kernel, shaped((NZ, 2, tok, DH), BF16), ctx, *kv_z, smem=1)
-    pieces = weight_pieces(after(tp, kv_mine), w_key, w_value)
     ikv = after(ikv, kv_mine)
     ikv_z = [ikv] + [send_z(ikv, k) for k in range(1, NZ)]
     mine = [kv_mine] + [send_y(kv_mine, k) for k in range(1, NY)]
-    others = [send_core(m) for m in mine]
     weights = [pieces[0]] + [send_x(pieces[k], k) for k in range(1, NX)]
     ikv_mine = call(order_kernel, shaped((NZ, 2, img, DH), BF16), ctx, *ikv_z, smem=1)
+    others = [send_core(after(m, ikv_mine)) for m in mine]
     imine = [ikv_mine] + [send_y(ikv_mine, k) for k in range(1, NY)]
     query = after(query_self, ikv_mine)
 
@@ -478,7 +501,9 @@
     )
     got = send_core(other)
     imine = [after(m, own) for m in imine]
-    iothers = [send_core(m) for m in imine]
+    iall = shaped((NY, NZ, 2, img, DH), BF16)
+    imine = call(merge_kernel, iall, *imine)
+    iothers = send_core(imine)
     piece = shaped((NZ * 2 * tok, DH), BF16)
     share = call(functools.partial(core_sum_kernel, 0), [piece] * NY, own, got)
     query = after(query_cross, share[0])
@@ -494,12 +519,12 @@
         gain,
         query,
         grad_cross,
-        imine,
-        iothers,
+        [imine],
+        [iothers],
     )
     igot = send_core(iother)
     piece = shaped((2 * tok, DH), BF16)
-    share[0] = after(share[0], iown, *weights[1:])
+    share[0] = after(share[0], iown)
     share = call(functools.partial(y_sum_kernel, 0), [piece] * NZ, ctx, *share, smem=1)
     iown = after(iown, share[0])
     share = [share[0]] + [send_z(share[k], k) for k in range(1, NZ)]
@@ -520,6 +545,7 @@
     ishare[0] = after(ishare[0], away)
     away = send_zh(away)
     home = project(0, both, weights)
+    ishare[0] = after(ishare[0], home)
     one = shaped((img, DH), BF16)
     gates = shaped((8, DH), F32)
     image_key_grad, image_value_grad, total = call(
@@ -528,8 +554,15 @@
     total = [total] + [send_x(total, k) for k in range(1, NX)]
     total = call(gate_sum_kernel, gates, *total)
     far = send_zh(total)
-    input_grad = call(add_kernel, shaped(home.shape, BF16), home, away)
-    gate_grad = call(gate_out_kernel, shaped((1, DH), F32), total, far, gain)
+    gate_grad, input_grad = call(
+        finish_kernel,
+        [shaped((1, DH), F32), shaped(home.shape, BF16)],
+        gain,
+        total,
+        far,
+        home,
+        away,
+    )
     return (
         query_grad,
         key_grad,

time: 219 us -> 150 us (0.68)
  Pallas kernels: 54 us -> 19.4 us
  starting transfers between devices: 94.5 us -> 72.9 us
  local copies, waits for them, and re-layouts: 15.2 us -> 4.57 us
    ppermute x12, starting transfers between devices: 50.8 us -> 30.7 us  [send_y(): return lax.ppermute(value, 'ctx', ctx_shift(k, 0, 0))]
    pallas_call x12, Pallas kernels: 20.3 us -> 4.14 us  [call(): pl.pallas_call(kernel, out_shape=outs, in_specs=specs, out_specs=VMEM if...]
    pallas_call x4, Pallas kernels: 24.6 us -> 13.3 us  [the longest x2 11.9 us: attention_grads(): pl.pallas_call(functools.partial(attn_kernel, block_rows, base, pad, merg...]
    unnamed x96 -> x20, local copies, waits for them, and re-layouts: 15.2 us -> 4.57 us
    ppermute x12, waiting for transfers between devices: 23.1 us -> 14.9 us  [send_z(): return lax.ppermute(value, 'ctx', ctx_shift(0, k, 0))]
    pallas_call x1, Pallas kernels: 7.59 us -> 1.11 us  [weight_pieces(): pl.pallas_call(weights_kernel, name='weight_pieces', grid_spec=pltpu.Pref...]
    ppermute x2, waiting for transfers between devices: 2.15 us -> 7.13 us  [send_zh(): return lax.ppermute(value, 'tp', [(t, t ^ NX) for t in range(2 * NX)])]
  transfers between devices with their start and end apart: 45 -> 42, of which waited for: 20 -> 22; matrix products, arithmetic and copies ran while one was open for 0% -> 0% of each run, Pallas kernels for 17% -> 8%
where the time goes in v3:
time: 150 us; the launch traced here: 149 us
  starting transfers between devices  72.9 us (49%)
  waiting for transfers between devices  50.6 us (34%)
  Pallas kernels  19.4 us (13%)
  local copies, waits for them, and re-layouts  4.57 us (3%)
  between operations  1.53 us (1%)
    ppermute x12, starting transfers between devices, send_y(): return lax.ppermute(value, 'ctx', ctx_shift(k, 0, 0))  30.7 us
    ppermute x12, starting transfers between devices, send_z(): return lax.ppermute(value, 'ctx', ctx_shift(0, k, 0))  21.8 us
    ppermute x12, waiting for transfers between devices, send_y(): return lax.ppermute(value, 'ctx', ctx_shift(k, 0, 0))  20.9 us
    ppermute x12, waiting for transfers between devices, send_z(): return lax.ppermute(value, 'ctx', ctx_shift(0, k, 0))  14.9 us
    ppermute x9, starting transfers between devices, send_x(): return lax.ppermute(value, 'tp', perm)  12.6 us
    pallas_call x2, Pallas kernels, attention_grads(): pl.pallas_call(functools.partial(attn_kernel, block_rows, base, pad, merg...  11.9 us
    ppermute x2, waiting for transfers between devices, send_zh(): return lax.ppermute(value, 'tp', [(t, t ^ NX) for t in range(2 * NX)])  7.13 us
    ppermute x2, starting transfers between devices, send_zh(): return lax.ppermute(value, 'tp', [(t, t ^ NX) for t in range(2 * NX)])  6.58 us
  transfers between devices with their start and end apart: 42, of which 22 were waited for; matrix products, arithmetic and copies ran while one was open for 0% of the time, Pallas kernels for 8%

profile of v3, /device:TPU:8, one launch (start us, length us, event | category | flops | bytes accessed | tf_op | source)
XLA Modules:
  0.0 149.0 jit_solution(10532388587364590943)
XLA Ops:
  0.6 1.4 shard_map.188
  2.1 1.9 %collective-permute-start = (bf16[2,128,128]{2,1,0:T(8,128)(2,1)}, bf16[2,128,128]{2,1,0:T(8,128)(2,1)S(1)}, u32[]{:S(2)}, u32[]{:S(2)}) collective-permute-start(bf16[2,128,128]{2,1,0:T(8,128)(2,1)} %get-tuple-element.79.refs_0_), channel_id=1, source_target_pairs={{0,16},{8,24},{16,32},{24,40},{32,48},{40,56},{48,0},{56,8},{64,80... | collective-permute-start | bytes 196616 | tf_op jit(solution)/shard_map/ppermute | solution.py:59
  4.0 3.3 %collective-permute-start.1 = (bf16[2,128,128]{2,1,0:T(8,128)(2,1)}, bf16[2,128,128]{2,1,0:T(8,128)(2,1)S(1)}, u32[]{:S(2)}, u32[]{:S(2)}) collective-permute-start(bf16[2,128,128]{2,1,0:T(8,128)(2,1)} %get-tuple-element.79.refs_0_), channel_id=1, source_target_pairs={{0,32},{8,40},{16,48},{24,56},{32,0},{40,8},{48,16},{56,24},{64,96... | collective-permute-start | bytes 196616 | tf_op jit(solution)/shard_map/ppermute | solution.py:59
  7.2 1.0 collective-permute-start.2
  10.3 0.9 rows.1
  11.2 1.6 %copy-done = bf16[8192,128]{1,0:T(8,128)(2,1)S(1)} copy-done((bf16[8192,128]{1,0:T(8,128)(2,1)S(1)}, bf16[8192,128]{1,0:T(8,128)(2,1)}, u32[]{:S(2)}) %copy-start) | copy-done | bytes 2097176
  12.8 1.6 %copy-done.1 = bf16[8192,128]{1,0:T(8,128)(2,1)S(1)} copy-done((bf16[8192,128]{1,0:T(8,128)(2,1)S(1)}, bf16[8192,128]{1,0:T(8,128)(2,1)}, u32[]{:S(2)}) %copy-start.1) | copy-done | bytes 2097176
  14.4 1.1 weight_pieces.1
  16.2 2.6 %collective-permute-start.7 = (bf16[4,2,128,128]{3,2,1,0:T(8,128)(2,1)S(1)}, bf16[4,2,128,128]{3,2,1,0:T(8,128)(2,1)S(1)}, u32[]{:S(2)}, u32[]{:S(2)}) collective-permute-start(bf16[4,2,128,128]{3,2,1,0:T(8,128)(2,1)S(1)} %shard_map.189.refs_7_), channel_id=1, source_target_pairs={{0,128},{8,136},{16,144},{24,152},{32,160},{40,168},{48,176},{56,1... | collective-permute-start | bytes 786440 | tf_op jit(solution)/shard_map/ppermute | solution.py:55
  18.7 1.9 %collective-permute-start.6 = (bf16[4,2,128,128]{3,2,1,0:T(8,128)(2,1)S(1)}, bf16[4,2,128,128]{3,2,1,0:T(8,128)(2,1)S(1)}, u32[]{:S(2)}, u32[]{:S(2)}) collective-permute-start(bf16[4,2,128,128]{3,2,1,0:T(8,128)(2,1)S(1)} %shard_map.189.refs_7_), channel_id=1, source_target_pairs={{0,64},{8,72},{16,80},{24,88},{32,96},{40,104},{48,112},{56,120},{... | collective-permute-start | bytes 786440 | tf_op jit(solution)/shard_map/ppermute | solution.py:55
  20.6 1.0 collective-permute-start.3
  21.7 4.7 %collective-permute-done.3.refs_1_ = bf16[2,64,128]{2,1,0:T(8,128)(2,1)S(1)} collective-permute-done((bf16[2,64,128]{2,1,0:T(8,128)(2,1)S(1)}, bf16[2,64,128]{2,1,0:T(8,128)(2,1)S(1)}, u32[]{:S(2)}, u32[]{:S(2)}) %collective-permute-start.3) | collective-permute-done | bytes 32800 | tf_op jit(solution)/shard_map/ppermute | solution.py:59
  27.1 3.3 %collective-permute-done.5.refs_3_ = bf16[2,64,128]{2,1,0:T(8,128)(2,1)S(1)} collective-permute-done((bf16[2,64,128]{2,1,0:T(8,128)(2,1)S(1)}, bf16[2,64,128]{2,1,0:T(8,128)(2,1)S(1)}, u32[]{:S(2)}, u32[]{:S(2)}) %collective-permute-start.5) | collective-permute-done | bytes 32800 | tf_op jit(solution)/shard_map/ppermute | solution.py:59
  33.1 4.8 %shard_map.191 = (bf16[128,1024]{1,0:T(8,128)(2,1)}, bf16[4096,128]{1,0:T(8,128)(2,1)S(1)}, bf16[4096,128]{1,0:T(8,128)(2,1)S(1)}) custom-call(s32[1]{0:T(128)} %bitcast.ctx_ref.refs_0_, s32[8]{0:T(128)S(1)} %get-tuple-element.73.refs_1_, s32[1,1024]{1,0:T(1,128)S(1)} %get-tuple-element.74.refs_2_, s32[1,1024]{1,0:T(1,128)S(1)} %get-tuple-element.75.refs_3_, ...), custom_call_target="tpu_custom_call" | custom-call | flops 3355443200 | bytes 4980736 | tf_op jit(solution)/shard_map/pallas_call | solution.py:416
  38.5 8.1 %collective-permute-start.15 = (bf16[4,2,64,128]{3,2,1,0:T(8,128)(2,1)S(1)}, bf16[4,2,64,128]{3,2,1,0:T(8,128)(2,1)S(1)}, u32[]{:S(2)}, u32[]{:S(2)}) collective-permute-start(bf16[4,2,64,128]{3,2,1,0:T(8,128)(2,1)S(1)} %shard_map.190.refs_0_), channel_id=1, source_target_pairs={{0,128},{8,136},{16,144},{24,152},{32,160},{40,168},{48,176},{56,1... | collective-permute-start | bytes 393224 | tf_op jit(solution)/shard_map/ppermute | solution.py:55
  46.6 2.5 %collective-permute-start.14 = (bf16[4,2,64,128]{3,2,1,0:T(8,128)(2,1)S(1)}, bf16[4,2,64,128]{3,2,1,0:T(8,128)(2,1)S(1)}, u32[]{:S(2)}, u32[]{:S(2)}) collective-permute-start(bf16[4,2,64,128]{3,2,1,0:T(8,128)(2,1)S(1)} %shard_map.190.refs_0_), channel_id=1, source_target_pairs={{0,64},{8,72},{16,80},{24,88},{32,96},{40,104},{48,112},{56,120},{... | collective-permute-start | bytes 393224 | tf_op jit(solution)/shard_map/ppermute | solution.py:55
  49.1 4.1 %collective-permute-done.15.refs_2_ = bf16[4,2,64,128]{3,2,1,0:T(8,128)(2,1)S(1)} collective-permute-done((bf16[4,2,64,128]{3,2,1,0:T(8,128)(2,1)S(1)}, bf16[4,2,64,128]{3,2,1,0:T(8,128)(2,1)S(1)}, u32[]{:S(2)}, u32[]{:S(2)}) %collective-permute-start.15) | collective-permute-done | bytes 131104 | tf_op jit(solution)/shard_map/ppermute | solution.py:55
  53.2 0.9 collective-permute-done.14.refs_1_
  54.3 1.6 %collective-permute-start.31 = (bf16[2,2,1024,128]{3,2,1,0:T(8,128)(2,1)S(1)}, bf16[2,2,1024,128]{3,2,1,0:T(8,128)(2,1)S(1)}, u32[]{:S(2)}, u32[]{:S(2)}) collective-permute-start(bf16[2,2,1024,128]{3,2,1,0:T(8,128)(2,1)S(1)} %get-tuple-element.119), channel_id=1, source_target_pairs={{0,1},{1,2},{2,3},{3,0},{4,5},{5,6},{6,7},{7,4},{8,9},{9,10},{10,1... | collective-permute-start | bytes 3145736 | tf_op jit(solution)/shard_map/ppermute | solution.py:68
  56.1 1.5 %collective-permute-start.18 = (bf16[1024,128]{1,0:T(8,128)(2,1)S(1)}, bf16[1024,128]{1,0:T(8,128)(2,1)S(1)}, u32[]{:S(2)}, u32[]{:S(2)}) collective-permute-start(bf16[1024,128]{1,0:T(8,128)(2,1)S(1)} %get-tuple-element.99), channel_id=1, source_target_pairs={{0,64},{8,72},{16,80},{24,88},{32,96},{40,104},{48,112},{56,120},{... | collective-permute-start | bytes 786440 | tf_op jit(solution)/shard_map/ppermute | solution.py:55
  57.6 2.7 %collective-permute-start.32 = (bf16[2,2,1024,128]{3,2,1,0:T(8,128)(2,1)S(1)}, bf16[2,2,1024,128]{3,2,1,0:T(8,128)(2,1)S(1)}, u32[]{:S(2)}, u32[]{:S(2)}) collective-permute-start(bf16[2,2,1024,128]{3,2,1,0:T(8,128)(2,1)S(1)} %get-tuple-element.120), channel_id=1, source_target_pairs={{0,2},{1,3},{2,0},{3,1},{4,6},{5,7},{6,4},{7,5},{8,10},{9,11},{10,... | collective-permute-start | bytes 3145736 | tf_op jit(solution)/shard_map/ppermute | solution.py:68
  60.3 1.4 collective-permute-start.33
  61.8 7.0 %shard_map.194 = (bf16[128,1024]{1,0:T(8,128)(2,1)}, bf16[2064,128]{1,0:T(8,128)(2,1)S(1)}, bf16[2064,128]{1,0:T(8,128)(2,1)S(1)}) custom-call(s32[1]{0:T(128)} %bitcast.ctx_ref.refs_0_, s32[8]{0:T(128)S(1)} %get-tuple-element.73.refs_1_, s32[1,1024]{1,0:T(1,128)S(1)} %broadcast_in_dim.7.refs_2_, s32[1,1024]{1,0:T(1,128)S(1)} %get-tuple-element.90.refs_3_, ...), custom_call_target="tpu_custom_call" | custom-call | flops 2684354560 | bytes 2883584 | tf_op jit(solution)/shard_map/pallas_call | solution.py:416
  68.8 5.6 %collective-permute-start.19 = (bf16[1024,128]{1,0:T(8,128)(2,1)S(1)}, bf16[1024,128]{1,0:T(8,128)(2,1)S(1)}, u32[]{:S(2)}, u32[]{:S(2)}) collective-permute-start(bf16[1024,128]{1,0:T(8,128)(2,1)S(1)} %get-tuple-element.100), channel_id=1, source_target_pairs={{0,128},{8,136},{16,144},{24,152},{32,160},{40,168},{48,176},{56,1... | collective-permute-start | bytes 786440 | tf_op jit(solution)/shard_map/ppermute | solution.py:55
  74.4 7.0 %collective-permute-done.19.s2_ref = bf16[1024,128]{1,0:T(8,128)(2,1)S(1)} collective-permute-done((bf16[1024,128]{1,0:T(8,128)(2,1)S(1)}, bf16[1024,128]{1,0:T(8,128)(2,1)S(1)}, u32[]{:S(2)}, u32[]{:S(2)}) %collective-permute-start.19) | collective-permute-done | bytes 262176 | tf_op jit(solution)/shard_map/ppermute | solution.py:55
  81.7 7.8 %collective-permute-done.20.s3_ref = bf16[1024,128]{1,0:T(8,128)(2,1)S(1)} collective-permute-done((bf16[1024,128]{1,0:T(8,128)(2,1)S(1)}, bf16[1024,128]{1,0:T(8,128)(2,1)S(1)}, u32[]{:S(2)}, u32[]{:S(2)}) %collective-permute-start.20) | collective-permute-done | bytes 262176 | tf_op jit(solution)/shard_map/ppermute | solution.py:55
  89.6 5.0 %collective-permute-start.22 = (bf16[256,128]{1,0:T(8,128)(2,1)S(1)}, bf16[256,128]{1,0:T(8,128)(2,1)S(1)}, u32[]{:S(2)}, u32[]{:S(2)}) collective-permute-start(bf16[256,128]{1,0:T(8,128)(2,1)S(1)} %get-tuple-element.107), channel_id=1, source_target_pairs={{0,16},{8,24},{16,32},{24,40},{32,48},{40,56},{48,0},{56,8},{64,80... | collective-permute-start | bytes 196616 | tf_op jit(solution)/shard_map/ppermute | solution.py:59
  94.7 2.2 %collective-permute-start.23 = (bf16[256,128]{1,0:T(8,128)(2,1)S(1)}, bf16[256,128]{1,0:T(8,128)(2,1)S(1)}, u32[]{:S(2)}, u32[]{:S(2)}) collective-permute-start(bf16[256,128]{1,0:T(8,128)(2,1)S(1)} %get-tuple-element.108), channel_id=1, source_target_pairs={{0,32},{8,40},{16,48},{24,56},{32,0},{40,8},{48,16},{56,24},{64,96... | collective-permute-start | bytes 196616 | tf_op jit(solution)/shard_map/ppermute | solution.py:59
  96.9 2.8 %collective-permute-start.24 = (bf16[256,128]{1,0:T(8,128)(2,1)S(1)}, bf16[256,128]{1,0:T(8,128)(2,1)S(1)}, u32[]{:S(2)}, u32[]{:S(2)}) collective-permute-start(bf16[256,128]{1,0:T(8,128)(2,1)S(1)} %get-tuple-element.109), channel_id=1, source_target_pairs={{0,48},{8,56},{16,0},{24,8},{32,16},{40,24},{48,32},{56,40},{64,11... | collective-permute-start | bytes 196616 | tf_op jit(solution)/shard_map/ppermute | solution.py:59
  99.9 2.1 %collective-permute-start.25 = (bf16[528,128]{1,0:T(8,128)(2,1)S(1)}, bf16[528,128]{1,0:T(8,128)(2,1)S(1)}, u32[]{:S(2)}, u32[]{:S(2)}) collective-permute-start(bf16[528,128]{1,0:T(8,128)(2,1)S(1)} %get-tuple-element.114), channel_id=1, source_target_pairs={{0,64},{8,72},{16,80},{24,88},{32,96},{40,104},{48,112},{56,120},{... | collective-permute-start | bytes 405512 | tf_op jit(solution)/shard_map/ppermute | solution.py:55
  102.0 2.5 %collective-permute-start.26 = (bf16[528,128]{1,0:T(8,128)(2,1)S(1)}, bf16[528,128]{1,0:T(8,128)(2,1)S(1)}, u32[]{:S(2)}, u32[]{:S(2)}) collective-permute-start(bf16[528,128]{1,0:T(8,128)(2,1)S(1)} %get-tuple-element.115), channel_id=1, source_target_pairs={{0,128},{8,136},{16,144},{24,152},{32,160},{40,168},{48,176},{56,1... | collective-permute-start | bytes 405512 | tf_op jit(solution)/shard_map/ppermute | solution.py:55
  104.5 2.5 %collective-permute-start.27 = (bf16[528,128]{1,0:T(8,128)(2,1)S(1)}, bf16[528,128]{1,0:T(8,128)(2,1)S(1)}, u32[]{:S(2)}, u32[]{:S(2)}) collective-permute-start(bf16[528,128]{1,0:T(8,128)(2,1)S(1)} %get-tuple-element.116), channel_id=1, source_target_pairs={{0,192},{8,200},{16,208},{24,216},{32,224},{40,232},{48,240},{56,2... | collective-permute-start | bytes 405512 | tf_op jit(solution)/shard_map/ppermute | solution.py:55
  109.1 0.8 collective-permute-done.27.s3_ref
  109.9 1.9 %collective-permute-start.30 = (bf16[256,128]{1,0:T(8,128)(2,1)S(1)}, bf16[256,128]{1,0:T(8,128)(2,1)S(1)}, u32[]{:S(2)}, u32[]{:S(2)}) collective-permute-start(bf16[256,128]{1,0:T(8,128)(2,1)S(1)} %get-tuple-element.123.refs_0_), channel_id=1, source_target_pairs={{0,3},{1,0},{2,1},{3,2},{4,7},{5,4},{6,5},{7,6},{8,11},{9,8},{10,9... | collective-permute-start | bytes 196616 | tf_op jit(solution)/shard_map/ppermute | solution.py:68
  111.9 1.2 collective-permute-done.28.refs_1_
  113.1 1.2 collective-permute-done.29.refs_2_
  115.4 6.2 %collective-permute-start.41 = (bf16[128,1024]{1,0:T(8,128)(2,1)S(1)}, bf16[128,1024]{1,0:T(8,128)(2,1)S(1)}, u32[]{:S(2)}, u32[]{:S(2)}) collective-permute-start(bf16[128,1024]{1,0:T(8,128)(2,1)S(1)} %shard_map.199), channel_id=1, source_target_pairs={{0,4},{1,5},{2,6},{3,7},{4,0},{5,1},{6,2},{7,3},{8,12},{9,13},{10,... | collective-permute-start | bytes 786440 | tf_op jit(solution)/shard_map/ppermute | solution.py:72
  121.6 1.3 collective-permute-start.34
  122.9 2.1 %collective-permute-start.35 = (bf16[144,128]{1,0:T(8,128)(2,1)S(1)}, bf16[144,128]{1,0:T(8,128)(2,1)S(1)}, u32[]{:S(2)}, u32[]{:S(2)}) collective-permute-start(bf16[144,128]{1,0:T(8,128)(2,1)S(1)} %get-tuple-element.126), channel_id=1, source_target_pairs={{0,32},{8,40},{16,48},{24,56},{32,0},{40,8},{48,16},{56,24},{64,96... | collective-permute-start | bytes 110600 | tf_op jit(solution)/shard_map/ppermute | solution.py:59
  125.0 1.1 collective-permute-start.36
  126.8 5.1 %collective-permute-done.34.s1_ref = bf16[144,128]{1,0:T(8,128)(2,1)S(1)} collective-permute-done((bf16[144,128]{1,0:T(8,128)(2,1)S(1)}, bf16[144,128]{1,0:T(8,128)(2,1)S(1)}, u32[]{:S(2)}, u32[]{:S(2)}) %collective-permute-start.34) | collective-permute-done | bytes 36896 | tf_op jit(solution)/shard_map/ppermute | solution.py:59
  131.9 1.2 collective-permute-done.35.s2_ref
  133.7 0.8 collective-permute-start.37
  134.5 2.7 %collective-permute-start.38 = (f32[8,128]{1,0:T(8,128)S(1)}, f32[8,128]{1,0:T(8,128)S(1)}, u32[]{:S(2)}, u32[]{:S(2)}) collective-permute-start(f32[8,128]{1,0:T(8,128)S(1)} %get-tuple-element.128.g0), channel_id=1, source_target_pairs={{0,2},{1,3},{2,0},{3,1},{4,6},{5,7},{6,4},{7,5},{8,10},{9,11},{10,... | collective-permute-start | bytes 12296 | tf_op jit(solution)/shard_map/ppermute | solution.py:68
  137.5 1.0 collective-permute-done.37.g1
  138.5 1.1 collective-permute-done.38.g2
  139.6 1.2 collective-permute-done.39.g3
  141.2 7.1 %collective-permute-done.40.far_ref = f32[8,128]{1,0:T(8,128)S(1)} collective-permute-done((f32[8,128]{1,0:T(8,128)S(1)}, f32[8,128]{1,0:T(8,128)S(1)}, u32[]{:S(2)}, u32[]{:S(2)}) %collective-permute-start.40) | collective-permute-done | bytes 4128 | tf_op jit(solution)/shard_map/ppermute | solution.py:72
  (77 shorter events, 13.0 us)
Async XLA Ops:
  2.1 13.5 %collective-permute-start = (bf16[2,128,128]{2,1,0:T(8,128)(2,1)}, bf16[2,128,128]{2,1,0:T(8,128)(2,1)S(1)}, u32[]{:S(2)}, u32[]{:S(2)}) collective-permute-start(bf16[2,128,128]{2,1,0:T(8,128)(2,1)} %get-tuple-element.79.refs_0_), channel_id=1, source_target_pairs={{0,16},{8,24},{16,32},{24,40},{32,48},{40,56},{48,0},{56,8},{64,80... | collective-permute-start | bytes 196616 | tf_op jit(solution)/shard_map/ppermute | solution.py:59
  4.0 11.6 %collective-permute-start.1 = (bf16[2,128,128]{2,1,0:T(8,128)(2,1)}, bf16[2,128,128]{2,1,0:T(8,128)(2,1)S(1)}, u32[]{:S(2)}, u32[]{:S(2)}) collective-permute-start(bf16[2,128,128]{2,1,0:T(8,128)(2,1)} %get-tuple-element.79.refs_0_), channel_id=1, source_target_pairs={{0,32},{8,40},{16,48},{24,56},{32,0},{40,8},{48,16},{56,24},{64,96... | collective-permute-start | bytes 196616 | tf_op jit(solution)/shard_map/ppermute | solution.py:59
  7.2 8.3 %collective-permute-start.2 = (bf16[2,128,128]{2,1,0:T(8,128)(2,1)}, bf16[2,128,128]{2,1,0:T(8,128)(2,1)S(1)}, u32[]{:S(2)}, u32[]{:S(2)}) collective-permute-start(bf16[2,128,128]{2,1,0:T(8,128)(2,1)} %get-tuple-element.79.refs_0_), channel_id=1, source_target_pairs={{0,48},{8,56},{16,0},{24,8},{32,16},{40,24},{48,32},{56,40},{64,11... | collective-permute-start | bytes 196616 | tf_op jit(solution)/shard_map/ppermute | solution.py:59
  11.2 1.6 %copy-start = (bf16[8192,128]{1,0:T(8,128)(2,1)S(1)}, bf16[8192,128]{1,0:T(8,128)(2,1)}, u32[]{:S(2)}) copy-start(bf16[8192,128]{1,0:T(8,128)(2,1)} %wk_ref.1) | copy-start | bytes 6291460
  14.4 6.2 %copy-start.3 = (bf16[2,64,128]{2,1,0:T(8,128)(2,1)S(1)}, bf16[2,64,128]{2,1,0:T(8,128)(2,1)}, u32[]{:S(2)}) copy-start(bf16[2,64,128]{2,1,0:T(8,128)(2,1)} %get-tuple-element.80.refs_0_) | copy-start | bytes 98308
  14.4 18.7 %copy-start.6 = (bf16[128,1024]{1,0:T(8,128)(2,1)S(1)}, bf16[128,1024]{1,0:T(8,128)(2,1)}, u32[]{:S(2)}) copy-start(bf16[128,1024]{1,0:T(8,128)(2,1)} %refs_5_) | copy-start | bytes 786436
  14.4 18.7 %copy-start.7 = (bf16[128,1024]{1,0:T(8,128)(2,1)S(1)}, bf16[128,1024]{1,0:T(8,128)(2,1)}, u32[]{:S(2)}) copy-start(bf16[128,1024]{1,0:T(8,128)(2,1)} %refs_6_.2) | copy-start | bytes 786436
  15.6 14.8 %collective-permute-start.8 = (bf16[4,2,128,128]{3,2,1,0:T(8,128)(2,1)S(1)}, bf16[4,2,128,128]{3,2,1,0:T(8,128)(2,1)S(1)}, u32[]{:S(2)}, u32[]{:S(2)}) collective-permute-start(bf16[4,2,128,128]{3,2,1,0:T(8,128)(2,1)S(1)} %shard_map.189.refs_7_), channel_id=1, source_target_pairs={{0,192},{8,200},{16,208},{24,216},{32,224},{40,232},{48,240},{56,2... | collective-permute-start | bytes 786440 | tf_op jit(solution)/shard_map/ppermute | solution.py:55
  16.2 14.8 %collective-permute-start.7 = (bf16[4,2,128,128]{3,2,1,0:T(8,128)(2,1)S(1)}, bf16[4,2,128,128]{3,2,1,0:T(8,128)(2,1)S(1)}, u32[]{:S(2)}, u32[]{:S(2)}) collective-permute-start(bf16[4,2,128,128]{3,2,1,0:T(8,128)(2,1)S(1)} %shard_map.189.refs_7_), channel_id=1, source_target_pairs={{0,128},{8,136},{16,144},{24,152},{32,160},{40,168},{48,176},{56,1... | collective-permute-start | bytes 786440 | tf_op jit(solution)/shard_map/ppermute | solution.py:55
  18.7 12.3 %collective-permute-start.6 = (bf16[4,2,128,128]{3,2,1,0:T(8,128)(2,1)S(1)}, bf16[4,2,128,128]{3,2,1,0:T(8,128)(2,1)S(1)}, u32[]{:S(2)}, u32[]{:S(2)}) collective-permute-start(bf16[4,2,128,128]{3,2,1,0:T(8,128)(2,1)S(1)} %shard_map.189.refs_7_), channel_id=1, source_target_pairs={{0,64},{8,72},{16,80},{24,88},{32,96},{40,104},{48,112},{56,120},{... | collective-permute-start | bytes 786440 | tf_op jit(solution)/shard_map/ppermute | solution.py:55
  20.6 5.8 %collective-permute-start.3 = (bf16[2,64,128]{2,1,0:T(8,128)(2,1)S(1)}, bf16[2,64,128]{2,1,0:T(8,128)(2,1)S(1)}, u32[]{:S(2)}, u32[]{:S(2)}) collective-permute-start(bf16[2,64,128]{2,1,0:T(8,128)(2,1)S(1)} %copy-done.3), channel_id=1, source_target_pairs={{0,16},{8,24},{16,32},{24,40},{32,48},{40,56},{48,0},{56,8},{64,80... | collective-permute-start | bytes 98312 | tf_op jit(solution)/shard_map/ppermute | solution.py:59
  21.7 5.4 %collective-permute-start.4 = (bf16[2,64,128]{2,1,0:T(8,128)(2,1)S(1)}, bf16[2,64,128]{2,1,0:T(8,128)(2,1)S(1)}, u32[]{:S(2)}, u32[]{:S(2)}) collective-permute-start(bf16[2,64,128]{2,1,0:T(8,128)(2,1)S(1)} %copy-done.3), channel_id=1, source_target_pairs={{0,32},{8,40},{16,48},{24,56},{32,0},{40,8},{48,16},{56,24},{64,96... | collective-permute-start | bytes 98312 | tf_op jit(solution)/shard_map/ppermute | solution.py:59
  26.4 3.9 %collective-permute-start.5 = (bf16[2,64,128]{2,1,0:T(8,128)(2,1)S(1)}, bf16[2,64,128]{2,1,0:T(8,128)(2,1)S(1)}, u32[]{:S(2)}, u32[]{:S(2)}) collective-permute-start(bf16[2,64,128]{2,1,0:T(8,128)(2,1)S(1)} %copy-done.3), channel_id=1, source_target_pairs={{0,48},{8,56},{16,0},{24,8},{32,16},{40,24},{48,32},{56,40},{64,11... | collective-permute-start | bytes 98312 | tf_op jit(solution)/shard_map/ppermute | solution.py:59
  30.3 1.6 %collective-permute-start.9 = (bf16[4,2,128,128]{3,2,1,0:T(8,128)(2,1)S(1)}, bf16[4,2,128,128]{3,2,1,0:T(8,128)(2,1)S(1)}, u32[]{:S(2)}, u32[]{:S(2)}) collective-permute-start(bf16[4,2,128,128]{3,2,1,0:T(8,128)(2,1)S(1)} %shard_map.189.refs_7_), channel_id=1, source_target_pairs={{0,8},{8,0},{16,24},{24,16},{32,40},{40,32},{48,56},{56,48},{64,72... | collective-permute-start | bytes 786440 | tf_op jit(solution)/shard_map/ppermute | solution.py:63
  30.4 1.9 %collective-permute-start.12 = (bf16[4,2,128,128]{3,2,1,0:T(8,128)(2,1)S(1)}, bf16[4,2,128,128]{3,2,1,0:T(8,128)(2,1)S(1)}, u32[]{:S(2)}, u32[]{:S(2)}) collective-permute-start(bf16[4,2,128,128]{3,2,1,0:T(8,128)(2,1)S(1)} %collective-permute-done.8.refs_10_), channel_id=1, source_target_pairs={{0,8},{8,0},{16,24},{24,16},{32,40},{40,32},{48,56},{56,48},{64,72... | collective-permute-start | bytes 786440 | tf_op jit(solution)/shard_map/ppermute | solution.py:63
  30.9 1.8 %collective-permute-start.11 = (bf16[4,2,128,128]{3,2,1,0:T(8,128)(2,1)S(1)}, bf16[4,2,128,128]{3,2,1,0:T(8,128)(2,1)S(1)}, u32[]{:S(2)}, u32[]{:S(2)}) collective-permute-start(bf16[4,2,128,128]{3,2,1,0:T(8,128)(2,1)S(1)} %collective-permute-done.7.refs_9_), channel_id=1, source_target_pairs={{0,8},{8,0},{16,24},{24,16},{32,40},{40,32},{48,56},{56,48},{64,72... | collective-permute-start | bytes 786440 | tf_op jit(solution)/shard_map/ppermute | solution.py:63
  31.1 2.0 %collective-permute-start.10 = (bf16[4,2,128,128]{3,2,1,0:T(8,128)(2,1)S(1)}, bf16[4,2,128,128]{3,2,1,0:T(8,128)(2,1)S(1)}, u32[]{:S(2)}, u32[]{:S(2)}) collective-permute-start(bf16[4,2,128,128]{3,2,1,0:T(8,128)(2,1)S(1)} %collective-permute-done.6.refs_8_), channel_id=1, source_target_pairs={{0,8},{8,0},{16,24},{24,16},{32,40},{40,32},{48,56},{56,48},{64,72... | collective-permute-start | bytes 786440 | tf_op jit(solution)/shard_map/ppermute | solution.py:63
  37.9 23.9 %copy-start.8 = (bf16[128,1024]{1,0:T(8,128)(2,1)S(1)}, bf16[128,1024]{1,0:T(8,128)(2,1)}, u32[]{:S(2)}) copy-start(bf16[128,1024]{1,0:T(8,128)(2,1)} %refs_5_.1) | copy-start | bytes 786436
  37.9 23.9 %copy-start.9 = (bf16[128,1024]{1,0:T(8,128)(2,1)S(1)}, bf16[128,1024]{1,0:T(8,128)(2,1)}, u32[]{:S(2)}) copy-start(bf16[128,1024]{1,0:T(8,128)(2,1)} %refs_6_.3) | copy-start | bytes 786436
  37.9 17.9 %collective-permute-start.13 = (bf16[4096,128]{1,0:T(8,128)(2,1)S(1)}, bf16[4096,128]{1,0:T(8,128)(2,1)S(1)}, u32[]{:S(2)}, u32[]{:S(2)}) collective-permute-start(bf16[4096,128]{1,0:T(8,128)(2,1)S(1)} %get-tuple-element.88), channel_id=1, source_target_pairs={{0,8},{8,0},{16,24},{24,16},{32,40},{40,32},{48,56},{56,48},{64,72... | collective-permute-start | bytes 3145736 | tf_op jit(solution)/shard_map/ppermute | solution.py:63
  37.9 11.2 %collective-permute-start.16 = (bf16[4,2,64,128]{3,2,1,0:T(8,128)(2,1)S(1)}, bf16[4,2,64,128]{3,2,1,0:T(8,128)(2,1)S(1)}, u32[]{:S(2)}, u32[]{:S(2)}) collective-permute-start(bf16[4,2,64,128]{3,2,1,0:T(8,128)(2,1)S(1)} %shard_map.190.refs_0_), channel_id=1, source_target_pairs={{0,192},{8,200},{16,208},{24,216},{32,224},{40,232},{48,240},{56,2... | collective-permute-start | bytes 393224 | tf_op jit(solution)/shard_map/ppermute | solution.py:55
  38.5 14.8 %collective-permute-start.15 = (bf16[4,2,64,128]{3,2,1,0:T(8,128)(2,1)S(1)}, bf16[4,2,64,128]{3,2,1,0:T(8,128)(2,1)S(1)}, u32[]{:S(2)}, u32[]{:S(2)}) collective-permute-start(bf16[4,2,64,128]{3,2,1,0:T(8,128)(2,1)S(1)} %shard_map.190.refs_0_), channel_id=1, source_target_pairs={{0,128},{8,136},{16,144},{24,152},{32,160},{40,168},{48,176},{56,1... | collective-permute-start | bytes 393224 | tf_op jit(solution)/shard_map/ppermute | solution.py:55
  46.6 7.5 %collective-permute-start.14 = (bf16[4,2,64,128]{3,2,1,0:T(8,128)(2,1)S(1)}, bf16[4,2,64,128]{3,2,1,0:T(8,128)(2,1)S(1)}, u32[]{:S(2)}, u32[]{:S(2)}) collective-permute-start(bf16[4,2,64,128]{3,2,1,0:T(8,128)(2,1)S(1)} %shard_map.190.refs_0_), channel_id=1, source_target_pairs={{0,64},{8,72},{16,80},{24,88},{32,96},{40,104},{48,112},{56,120},{... | collective-permute-start | bytes 393224 | tf_op jit(solution)/shard_map/ppermute | solution.py:55
  54.2 7.6 %collective-permute-start.17 = (bf16[4,4,2,64,128]{4,3,2,1,0:T(8,128)(2,1)S(1)}, bf16[4,4,2,64,128]{4,3,2,1,0:T(8,128)(2,1)S(1)}, u32[]{:S(2)}, u32[]{:S(2)}) collective-permute-start(bf16[4,4,2,64,128]{4,3,2,1,0:T(8,128)(2,1)S(1)} %shard_map.193.refs_7_), channel_id=1, source_target_pairs={{0,8},{8,0},{16,24},{24,16},{32,40},{40,32},{48,56},{56,48},{64,72... | collective-permute-start | bytes 1572872 | tf_op jit(solution)/shard_map/ppermute | solution.py:63
  54.3 40.4 %collective-permute-start.31 = (bf16[2,2,1024,128]{3,2,1,0:T(8,128)(2,1)S(1)}, bf16[2,2,1024,128]{3,2,1,0:T(8,128)(2,1)S(1)}, u32[]{:S(2)}, u32[]{:S(2)}) collective-permute-start(bf16[2,2,1024,128]{3,2,1,0:T(8,128)(2,1)S(1)} %get-tuple-element.119), channel_id=1, source_target_pairs={{0,1},{1,2},{2,3},{3,0},{4,5},{5,6},{6,7},{7,4},{8,9},{9,10},{10,1... | collective-permute-start | bytes 3145736 | tf_op jit(solution)/shard_map/ppermute | solution.py:68
  56.1 12.8 %collective-permute-start.18 = (bf16[1024,128]{1,0:T(8,128)(2,1)S(1)}, bf16[1024,128]{1,0:T(8,128)(2,1)S(1)}, u32[]{:S(2)}, u32[]{:S(2)}) collective-permute-start(bf16[1024,128]{1,0:T(8,128)(2,1)S(1)} %get-tuple-element.99), channel_id=1, source_target_pairs={{0,64},{8,72},{16,80},{24,88},{32,96},{40,104},{48,112},{56,120},{... | collective-permute-start | bytes 786440 | tf_op jit(solution)/shard_map/ppermute | solution.py:55
  57.6 54.3 %collective-permute-start.32 = (bf16[2,2,1024,128]{3,2,1,0:T(8,128)(2,1)S(1)}, bf16[2,2,1024,128]{3,2,1,0:T(8,128)(2,1)S(1)}, u32[]{:S(2)}, u32[]{:S(2)}) collective-permute-start(bf16[2,2,1024,128]{3,2,1,0:T(8,128)(2,1)S(1)} %get-tuple-element.120), channel_id=1, source_target_pairs={{0,2},{1,3},{2,0},{3,1},{4,6},{5,7},{6,4},{7,5},{8,10},{9,11},{10,... | collective-permute-start | bytes 3145736 | tf_op jit(solution)/shard_map/ppermute | solution.py:68
  60.3 51.5 %collective-permute-start.33 = (bf16[2,2,1024,128]{3,2,1,0:T(8,128)(2,1)S(1)}, bf16[2,2,1024,128]{3,2,1,0:T(8,128)(2,1)S(1)}, u32[]{:S(2)}, u32[]{:S(2)}) collective-permute-start(bf16[2,2,1024,128]{3,2,1,0:T(8,128)(2,1)S(1)} %get-tuple-element.121), channel_id=1, source_target_pairs={{0,3},{1,0},{2,1},{3,2},{4,7},{5,4},{6,5},{7,6},{8,11},{9,8},{10,9... | collective-permute-start | bytes 3145736 | tf_op jit(solution)/shard_map/ppermute | solution.py:68
  68.8 28.1 %collective-permute-start.21 = (bf16[2064,128]{1,0:T(8,128)(2,1)S(1)}, bf16[2064,128]{1,0:T(8,128)(2,1)S(1)}, u32[]{:S(2)}, u32[]{:S(2)}) collective-permute-start(bf16[2064,128]{1,0:T(8,128)(2,1)S(1)} %get-tuple-element.104), channel_id=1, source_target_pairs={{0,8},{8,0},{16,24},{24,16},{32,40},{40,32},{48,56},{56,48},{64,72... | collective-permute-start | bytes 1585160 | tf_op jit(solution)/shard_map/ppermute | solution.py:63
  68.8 12.5 %collective-permute-start.19 = (bf16[1024,128]{1,0:T(8,128)(2,1)S(1)}, bf16[1024,128]{1,0:T(8,128)(2,1)S(1)}, u32[]{:S(2)}, u32[]{:S(2)}) collective-permute-start(bf16[1024,128]{1,0:T(8,128)(2,1)S(1)} %get-tuple-element.100), channel_id=1, source_target_pairs={{0,128},{8,136},{16,144},{24,152},{32,160},{40,168},{48,176},{56,1... | collective-permute-start | bytes 786440 | tf_op jit(solution)/shard_map/ppermute | solution.py:55
  81.4 8.1 %collective-permute-start.20 = (bf16[1024,128]{1,0:T(8,128)(2,1)S(1)}, bf16[1024,128]{1,0:T(8,128)(2,1)S(1)}, u32[]{:S(2)}, u32[]{:S(2)}) collective-permute-start(bf16[1024,128]{1,0:T(8,128)(2,1)S(1)} %get-tuple-element.101), channel_id=1, source_target_pairs={{0,192},{8,200},{16,208},{24,216},{32,224},{40,232},{48,240},{56,2... | collective-permute-start | bytes 786440 | tf_op jit(solution)/shard_map/ppermute | solution.py:55
  89.6 10.2 %collective-permute-start.22 = (bf16[256,128]{1,0:T(8,128)(2,1)S(1)}, bf16[256,128]{1,0:T(8,128)(2,1)S(1)}, u32[]{:S(2)}, u32[]{:S(2)}) collective-permute-start(bf16[256,128]{1,0:T(8,128)(2,1)S(1)} %get-tuple-element.107), channel_id=1, source_target_pairs={{0,16},{8,24},{16,32},{24,40},{32,48},{40,56},{48,0},{56,8},{64,80... | collective-permute-start | bytes 196616 | tf_op jit(solution)/shard_map/ppermute | solution.py:59
  94.7 7.3 %collective-permute-start.23 = (bf16[256,128]{1,0:T(8,128)(2,1)S(1)}, bf16[256,128]{1,0:T(8,128)(2,1)S(1)}, u32[]{:S(2)}, u32[]{:S(2)}) collective-permute-start(bf16[256,128]{1,0:T(8,128)(2,1)S(1)} %get-tuple-element.108), channel_id=1, source_target_pairs={{0,32},{8,40},{16,48},{24,56},{32,0},{40,8},{48,16},{56,24},{64,96... | collective-permute-start | bytes 196616 | tf_op jit(solution)/shard_map/ppermute | solution.py:59
  96.9 7.6 %collective-permute-start.24 = (bf16[256,128]{1,0:T(8,128)(2,1)S(1)}, bf16[256,128]{1,0:T(8,128)(2,1)S(1)}, u32[]{:S(2)}, u32[]{:S(2)}) collective-permute-start(bf16[256,128]{1,0:T(8,128)(2,1)S(1)} %get-tuple-element.109), channel_id=1, source_target_pairs={{0,48},{8,56},{16,0},{24,8},{32,16},{40,24},{48,32},{56,40},{64,11... | collective-permute-start | bytes 196616 | tf_op jit(solution)/shard_map/ppermute | solution.py:59
  99.9 7.8 %collective-permute-start.25 = (bf16[528,128]{1,0:T(8,128)(2,1)S(1)}, bf16[528,128]{1,0:T(8,128)(2,1)S(1)}, u32[]{:S(2)}, u32[]{:S(2)}) collective-permute-start(bf16[528,128]{1,0:T(8,128)(2,1)S(1)} %get-tuple-element.114), channel_id=1, source_target_pairs={{0,64},{8,72},{16,80},{24,88},{32,96},{40,104},{48,112},{56,120},{... | collective-permute-start | bytes 405512 | tf_op jit(solution)/shard_map/ppermute | solution.py:55
  102.0 6.6 %collective-permute-start.26 = (bf16[528,128]{1,0:T(8,128)(2,1)S(1)}, bf16[528,128]{1,0:T(8,128)(2,1)S(1)}, u32[]{:S(2)}, u32[]{:S(2)}) collective-permute-start(bf16[528,128]{1,0:T(8,128)(2,1)S(1)} %get-tuple-element.115), channel_id=1, source_target_pairs={{0,128},{8,136},{16,144},{24,152},{32,160},{40,168},{48,176},{56,1... | collective-permute-start | bytes 405512 | tf_op jit(solution)/shard_map/ppermute | solution.py:55
  104.5 5.5 %collective-permute-start.27 = (bf16[528,128]{1,0:T(8,128)(2,1)S(1)}, bf16[528,128]{1,0:T(8,128)(2,1)S(1)}, u32[]{:S(2)}, u32[]{:S(2)}) collective-permute-start(bf16[528,128]{1,0:T(8,128)(2,1)S(1)} %get-tuple-element.116), channel_id=1, source_target_pairs={{0,192},{8,200},{16,208},{24,216},{32,224},{40,232},{48,240},{56,2... | collective-permute-start | bytes 405512 | tf_op jit(solution)/shard_map/ppermute | solution.py:55
  107.6 5.5 %collective-permute-start.28 = (bf16[256,128]{1,0:T(8,128)(2,1)S(1)}, bf16[256,128]{1,0:T(8,128)(2,1)S(1)}, u32[]{:S(2)}, u32[]{:S(2)}) collective-permute-start(bf16[256,128]{1,0:T(8,128)(2,1)S(1)} %get-tuple-element.123.refs_0_), channel_id=1, source_target_pairs={{0,1},{1,2},{2,3},{3,0},{4,5},{5,6},{6,7},{7,4},{8,9},{9,10},{10,1... | collective-permute-start | bytes 196616 | tf_op jit(solution)/shard_map/ppermute | solution.py:68
  108.5 5.8 %collective-permute-start.29 = (bf16[256,128]{1,0:T(8,128)(2,1)S(1)}, bf16[256,128]{1,0:T(8,128)(2,1)S(1)}, u32[]{:S(2)}, u32[]{:S(2)}) collective-permute-start(bf16[256,128]{1,0:T(8,128)(2,1)S(1)} %get-tuple-element.123.refs_0_), channel_id=1, source_target_pairs={{0,2},{1,3},{2,0},{3,1},{4,6},{5,7},{6,4},{7,5},{8,10},{9,11},{10,... | collective-permute-start | bytes 196616 | tf_op jit(solution)/shard_map/ppermute | solution.py:68
  109.9 4.8 %collective-permute-start.30 = (bf16[256,128]{1,0:T(8,128)(2,1)S(1)}, bf16[256,128]{1,0:T(8,128)(2,1)S(1)}, u32[]{:S(2)}, u32[]{:S(2)}) collective-permute-start(bf16[256,128]{1,0:T(8,128)(2,1)S(1)} %get-tuple-element.123.refs_0_), channel_id=1, source_target_pairs={{0,3},{1,0},{2,1},{3,2},{4,7},{5,4},{6,5},{7,6},{8,11},{9,8},{10,9... | collective-permute-start | bytes 196616 | tf_op jit(solution)/shard_map/ppermute | solution.py:68
  115.4 32.9 %collective-permute-start.41 = (bf16[128,1024]{1,0:T(8,128)(2,1)S(1)}, bf16[128,1024]{1,0:T(8,128)(2,1)S(1)}, u32[]{:S(2)}, u32[]{:S(2)}) collective-permute-start(bf16[128,1024]{1,0:T(8,128)(2,1)S(1)} %shard_map.199), channel_id=1, source_target_pairs={{0,4},{1,5},{2,6},{3,7},{4,0},{5,1},{6,2},{7,3},{8,12},{9,13},{10,... | collective-permute-start | bytes 786440 | tf_op jit(solution)/shard_map/ppermute | solution.py:72
  121.6 10.3 %collective-permute-start.34 = (bf16[144,128]{1,0:T(8,128)(2,1)S(1)}, bf16[144,128]{1,0:T(8,128)(2,1)S(1)}, u32[]{:S(2)}, u32[]{:S(2)}) collective-permute-start(bf16[144,128]{1,0:T(8,128)(2,1)S(1)} %get-tuple-element.125), channel_id=1, source_target_pairs={{0,16},{8,24},{16,32},{24,40},{32,48},{40,56},{48,0},{56,8},{64,80... | collective-permute-start | bytes 110600 | tf_op jit(solution)/shard_map/ppermute | solution.py:59
  122.9 10.1 %collective-permute-start.35 = (bf16[144,128]{1,0:T(8,128)(2,1)S(1)}, bf16[144,128]{1,0:T(8,128)(2,1)S(1)}, u32[]{:S(2)}, u32[]{:S(2)}) collective-permute-start(bf16[144,128]{1,0:T(8,128)(2,1)S(1)} %get-tuple-element.126), channel_id=1, source_target_pairs={{0,32},{8,40},{16,48},{24,56},{32,0},{40,8},{48,16},{56,24},{64,96... | collective-permute-start | bytes 110600 | tf_op jit(solution)/shard_map/ppermute | solution.py:59
  125.0 8.0 %collective-permute-start.36 = (bf16[144,128]{1,0:T(8,128)(2,1)S(1)}, bf16[144,128]{1,0:T(8,128)(2,1)S(1)}, u32[]{:S(2)}, u32[]{:S(2)}) collective-permute-start(bf16[144,128]{1,0:T(8,128)(2,1)S(1)} %get-tuple-element.127), channel_id=1, source_target_pairs={{0,48},{8,56},{16,0},{24,8},{32,16},{40,24},{48,32},{56,40},{64,11... | collective-permute-start | bytes 110600 | tf_op jit(solution)/shard_map/ppermute | solution.py:59
  133.7 4.8 %collective-permute-start.37 = (f32[8,128]{1,0:T(8,128)S(1)}, f32[8,128]{1,0:T(8,128)S(1)}, u32[]{:S(2)}, u32[]{:S(2)}) collective-permute-start(f32[8,128]{1,0:T(8,128)S(1)} %get-tuple-element.128.g0), channel_id=1, source_target_pairs={{0,1},{1,2},{2,3},{3,0},{4,5},{5,6},{6,7},{7,4},{8,9},{9,10},{10,1... | collective-permute-start | bytes 12296 | tf_op jit(solution)/shard_map/ppermute | solution.py:68
  134.5 5.1 %collective-permute-start.38 = (f32[8,128]{1,0:T(8,128)S(1)}, f32[8,128]{1,0:T(8,128)S(1)}, u32[]{:S(2)}, u32[]{:S(2)}) collective-permute-start(f32[8,128]{1,0:T(8,128)S(1)} %get-tuple-element.128.g0), channel_id=1, source_target_pairs={{0,2},{1,3},{2,0},{3,1},{4,6},{5,7},{6,4},{7,5},{8,10},{9,11},{10,... | collective-permute-start | bytes 12296 | tf_op jit(solution)/shard_map/ppermute | solution.py:68
  137.1 3.6 %collective-permute-start.39 = (f32[8,128]{1,0:T(8,128)S(1)}, f32[8,128]{1,0:T(8,128)S(1)}, u32[]{:S(2)}, u32[]{:S(2)}) collective-permute-start(f32[8,128]{1,0:T(8,128)S(1)} %get-tuple-element.128.g0), channel_id=1, source_target_pairs={{0,3},{1,0},{2,1},{3,2},{4,7},{5,4},{6,5},{7,6},{8,11},{9,8},{10,9... | collective-permute-start | bytes 12296 | tf_op jit(solution)/shard_map/ppermute | solution.py:68
  140.8 7.5 %collective-permute-start.40 = (f32[8,128]{1,0:T(8,128)S(1)}, f32[8,128]{1,0:T(8,128)S(1)}, u32[]{:S(2)}, u32[]{:S(2)}) collective-permute-start(f32[8,128]{1,0:T(8,128)S(1)} %shard_map.202.near_ref), channel_id=1, source_target_pairs={{0,4},{1,5},{2,6},{3,7},{4,0},{5,1},{6,2},{7,3},{8,12},{9,13},{10,... | collective-permute-start | bytes 12296 | tf_op jit(solution)/shard_map/ppermute | solution.py:72
  (4 other events, 4.1 us)

commit v4 on v3

--- a/solution.py
+++ b/solution.py
@@ -16,6 +16,7 @@
 DOC_MAX = 2176
 
 NEG_FILL = -1e30
+MASKED = -2e30
 SCALE = DH ** (-0.5)
 LOG2E = math.log2(math.e)
 KB = 256
@@ -134,37 +135,48 @@
         refs[-1][k] = refs[k][...]
 
 
-def weights_kernel(order_ref, wk_ref, wv_ref, *out_refs):
-    step = pl.program_id(0)
-    for k in range(NX):
-
-        @pl.when(lax.shift_right_logical(step, 1) == k)
-        def _():
-            out_refs[k][0, 0] = wk_ref[...]
-            out_refs[k][0, 1] = wv_ref[...]
+def weights_kernel(tp_ref, wk_ref, wv_ref, *refs):
+    out_refs, held, came, left = refs[:NX], refs[NX], refs[NX + 1], refs[NX + 2]
+    rows = held.shape[1]
+    zh = lax.shift_right_logical(tp_ref[0], 2)
+    x = tp_ref[0] & (NX - 1)
+    ins, outs = [], []
+    for k in (2, 1, 3, 0):
+        for half in range(2):
+            at = ((zh ^ half) * NX + ((x + k) & (NX - 1))) * rows
+            at = pl.multiple_of(at, rows)
+            for i, ref in enumerate((wk_ref, wv_ref)):
+                n = len(ins)
+                ins.append(
+                    pltpu.make_async_copy(ref.at[pl.ds(at, rows), :], held.at[n], came.at[n])
+                )
+                outs.append(
+                    pltpu.make_async_copy(held.at[n], out_refs[k].at[half, i], left.at[n])
+                )
+    for copy in ins:
+        copy.start()
+    for came_in, copy in zip(ins, outs):
+        came_in.wait()
+        copy.start()
+    for copy in outs:
+        copy.wait()
 
 
 def weight_pieces(tp, w_key, w_value):
     rows = w_key.shape[0] // (2 * NX)
-    zh, x = tp // NX, tp % NX
-    step = jnp.arange(2 * NX, dtype=jnp.int32)
-    order = ((zh + (step & 1)) & 1) * NX + ((x + (step >> 1)) & (NX - 1))
-
-    def piece_map(k):
-        return lambda g, order: (jnp.clip(g - 2 * k, 0, 1), 0, 0, 0)
-
+    whole = pl.BlockSpec(memory_space=pl.ANY)
     return pl.pallas_call(
         weights_kernel,
         name="weight_pieces",
-        grid_spec=pltpu.PrefetchScalarGridSpec(
-            num_scalar_prefetch=1,
-            grid=(2 * NX,),
-            in_specs=[pl.BlockSpec((rows, DH), lambda g, order: (order[g], 0))] * 2,
-            out_specs=[pl.BlockSpec((1, 2, rows, DH), piece_map(k)) for k in range(NX)],
-        ),
+        in_specs=[SMEM, whole, whole],
+        out_specs=[whole] * NX,
         out_shape=[shaped((2, 2, rows, DH), BF16)] * NX,
-        compiler_params=pltpu.CompilerParams(vmem_limit_bytes=16 * 1024 * 1024),
-    )(order, w_key, w_value)
+        scratch_shapes=[
+            pltpu.VMEM((4 * NX, rows, DH), BF16),
+            pltpu.SemaphoreType.DMA((4 * NX,)),
+            pltpu.SemaphoreType.DMA((4 * NX,)),
+        ],
+    )(tp, w_key, w_value)
 
 
 def split_gate(total):
@@ -207,55 +219,73 @@
             out_refs[k][n : n + pad] = tail
 
 
-def z_sum_kernel(pad, s0_ref, s1_ref, s2_ref, s3_ref, *out_refs):
+def z_sum_kernel(gate_ref, s0_ref, s1_ref, s2_ref, s3_ref, k_ref, v_ref, both_ref):
     ins = (s0_ref, s1_ref, s2_ref, s3_ref)
-    n = ins[0].shape[0] - pad
+    n = ins[0].shape[0]
+    total = sum(r[...].astype(F32) for r in ins).astype(BF16)
+    both_ref[0:n] = total
+    both_ref[n : n + PAD] = gate_ref[...]
+    k_ref[...] = total[: n // 2]
+    v_ref[...] = total[n // 2 :]
+
+
+def image_z_sum_kernel(s0_ref, s1_ref, s2_ref, s3_ref, k_ref, v_ref, gate_ref):
+    ins = (s0_ref, s1_ref, s2_ref, s3_ref)
+    n = ins[0].shape[0] - PAD
     total = sum(r[0:n].astype(F32) for r in ins).astype(BF16)
-    if pad:
-        gate = sum(join_gate(r[n : n + pad]) for r in ins)
-        out_refs[2][...] = jnp.broadcast_to(gate, out_refs[2].shape)
-    else:
-        out_refs[2][...] = total
-    out_refs[0][...] = total[: n // 2]
-    out_refs[1][...] = total[n // 2 :]
+    gate_ref[...] = split_gate(sum(join_gate(r[n : n + PAD]) for r in ins))
+    k_ref[...] = total[: n // 2]
+    v_ref[...] = total[n // 2 :]
 
 
 def project_kernel(half, *refs):
     grads, weights, out_ref = refs[:NX], refs[NX : 2 * NX], refs[2 * NX]
-    tok = grads[0].shape[0] // 2
+    tok = (grads[0].shape[0] - PAD) // 2
     cols = 256
-    for j in range(out_ref.shape[1] // cols):
+    rows = weights[0].shape[2]
+    if half:
+        gate = split_gate(sum(join_gate(g[2 * tok : 2 * tok + PAD]) for g in grads))
+        at = out_ref.shape[0] - PAD
+        out_ref[at : at + PAD] = gate
+    for j in range(rows // cols):
         total = None
         for g, w in zip(grads, weights):
             for i in range(2):
                 part = dot_t(g[i * tok : (i + 1) * tok], w[half, i, j * cols : (j + 1) * cols])
                 total = part if total is None else total + part
-        out_ref[:, j * cols : (j + 1) * cols] = total.astype(out_ref.dtype)
+        if half:
+            for i in range(cols // DH):
+                at = (j * (cols // DH) + i) * tok
+                out_ref[at : at + tok] = total[:, i * DH : (i + 1) * DH].astype(BF16)
+        else:
+            out_ref[:, j * cols : (j + 1) * cols] = total
 
 
 def project(half, grads, weights):
-    tok = grads[0].shape[0] // 2
+    tok = (grads[0].shape[0] - PAD) // 2
     rows = weights[0].shape[2]
     return pl.pallas_call(
         functools.partial(project_kernel, half),
         in_specs=[VMEM] * (2 * NX),
         out_specs=VMEM,
         compiler_params=pltpu.CompilerParams(vmem_limit_bytes=16 * 1024 * 1024),
-        out_shape=shaped((tok, rows), BF16 if half == 1 else F32),
+        out_shape=shaped((rows // DH * tok + PAD, DH), BF16) if half else shaped((tok, rows), F32),
         cost_estimate=pl.CostEstimate(
             flops=4 * NX * tok * rows * DH, transcendentals=0, bytes_accessed=4 * NX * rows * DH
         ),
     )(*grads, *weights)
 
 
-def gate_sum_kernel(g0, g1, g2, g3, o_ref):
-    o_ref[...] = g0[...] + g1[...] + g2[...] + g3[...]
-
-
-def finish_kernel(gain_ref, near_ref, far_ref, home_ref, away_ref, gate_ref, out_ref):
+def finish_kernel(gain_ref, near_ref, far_ref, home_ref, gate_ref, out_ref):
+    tok, cols = home_ref.shape
+    at = near_ref.shape[0] - PAD
     t = gain_ref[0:1, 0:DH]
-    gate_ref[...] = (1.0 - t * t) * (near_ref[0:1] + far_ref[0:1])
-    out_ref[...] = (home_ref[...] + away_ref[...].astype(F32)).astype(out_ref.dtype)
+    total = join_gate(near_ref[at : at + PAD]) + join_gate(far_ref[at : at + PAD])
+    gate_ref[...] = (1.0 - t * t) * total
+    for i in range(cols // DH):
+        part = far_ref[i * tok : (i + 1) * tok].astype(F32)
+        total = home_ref[:, i * DH : (i + 1) * DH] + part
+        out_ref[:, i * DH : (i + 1) * DH] = total.astype(out_ref.dtype)
 
 
 def call(kernel, outs, *args, smem=0, params=SMALL):
@@ -279,7 +309,7 @@
         mine, others = refs[7 : 7 + NY], refs[7 + NY : 7 + 2 * NY]
         refs = refs[7 + 2 * NY :]
     dq_ref, own_ref, oth_ref = refs[:3]
-    (k_s, v_s, e_s, d_s, peak_s, kt_s, qt_s, gt_s, qr_s, gr_s, dk_s, dv_s) = refs[3:]
+    (k_s, v_s, e_s, d_s, peak_s, kt_s, qt_s, gt_s, qr_s, gr_s, dk_s, dv_s, dq_s) = refs[3:]
     first, clear0, clear1, last = (bounds_ref[base + i] for i in range(4))
     c = ctx_ref[0]
     core, my_y = c & 1, lax.shift_right_logical(c, 3)
@@ -322,17 +352,14 @@
             peak, total, dsum = carry
             start = pl.multiple_of(b * KB, KB)
             where = pl.multiple_of((b - first) * KB, KB)
-            s = dot(k_s[pl.ds(start, KB), :], qt) * (SCALE * LOG2E)
+            s = dot(k_s[pl.ds(start, KB), :], qt)
             dp = dot(v_s[pl.ds(start, KB), :], gt)
             if masked:
-                pos = start + lax.broadcasted_iota(jnp.int32, (KB, PAIR), 0)
-                allowed = (pos >= low) & (pos <= high)
-                s = jnp.where(allowed, s, NEG_FILL)
+                pos = lax.broadcasted_iota(jnp.int32, (KB, PAIR), 0)
+                s = jnp.where((pos >= low - start) & (pos <= high - start), s, MASKED)
             new = jnp.maximum(peak, jnp.max(s, axis=0, keepdims=True))
-            e = jnp.exp2(s - new)
-            if masked:
-                e = jnp.where(allowed, e, 0.0)
-            factor = jnp.exp2(peak - new)
+            e = jnp.exp2((s - new) * (SCALE * LOG2E))
+            factor = jnp.exp2((peak - new) * (SCALE * LOG2E))
             e_s[pl.ds(where, KB), :] = e
             d_s[pl.ds(where, KB), :] = dp
             peak_s[b - first] = new
@@ -357,16 +384,19 @@
         inv = 1.0 / total
         delta = dsum * inv
 
-        def grads(b, dqt):
+        def grads(b, carry):
             where = pl.multiple_of((b - first) * KB, KB)
-            norm = jnp.exp2(peak_s[b - first] - peak) * inv
+            norm = jnp.exp2((peak_s[b - first] - peak) * (SCALE * LOG2E)) * inv
             prob = e_s[pl.ds(where, KB), :] * norm
             ds = (prob * (d_s[pl.ds(where, KB), :] - delta)).astype(BF16)
             dv_s[pl.ds(where, KB), :] += dot(prob.astype(BF16), gr_s[p])
             dk_s[pl.ds(where, KB), :] += dot(ds, qr_s[p])
-            return dqt + dot(kt_s[b - first], ds)
-
-        dqt = lax.fori_loop(first, last, grads, jnp.zeros((DH, PAIR), F32))
+            dq_s[...] += dot(kt_s[b - first], ds)
+            return carry
+
+        dq_s[...] = jnp.zeros((DH, PAIR), F32)
+        lax.fori_loop(first, last, grads, 0)
+        dqt = dq_s[...]
         for i in range(PAIR // tok):
             at = pl.multiple_of(p * (PAIR // tok) * DH + i * DH, DH)
             part = dqt[:, i * tok : (i + 1) * tok] * (gain * SCALE)
@@ -376,19 +406,20 @@
     dots = lax.fori_loop(0, GROUP * tok // PAIR, one_pair, jnp.zeros((1, PAIR), F32))
 
     n = NZ * 2 * block_rows
-    own_ref[...] = jnp.zeros(own_ref.shape, own_ref.dtype)
-    oth_ref[...] = jnp.zeros(oth_ref.shape, oth_ref.dtype)
     per_step = KB // block_rows
 
-    def flush(b, carry):
+    def flush(live, b, carry):
         for i in range(per_step):
             block = b * per_step + i
             k = (lax.shift_right_logical(block, 3) - my_y) & (NY - 1)
             z = lax.shift_right_logical(block, 1) & (NZ - 1)
             at = pl.multiple_of(k * n + z * 2 * block_rows, block_rows)
-            where = pl.multiple_of((b - first) * KB + i * block_rows, block_rows)
-            dk = (dk_s[pl.ds(where, block_rows), :] * (gain * SCALE)).astype(BF16)
-            dv = (dv_s[pl.ds(where, block_rows), :] * gain).astype(BF16)
+            if live:
+                where = pl.multiple_of((b - first) * KB + i * block_rows, block_rows)
+                dk = (dk_s[pl.ds(where, block_rows), :] * (gain * SCALE)).astype(BF16)
+                dv = (dv_s[pl.ds(where, block_rows), :] * gain).astype(BF16)
+            else:
+                dk = dv = jnp.zeros((block_rows, DH), BF16)
             for same, ref in ((True, own_ref), (False, oth_ref)):
 
                 @pl.when((core == (i & 1)) if same else (core != (i & 1)))
@@ -398,7 +429,9 @@
 
         return carry
 
-    lax.fori_loop(first, last, flush, 0)
+    lax.fori_loop(0, first, functools.partial(flush, False), 0)
+    lax.fori_loop(first, last, functools.partial(flush, True), 0)
+    lax.fori_loop(last, k_s.shape[0] // KB, functools.partial(flush, False), 0)
     if pad:
         gate = jnp.broadcast_to(jnp.sum(dots, axis=1, keepdims=True), (1, DH))
         own_ref[NY * n : NY * n + pad] = split_gate(gate)
@@ -431,6 +464,7 @@
             pltpu.VMEM((pairs, PAIR, DH), BF16),
             pltpu.VMEM((steps, DH), F32),
             pltpu.VMEM((steps, DH), F32),
+            pltpu.VMEM((DH, PAIR), F32),
         ],
         cost_estimate=pl.CostEstimate(
             flops=10 * GROUP * tok * steps * DH,
@@ -460,7 +494,7 @@
     img = image_keys.shape[0]
     seq = document_id.shape[0]
     ctx = lax.axis_index("ctx").reshape(1)
-    tp = lax.axis_index("tp")
+    tp = lax.axis_index("tp").reshape(1)
 
     kv, ikv = call(
         stack_kernel,
@@ -472,7 +506,17 @@
         params=None,
     )
     kv_z = [kv] + [send_z(kv, k) for k in range(1, NZ)]
-    rows_doc = after(document_id.reshape(seq // tok, tok), kv)
+    pieces = weight_pieces(after(tp, kv), w_key, w_value)
+    kv_z[0] = after(kv_z[0], pieces[0])
+    kv_mine = call(order_kernel, shaped((NZ, 2, tok, DH), BF16), ctx, *kv_z, smem=1)
+    ikv = after(ikv, kv_mine)
+    ikv_z = [ikv] + [send_z(ikv, k) for k in range(1, NZ)]
+    mine = [kv_mine] + [send_y(kv_mine, k) for k in range(1, NY)]
+    weights = [pieces[0]] + [send_x(pieces[k], k) for k in range(1, NX)]
+    ikv_mine = call(order_kernel, shaped((NZ, 2, img, DH), BF16), ctx, *ikv_z, smem=1)
+    others = [send_core(after(m, ikv_mine)) for m in mine]
+    imine = [ikv_mine] + [send_y(ikv_mine, k) for k in range(1, NY)]
+    rows_doc = after(document_id.reshape(seq // tok, tok), ikv_mine)
     low, high, limit, gain, bounds = pl.pallas_call(
         rows_kernel,
         name="rows",
@@ -482,16 +526,6 @@
         out_specs=(VMEM,) * 4 + (SMEM,),
         compiler_params=SMALL,
     )(ctx, gate, rows_doc, image_block.reshape(1, tok))
-    pieces = weight_pieces(after(tp, bounds), w_key, w_value)
-    kv_z[0] = after(kv_z[0], pieces[0])
-    kv_mine = call(order_kernel, shaped((NZ, 2, tok, DH), BF16), ctx, *kv_z, smem=1)
-    ikv = after(ikv, kv_mine)
-    ikv_z = [ikv] + [send_z(ikv, k) for k in range(1, NZ)]
-    mine = [kv_mine] + [send_y(kv_mine, k) for k in range(1, NY)]
-    weights = [pieces[0]] + [send_x(pieces[k], k) for k in range(1, NX)]
-    ikv_mine = call(order_kernel, shaped((NZ, 2, img, DH), BF16), ctx, *ikv_z, smem=1)
-    others = [send_core(after(m, ikv_mine)) for m in mine]
-    imine = [ikv_mine] + [send_y(ikv_mine, k) for k in range(1, NY)]
     query = after(query_self, ikv_mine)
 
     ones = jnp.ones((8, DH), F32)
@@ -523,45 +557,30 @@
         [iothers],
     )
     igot = send_core(iother)
-    piece = shaped((2 * tok, DH), BF16)
-    share[0] = after(share[0], iown)
-    share = call(functools.partial(y_sum_kernel, 0), [piece] * NZ, ctx, *share, smem=1)
-    iown = after(iown, share[0])
-    share = [share[0]] + [send_z(share[k], k) for k in range(1, NZ)]
     ipiece = shaped((NZ * 2 * img + PAD, DH), BF16)
     ishare = call(functools.partial(core_sum_kernel, PAD), [ipiece] * NY, iown, igot)
     share[0] = after(share[0], ishare[0])
     ishare = [ishare[0]] + [send_y(ishare[k], k) for k in range(1, NY)]
-    one = shaped((tok, DH), BF16)
-    key_grad, value_grad, both = call(functools.partial(z_sum_kernel, 0), [one, one, piece], *share)
-    ishare[0] = after(ishare[0], both)
-    both = [both] + [send_x(both, k) for k in range(1, NX)]
+    piece = shaped((2 * tok, DH), BF16)
+    share = call(functools.partial(y_sum_kernel, 0), [piece] * NZ, ctx, *share, smem=1)
+    ishare[0] = after(ishare[0], share[0])
+    share = [share[0]] + [send_z(share[k], k) for k in range(1, NZ)]
     ipiece = shaped((2 * img + PAD, DH), BF16)
     ishare = call(functools.partial(y_sum_kernel, PAD), [ipiece] * NZ, ctx, *ishare, smem=1)
-    both[0] = after(both[0], ishare[0])
     ishare = [ishare[0]] + [send_z(ishare[k], k) for k in range(1, NZ)]
-    away = project(1, both, weights)
-    both[0] = after(both[0], away)
-    ishare[0] = after(ishare[0], away)
-    away = send_zh(away)
+    one = shaped((img, DH), BF16)
+    gates = shaped((PAD, DH), BF16)
+    image_key_grad, image_value_grad, gates = call(image_z_sum_kernel, [one, one, gates], *ishare)
+    one = shaped((tok, DH), BF16)
+    both = shaped((2 * tok + PAD, DH), BF16)
+    key_grad, value_grad, both = call(z_sum_kernel, [one, one, both], gates, *share)
+    both = [both] + [send_x(both, k) for k in range(1, NX)]
+    near = project(1, both, weights)
+    both[0] = after(both[0], near)
+    far = send_zh(near)
     home = project(0, both, weights)
-    ishare[0] = after(ishare[0], home)
-    one = shaped((img, DH), BF16)
-    gates = shaped((8, DH), F32)
-    image_key_grad, image_value_grad, total = call(
-        functools.partial(z_sum_kernel, PAD), [one, one, gates], *ishare
-    )
-    total = [total] + [send_x(total, k) for k in range(1, NX)]
-    total = call(gate_sum_kernel, gates, *total)
-    far = send_zh(total)
     gate_grad, input_grad = call(
-        finish_kernel,
-        [shaped((1, DH), F32), shaped(home.shape, BF16)],
-        gain,
-        total,
-        far,
-        home,
-        away,
+        finish_kernel, [shaped((1, DH), F32), shaped(home.shape, BF16)], gain, near, far, home
     )
     return (
         query_grad,

time: 150 us -> 143 us (0.953)
  the two profiles are of different devices: /device:TPU:8 before, /device:TPU:26 now
where the time goes in v4:
time: 143 us
  waiting for transfers between devices  58.1 us (41%)
  starting transfers between devices  52.4 us (37%)
  Pallas kernels  30.4 us (21%)
  between operations  1.52 us (1%)
    ppermute x12, waiting for transfers between devices, send_y(): return lax.ppermute(value, 'ctx', ctx_shift(k, 0, 0))  33.9 us
    ppermute x12, starting transfers between devices, send_z(): return lax.ppermute(value, 'ctx', ctx_shift(0, k, 0))  26.5 us
    pallas_call x2, Pallas kernels, attention_grads(): pl.pallas_call(functools.partial(attn_kernel, block_rows, base, pad, merg...  20 us
    ppermute x12, waiting for transfers between devices, send_z(): return lax.ppermute(value, 'ctx', ctx_shift(0, k, 0))  10.2 us
    ppermute x12, starting transfers between devices, send_y(): return lax.ppermute(value, 'ctx', ctx_shift(k, 0, 0))  10.1 us
    ppermute x6, starting transfers between devices, send_x(): return lax.ppermute(value, 'tp', perm)  8.54 us
    ppermute x1, waiting for transfers between devices, send_zh(): return lax.ppermute(value, 'tp', [(t, t ^ NX) for t in range(2 * NX)])  8.32 us
    ppermute x1, starting transfers between devices, send_zh(): return lax.ppermute(value, 'tp', [(t, t ^ NX) for t in range(2 * NX)])  5.92 us
  transfers between devices with their start and end apart: 38, of which 21 were waited for; matrix products, arithmetic and copies ran while one was open for 0% of the time, Pallas kernels for 5%

profile of v4, /device:TPU:26, one launch (start us, length us, event | category | flops | bytes accessed | tf_op | source)
XLA Modules:
  0.0 142.6 jit_solution(18445559528323744917)
XLA Ops:
  0.6 1.4 shard_map.188
  2.1 1.9 %collective-permute-start = (bf16[2,128,128]{2,1,0:T(8,128)(2,1)}, bf16[2,128,128]{2,1,0:T(8,128)(2,1)S(1)}, u32[]{:S(2)}, u32[]{:S(2)}) collective-permute-start(bf16[2,128,128]{2,1,0:T(8,128)(2,1)} %get-tuple-element.70.refs_0_), channel_id=1, source_target_pairs={{0,16},{8,24},{16,32},{24,40},{32,48},{40,56},{48,0},{56,8},{64,80... | collective-permute-start | bytes 196616 | tf_op jit(solution)/shard_map/ppermute | solution.py:60
  4.0 3.3 %collective-permute-start.1 = (bf16[2,128,128]{2,1,0:T(8,128)(2,1)}, bf16[2,128,128]{2,1,0:T(8,128)(2,1)S(1)}, u32[]{:S(2)}, u32[]{:S(2)}) collective-permute-start(bf16[2,128,128]{2,1,0:T(8,128)(2,1)} %get-tuple-element.70.refs_0_), channel_id=1, source_target_pairs={{0,32},{8,40},{16,48},{24,56},{32,0},{40,8},{48,16},{56,24},{64,96... | collective-permute-start | bytes 196616 | tf_op jit(solution)/shard_map/ppermute | solution.py:60
  7.2 1.0 collective-permute-start.2
  8.3 3.9 %weight_pieces.1 = (bf16[2,2,1024,128]{3,2,1,0:T(8,128)(2,1)}, bf16[2,2,1024,128]{3,2,1,0:T(8,128)(2,1)}, bf16[2,2,1024,128]{3,2,1,0:T(8,128)(2,1)}, bf16[2,2,1024,128]{3,2,1,0:T(8,128)(2,1)}) custom-call(s32[1]{0:T(128)} %bitcast.2.tp_ref, bf16[8192,128]{1,0:T(8,128)(2,1)} %wk_ref.1, bf16[8192,128]{1,0:T(8,128)(2,1)} %wv_ref.1), custom_call_target="tpu_custom_call" | custom-call | tf_op jit(solution)/shard_map/weight_pieces/pallas_call | solution.py:168
  12.3 0.8 collective-permute-start.8
  13.1 0.9 collective-permute-start.7
  14.1 2.2 %collective-permute-start.6 = (bf16[4,2,128,128]{3,2,1,0:T(8,128)(2,1)S(1)}, bf16[4,2,128,128]{3,2,1,0:T(8,128)(2,1)S(1)}, u32[]{:S(2)}, u32[]{:S(2)}) collective-permute-start(bf16[4,2,128,128]{3,2,1,0:T(8,128)(2,1)S(1)} %shard_map.189.refs_7_), channel_id=1, source_target_pairs={{0,64},{8,72},{16,80},{24,88},{32,96},{40,104},{48,112},{56,120},{... | collective-permute-start | bytes 786440 | tf_op jit(solution)/shard_map/ppermute | solution.py:56
  16.3 1.5 %collective-permute-start.3 = (bf16[2,64,128]{2,1,0:T(8,128)(2,1)S(1)}, bf16[2,64,128]{2,1,0:T(8,128)(2,1)S(1)}, u32[]{:S(2)}, u32[]{:S(2)}) collective-permute-start(bf16[2,64,128]{2,1,0:T(8,128)(2,1)S(1)} %copy-done.2), channel_id=1, source_target_pairs={{0,16},{8,24},{16,32},{24,40},{32,48},{40,56},{48,0},{56,8},{64,80... | collective-permute-start | bytes 98312 | tf_op jit(solution)/shard_map/ppermute | solution.py:60
  17.7 1.7 %collective-permute-start.4 = (bf16[2,64,128]{2,1,0:T(8,128)(2,1)S(1)}, bf16[2,64,128]{2,1,0:T(8,128)(2,1)S(1)}, u32[]{:S(2)}, u32[]{:S(2)}) collective-permute-start(bf16[2,64,128]{2,1,0:T(8,128)(2,1)S(1)} %copy-done.2), channel_id=1, source_target_pairs={{0,32},{8,40},{16,48},{24,56},{32,0},{40,8},{48,16},{56,24},{64,96... | collective-permute-start | bytes 98312 | tf_op jit(solution)/shard_map/ppermute | solution.py:60
  19.5 2.9 %collective-permute-done.3.refs_1_ = bf16[2,64,128]{2,1,0:T(8,128)(2,1)S(1)} collective-permute-done((bf16[2,64,128]{2,1,0:T(8,128)(2,1)S(1)}, bf16[2,64,128]{2,1,0:T(8,128)(2,1)S(1)}, u32[]{:S(2)}, u32[]{:S(2)}) %collective-permute-start.3) | collective-permute-done | bytes 32800 | tf_op jit(solution)/shard_map/ppermute | solution.py:60
  22.4 0.5 collective-permute-start.5
  23.2 3.1 %collective-permute-done.5.refs_3_ = bf16[2,64,128]{2,1,0:T(8,128)(2,1)S(1)} collective-permute-done((bf16[2,64,128]{2,1,0:T(8,128)(2,1)S(1)}, bf16[2,64,128]{2,1,0:T(8,128)(2,1)S(1)}, u32[]{:S(2)}, u32[]{:S(2)}) %collective-permute-start.5) | collective-permute-done | bytes 32800 | tf_op jit(solution)/shard_map/ppermute | solution.py:60
  28.2 0.9 rows.1
  29.2 11.5 %shard_map.191 = (bf16[128,1024]{1,0:T(8,128)(2,1)}, bf16[4096,128]{1,0:T(8,128)(2,1)S(1)}, bf16[4096,128]{1,0:T(8,128)(2,1)S(1)}) custom-call(s32[1]{0:T(128)} %bitcast.ctx_ref.refs_0_, s32[8]{0:T(128)S(1)} %get-tuple-element.73.refs_1_, s32[1,1024]{1,0:T(1,128)S(1)} %get-tuple-element.74.refs_2_, s32[1,1024]{1,0:T(1,128)S(1)} %get-tuple-element.75.refs_3_, ...), custom_call_target="tpu_custom_call" | custom-call | flops 3355443200 | bytes 4980736 | tf_op jit(solution)/shard_map/pallas_call | solution.py:449
  41.2 3.2 %collective-permute-start.14 = (bf16[4,2,64,128]{3,2,1,0:T(8,128)(2,1)S(1)}, bf16[4,2,64,128]{3,2,1,0:T(8,128)(2,1)S(1)}, u32[]{:S(2)}, u32[]{:S(2)}) collective-permute-start(bf16[4,2,64,128]{3,2,1,0:T(8,128)(2,1)S(1)} %shard_map.190.refs_0_), channel_id=1, source_target_pairs={{0,64},{8,72},{16,80},{24,88},{32,96},{40,104},{48,112},{56,120},{... | collective-permute-start | bytes 393224 | tf_op jit(solution)/shard_map/ppermute | solution.py:56
  44.4 6.4 %collective-permute-done.16.refs_3_ = bf16[4,2,64,128]{3,2,1,0:T(8,128)(2,1)S(1)} collective-permute-done((bf16[4,2,64,128]{3,2,1,0:T(8,128)(2,1)S(1)}, bf16[4,2,64,128]{3,2,1,0:T(8,128)(2,1)S(1)}, u32[]{:S(2)}, u32[]{:S(2)}) %collective-permute-start.16) | collective-permute-done | bytes 131104 | tf_op jit(solution)/shard_map/ppermute | solution.py:56
  50.9 0.6 collective-permute-done.14.refs_1_
  51.9 1.6 %collective-permute-done.17.refs_8_ = bf16[4,4,2,64,128]{4,3,2,1,0:T(8,128)(2,1)S(1)} collective-permute-done((bf16[4,4,2,64,128]{4,3,2,1,0:T(8,128)(2,1)S(1)}, bf16[4,4,2,64,128]{4,3,2,1,0:T(8,128)(2,1)S(1)}, u32[]{:S(2)}, u32[]{:S(2)}) %collective-permute-start.17) | collective-permute-done | bytes 524320 | tf_op jit(solution)/shard_map/ppermute | solution.py:64
  53.6 8.6 %shard_map.194 = (bf16[128,1024]{1,0:T(8,128)(2,1)}, bf16[2064,128]{1,0:T(8,128)(2,1)S(1)}, bf16[2064,128]{1,0:T(8,128)(2,1)S(1)}) custom-call(s32[1]{0:T(128)} %bitcast.ctx_ref.refs_0_, s32[8]{0:T(128)S(1)} %get-tuple-element.73.refs_1_, s32[1,1024]{1,0:T(1,128)S(1)} %broadcast_in_dim.7.refs_2_, s32[1,1024]{1,0:T(1,128)S(1)} %get-tuple-element.82.refs_3_, ...), custom_call_target="tpu_custom_call" | custom-call | flops 2684354560 | bytes 2883584 | tf_op jit(solution)/shard_map/pallas_call | solution.py:449
  62.3 1.5 %collective-permute-start.34 = (bf16[2,2,1024,128]{3,2,1,0:T(8,128)(2,1)S(1)}, bf16[2,2,1024,128]{3,2,1,0:T(8,128)(2,1)S(1)}, u32[]{:S(2)}, u32[]{:S(2)}) collective-permute-start(bf16[2,2,1024,128]{3,2,1,0:T(8,128)(2,1)S(1)} %copy-done.11), channel_id=1, source_target_pairs={{0,1},{1,2},{2,3},{3,0},{4,5},{5,6},{6,7},{7,4},{8,9},{9,10},{10,1... | collective-permute-start | bytes 3145736 | tf_op jit(solution)/shard_map/ppermute | solution.py:69
  63.8 1.1 collective-permute-start.35
  64.9 2.1 %collective-permute-start.36 = (bf16[2,2,1024,128]{3,2,1,0:T(8,128)(2,1)S(1)}, bf16[2,2,1024,128]{3,2,1,0:T(8,128)(2,1)S(1)}, u32[]{:S(2)}, u32[]{:S(2)}) collective-permute-start(bf16[2,2,1024,128]{3,2,1,0:T(8,128)(2,1)S(1)} %copy-done.9), channel_id=1, source_target_pairs={{0,3},{1,0},{2,1},{3,2},{4,7},{5,4},{6,5},{7,6},{8,11},{9,8},{10,9... | collective-permute-start | bytes 3145736 | tf_op jit(solution)/shard_map/ppermute | solution.py:69
  67.0 7.7 %collective-permute-done.19.s1_ref = bf16[1024,128]{1,0:T(8,128)(2,1)S(1)} collective-permute-done((bf16[1024,128]{1,0:T(8,128)(2,1)S(1)}, bf16[1024,128]{1,0:T(8,128)(2,1)S(1)}, u32[]{:S(2)}, u32[]{:S(2)}) %collective-permute-start.19) | collective-permute-done | bytes 262176 | tf_op jit(solution)/shard_map/ppermute | solution.py:56
  74.8 2.3 %collective-permute-start.21 = (bf16[1024,128]{1,0:T(8,128)(2,1)S(1)}, bf16[1024,128]{1,0:T(8,128)(2,1)S(1)}, u32[]{:S(2)}, u32[]{:S(2)}) collective-permute-start(bf16[1024,128]{1,0:T(8,128)(2,1)S(1)} %get-tuple-element.98), channel_id=1, source_target_pairs={{0,192},{8,200},{16,208},{24,216},{32,224},{40,232},{48,240},{56,2... | collective-permute-start | bytes 786440 | tf_op jit(solution)/shard_map/ppermute | solution.py:56
  77.3 8.2 %collective-permute-done.20.s2_ref = bf16[1024,128]{1,0:T(8,128)(2,1)S(1)} collective-permute-done((bf16[1024,128]{1,0:T(8,128)(2,1)S(1)}, bf16[1024,128]{1,0:T(8,128)(2,1)S(1)}, u32[]{:S(2)}, u32[]{:S(2)}) %collective-permute-start.20) | collective-permute-done | bytes 262176 | tf_op jit(solution)/shard_map/ppermute | solution.py:56
  85.5 3.0 %collective-permute-done.21.s3_ref = bf16[1024,128]{1,0:T(8,128)(2,1)S(1)} collective-permute-done((bf16[1024,128]{1,0:T(8,128)(2,1)S(1)}, bf16[1024,128]{1,0:T(8,128)(2,1)S(1)}, u32[]{:S(2)}, u32[]{:S(2)}) %collective-permute-start.21) | collective-permute-done | bytes 262176 | tf_op jit(solution)/shard_map/ppermute | solution.py:56
  88.5 0.6 collective-permute-start.23
  89.1 2.7 %collective-permute-done.22.s1_ref = bf16[528,128]{1,0:T(8,128)(2,1)S(1)} collective-permute-done((bf16[528,128]{1,0:T(8,128)(2,1)S(1)}, bf16[528,128]{1,0:T(8,128)(2,1)S(1)}, u32[]{:S(2)}, u32[]{:S(2)}) %collective-permute-start.22) | collective-permute-done | bytes 135200 | tf_op jit(solution)/shard_map/ppermute | solution.py:56
  91.9 4.6 %collective-permute-done.23.s2_ref = bf16[528,128]{1,0:T(8,128)(2,1)S(1)} collective-permute-done((bf16[528,128]{1,0:T(8,128)(2,1)S(1)}, bf16[528,128]{1,0:T(8,128)(2,1)S(1)}, u32[]{:S(2)}, u32[]{:S(2)}) %collective-permute-start.23) | collective-permute-done | bytes 135200 | tf_op jit(solution)/shard_map/ppermute | solution.py:56
  96.5 5.7 %collective-permute-start.28 = (bf16[256,128]{1,0:T(8,128)(2,1)S(1)}, bf16[256,128]{1,0:T(8,128)(2,1)S(1)}, u32[]{:S(2)}, u32[]{:S(2)}) collective-permute-start(bf16[256,128]{1,0:T(8,128)(2,1)S(1)} %get-tuple-element.109), channel_id=1, source_target_pairs={{0,16},{8,24},{16,32},{24,40},{32,48},{40,56},{48,0},{56,8},{64,80... | collective-permute-start | bytes 196616 | tf_op jit(solution)/shard_map/ppermute | solution.py:60
  102.3 1.9 %collective-permute-start.25 = (bf16[144,128]{1,0:T(8,128)(2,1)S(1)}, bf16[144,128]{1,0:T(8,128)(2,1)S(1)}, u32[]{:S(2)}, u32[]{:S(2)}) collective-permute-start(bf16[144,128]{1,0:T(8,128)(2,1)S(1)} %get-tuple-element.105), channel_id=1, source_target_pairs={{0,16},{8,24},{16,32},{24,40},{32,48},{40,56},{48,0},{56,8},{64,80... | collective-permute-start | bytes 110600 | tf_op jit(solution)/shard_map/ppermute | solution.py:60
  104.1 4.4 %collective-permute-start.26 = (bf16[144,128]{1,0:T(8,128)(2,1)S(1)}, bf16[144,128]{1,0:T(8,128)(2,1)S(1)}, u32[]{:S(2)}, u32[]{:S(2)}) collective-permute-start(bf16[144,128]{1,0:T(8,128)(2,1)S(1)} %get-tuple-element.106), channel_id=1, source_target_pairs={{0,32},{8,40},{16,48},{24,56},{32,0},{40,8},{48,16},{56,24},{64,96... | collective-permute-start | bytes 110600 | tf_op jit(solution)/shard_map/ppermute | solution.py:60
  108.9 1.5 %collective-permute-done.26.s2_ref = bf16[144,128]{1,0:T(8,128)(2,1)S(1)} collective-permute-done((bf16[144,128]{1,0:T(8,128)(2,1)S(1)}, bf16[144,128]{1,0:T(8,128)(2,1)S(1)}, u32[]{:S(2)}, u32[]{:S(2)}) %collective-permute-start.26) | collective-permute-done | bytes 36896 | tf_op jit(solution)/shard_map/ppermute | solution.py:60
  110.5 2.9 %collective-permute-start.29 = (bf16[256,128]{1,0:T(8,128)(2,1)S(1)}, bf16[256,128]{1,0:T(8,128)(2,1)S(1)}, u32[]{:S(2)}, u32[]{:S(2)}) collective-permute-start(bf16[256,128]{1,0:T(8,128)(2,1)S(1)} %get-tuple-element.110), channel_id=1, source_target_pairs={{0,32},{8,40},{16,48},{24,56},{32,0},{40,8},{48,16},{56,24},{64,96... | collective-permute-start | bytes 196616 | tf_op jit(solution)/shard_map/ppermute | solution.py:60
  113.4 1.3 collective-permute-start.30
  114.7 0.6 shard_map.198
  115.3 1.0 collective-permute-done.29.s2_ref
  116.3 1.3 collective-permute-done.30.s3_ref
  117.6 0.7 shard_map.199
  118.3 3.5 %collective-permute-start.32 = (bf16[272,128]{1,0:T(8,128)(2,1)S(1)}, bf16[272,128]{1,0:T(8,128)(2,1)S(1)}, u32[]{:S(2)}, u32[]{:S(2)}) collective-permute-start(bf16[272,128]{1,0:T(8,128)(2,1)S(1)} %get-tuple-element.118.refs_0_), channel_id=1, source_target_pairs={{0,2},{1,3},{2,0},{3,1},{4,6},{5,7},{6,4},{7,5},{8,10},{9,11},{10,... | collective-permute-start | bytes 208904 | tf_op jit(solution)/shard_map/ppermute | solution.py:69
  122.6 1.5 %collective-permute-done.32.refs_2_ = bf16[272,128]{1,0:T(8,128)(2,1)S(1)} collective-permute-done((bf16[272,128]{1,0:T(8,128)(2,1)S(1)}, bf16[272,128]{1,0:T(8,128)(2,1)S(1)}, u32[]{:S(2)}, u32[]{:S(2)}) %collective-permute-start.32) | collective-permute-done | bytes 69664 | tf_op jit(solution)/shard_map/ppermute | solution.py:69
  124.1 2.0 %collective-permute-done.33.refs_3_ = bf16[272,128]{1,0:T(8,128)(2,1)S(1)} collective-permute-done((bf16[272,128]{1,0:T(8,128)(2,1)S(1)}, bf16[272,128]{1,0:T(8,128)(2,1)S(1)}, u32[]{:S(2)}, u32[]{:S(2)}) %collective-permute-start.33) | collective-permute-done | bytes 69664 | tf_op jit(solution)/shard_map/ppermute | solution.py:69
  126.1 0.7 shard_map.200.near_ref
  126.8 5.9 %collective-permute-start.37 = (bf16[1040,128]{1,0:T(8,128)(2,1)S(1)}, bf16[1040,128]{1,0:T(8,128)(2,1)S(1)}, u32[]{:S(2)}, u32[]{:S(2)}) collective-permute-start(bf16[1040,128]{1,0:T(8,128)(2,1)S(1)} %shard_map.200.near_ref), channel_id=1, source_target_pairs={{0,4},{1,5},{2,6},{3,7},{4,0},{5,1},{6,2},{7,3},{8,12},{9,13},{10,... | collective-permute-start | bytes 798728 | tf_op jit(solution)/shard_map/ppermute | solution.py:73
  132.7 0.7 shard_map.201.home_ref
  133.5 8.3 %collective-permute-done.37.far_ref = bf16[1040,128]{1,0:T(8,128)(2,1)S(1)} collective-permute-done((bf16[1040,128]{1,0:T(8,128)(2,1)S(1)}, bf16[1040,128]{1,0:T(8,128)(2,1)S(1)}, u32[]{:S(2)}, u32[]{:S(2)}) %collective-permute-start.37) | collective-permute-done | bytes 266272 | tf_op jit(solution)/shard_map/ppermute | solution.py:73
  141.8 0.8 shard_map.202
  (71 shorter events, 4.3 us)
Async XLA Ops:
  2.1 10.2 %collective-permute-start = (bf16[2,128,128]{2,1,0:T(8,128)(2,1)}, bf16[2,128,128]{2,1,0:T(8,128)(2,1)S(1)}, u32[]{:S(2)}, u32[]{:S(2)}) collective-permute-start(bf16[2,128,128]{2,1,0:T(8,128)(2,1)} %get-tuple-element.70.refs_0_), channel_id=1, source_target_pairs={{0,16},{8,24},{16,32},{24,40},{32,48},{40,56},{48,0},{56,8},{64,80... | collective-permute-start | bytes 196616 | tf_op jit(solution)/shard_map/ppermute | solution.py:60
  4.0 8.3 %collective-permute-start.1 = (bf16[2,128,128]{2,1,0:T(8,128)(2,1)}, bf16[2,128,128]{2,1,0:T(8,128)(2,1)S(1)}, u32[]{:S(2)}, u32[]{:S(2)}) collective-permute-start(bf16[2,128,128]{2,1,0:T(8,128)(2,1)} %get-tuple-element.70.refs_0_), channel_id=1, source_target_pairs={{0,32},{8,40},{16,48},{24,56},{32,0},{40,8},{48,16},{56,24},{64,96... | collective-permute-start | bytes 196616 | tf_op jit(solution)/shard_map/ppermute | solution.py:60
  7.2 5.1 %collective-permute-start.2 = (bf16[2,128,128]{2,1,0:T(8,128)(2,1)}, bf16[2,128,128]{2,1,0:T(8,128)(2,1)S(1)}, u32[]{:S(2)}, u32[]{:S(2)}) collective-permute-start(bf16[2,128,128]{2,1,0:T(8,128)(2,1)} %get-tuple-element.70.refs_0_), channel_id=1, source_target_pairs={{0,48},{8,56},{16,0},{24,8},{32,16},{40,24},{48,32},{56,40},{64,11... | collective-permute-start | bytes 196616 | tf_op jit(solution)/shard_map/ppermute | solution.py:60
  8.3 19.9 %copy-start.3 = (s32[4096]{0:T(1024)S(1)}, s32[4096]{0:T(1024)}, u32[]{:S(2)}) copy-start(s32[4096]{0:T(1024)} %param.17) | copy-start | bytes 49156
  8.3 19.9 %copy-start.4 = (s32[128]{0:T(128)S(1)}, s32[128]{0:T(128)}, u32[]{:S(2)}) copy-start(s32[128]{0:T(128)} %param.22) | copy-start | bytes 1540
  8.3 20.9 %copy-start.5 = (bf16[128,1024]{1,0:T(8,128)(2,1)S(1)}, bf16[128,1024]{1,0:T(8,128)(2,1)}, u32[]{:S(2)}) copy-start(bf16[128,1024]{1,0:T(8,128)(2,1)} %refs_5_) | copy-start | bytes 786436
  8.3 20.9 %copy-start.6 = (bf16[128,1024]{1,0:T(8,128)(2,1)S(1)}, bf16[128,1024]{1,0:T(8,128)(2,1)}, u32[]{:S(2)}) copy-start(bf16[128,1024]{1,0:T(8,128)(2,1)} %refs_6_.2) | copy-start | bytes 786436
  12.3 14.6 %collective-permute-start.8 = (bf16[4,2,128,128]{3,2,1,0:T(8,128)(2,1)S(1)}, bf16[4,2,128,128]{3,2,1,0:T(8,128)(2,1)S(1)}, u32[]{:S(2)}, u32[]{:S(2)}) collective-permute-start(bf16[4,2,128,128]{3,2,1,0:T(8,128)(2,1)S(1)} %shard_map.189.refs_7_), channel_id=1, source_target_pairs={{0,192},{8,200},{16,208},{24,216},{32,224},{40,232},{48,240},{56,2... | collective-permute-start | bytes 786440 | tf_op jit(solution)/shard_map/ppermute | solution.py:56
  13.1 13.8 %collective-permute-start.7 = (bf16[4,2,128,128]{3,2,1,0:T(8,128)(2,1)S(1)}, bf16[4,2,128,128]{3,2,1,0:T(8,128)(2,1)S(1)}, u32[]{:S(2)}, u32[]{:S(2)}) collective-permute-start(bf16[4,2,128,128]{3,2,1,0:T(8,128)(2,1)S(1)} %shard_map.189.refs_7_), channel_id=1, source_target_pairs={{0,128},{8,136},{16,144},{24,152},{32,160},{40,168},{48,176},{56,1... | collective-permute-start | bytes 786440 | tf_op jit(solution)/shard_map/ppermute | solution.py:56
  14.1 13.4 %collective-permute-start.6 = (bf16[4,2,128,128]{3,2,1,0:T(8,128)(2,1)S(1)}, bf16[4,2,128,128]{3,2,1,0:T(8,128)(2,1)S(1)}, u32[]{:S(2)}, u32[]{:S(2)}) collective-permute-start(bf16[4,2,128,128]{3,2,1,0:T(8,128)(2,1)S(1)} %shard_map.189.refs_7_), channel_id=1, source_target_pairs={{0,64},{8,72},{16,80},{24,88},{32,96},{40,104},{48,112},{56,120},{... | collective-permute-start | bytes 786440 | tf_op jit(solution)/shard_map/ppermute | solution.py:56
  16.3 6.1 %collective-permute-start.3 = (bf16[2,64,128]{2,1,0:T(8,128)(2,1)S(1)}, bf16[2,64,128]{2,1,0:T(8,128)(2,1)S(1)}, u32[]{:S(2)}, u32[]{:S(2)}) collective-permute-start(bf16[2,64,128]{2,1,0:T(8,128)(2,1)S(1)} %copy-done.2), channel_id=1, source_target_pairs={{0,16},{8,24},{16,32},{24,40},{32,48},{40,56},{48,0},{56,8},{64,80... | collective-permute-start | bytes 98312 | tf_op jit(solution)/shard_map/ppermute | solution.py:60
  17.7 5.4 %collective-permute-start.4 = (bf16[2,64,128]{2,1,0:T(8,128)(2,1)S(1)}, bf16[2,64,128]{2,1,0:T(8,128)(2,1)S(1)}, u32[]{:S(2)}, u32[]{:S(2)}) collective-permute-start(bf16[2,64,128]{2,1,0:T(8,128)(2,1)S(1)} %copy-done.2), channel_id=1, source_target_pairs={{0,32},{8,40},{16,48},{24,56},{32,0},{40,8},{48,16},{56,24},{64,96... | collective-permute-start | bytes 98312 | tf_op jit(solution)/shard_map/ppermute | solution.py:60
  22.4 3.9 %collective-permute-start.5 = (bf16[2,64,128]{2,1,0:T(8,128)(2,1)S(1)}, bf16[2,64,128]{2,1,0:T(8,128)(2,1)S(1)}, u32[]{:S(2)}, u32[]{:S(2)}) collective-permute-start(bf16[2,64,128]{2,1,0:T(8,128)(2,1)S(1)} %copy-done.2), channel_id=1, source_target_pairs={{0,48},{8,56},{16,0},{24,8},{32,16},{40,24},{48,32},{56,40},{64,11... | collective-permute-start | bytes 98312 | tf_op jit(solution)/shard_map/ppermute | solution.py:60
  26.3 2.8 %collective-permute-start.9 = (bf16[4,2,128,128]{3,2,1,0:T(8,128)(2,1)S(1)}, bf16[4,2,128,128]{3,2,1,0:T(8,128)(2,1)S(1)}, u32[]{:S(2)}, u32[]{:S(2)}) collective-permute-start(bf16[4,2,128,128]{3,2,1,0:T(8,128)(2,1)S(1)} %shard_map.189.refs_7_), channel_id=1, source_target_pairs={{0,8},{8,0},{16,24},{24,16},{32,40},{40,32},{48,56},{56,48},{64,72... | collective-permute-start | bytes 786440 | tf_op jit(solution)/shard_map/ppermute | solution.py:64
  26.9 2.2 %collective-permute-start.12 = (bf16[4,2,128,128]{3,2,1,0:T(8,128)(2,1)S(1)}, bf16[4,2,128,128]{3,2,1,0:T(8,128)(2,1)S(1)}, u32[]{:S(2)}, u32[]{:S(2)}) collective-permute-start(bf16[4,2,128,128]{3,2,1,0:T(8,128)(2,1)S(1)} %collective-permute-done.8.refs_10_), channel_id=1, source_target_pairs={{0,8},{8,0},{16,24},{24,16},{32,40},{40,32},{48,56},{56,48},{64,72... | collective-permute-start | bytes 786440 | tf_op jit(solution)/shard_map/ppermute | solution.py:64
  26.9 2.2 %collective-permute-start.11 = (bf16[4,2,128,128]{3,2,1,0:T(8,128)(2,1)S(1)}, bf16[4,2,128,128]{3,2,1,0:T(8,128)(2,1)S(1)}, u32[]{:S(2)}, u32[]{:S(2)}) collective-permute-start(bf16[4,2,128,128]{3,2,1,0:T(8,128)(2,1)S(1)} %collective-permute-done.7.refs_9_), channel_id=1, source_target_pairs={{0,8},{8,0},{16,24},{24,16},{32,40},{40,32},{48,56},{56,48},{64,72... | collective-permute-start | bytes 786440 | tf_op jit(solution)/shard_map/ppermute | solution.py:64
  27.5 1.7 %collective-permute-start.10 = (bf16[4,2,128,128]{3,2,1,0:T(8,128)(2,1)S(1)}, bf16[4,2,128,128]{3,2,1,0:T(8,128)(2,1)S(1)}, u32[]{:S(2)}, u32[]{:S(2)}) collective-permute-start(bf16[4,2,128,128]{3,2,1,0:T(8,128)(2,1)S(1)} %collective-permute-done.6.refs_8_), channel_id=1, source_target_pairs={{0,8},{8,0},{16,24},{24,16},{32,40},{40,32},{48,56},{56,48},{64,72... | collective-permute-start | bytes 786440 | tf_op jit(solution)/shard_map/ppermute | solution.py:64
  40.7 12.9 %copy-start.7 = (bf16[128,1024]{1,0:T(8,128)(2,1)S(1)}, bf16[128,1024]{1,0:T(8,128)(2,1)}, u32[]{:S(2)}) copy-start(bf16[128,1024]{1,0:T(8,128)(2,1)} %refs_5_.1) | copy-start | bytes 786436
  40.7 12.9 %copy-start.8 = (bf16[128,1024]{1,0:T(8,128)(2,1)S(1)}, bf16[128,1024]{1,0:T(8,128)(2,1)}, u32[]{:S(2)}) copy-start(bf16[128,1024]{1,0:T(8,128)(2,1)} %refs_6_.3) | copy-start | bytes 786436
  40.7 11.0 %collective-permute-start.13 = (bf16[4096,128]{1,0:T(8,128)(2,1)S(1)}, bf16[4096,128]{1,0:T(8,128)(2,1)S(1)}, u32[]{:S(2)}, u32[]{:S(2)}) collective-permute-start(bf16[4096,128]{1,0:T(8,128)(2,1)S(1)} %get-tuple-element.85), channel_id=1, source_target_pairs={{0,8},{8,0},{16,24},{24,16},{32,40},{40,32},{48,56},{56,48},{64,72... | collective-permute-start | bytes 3145736 | tf_op jit(solution)/shard_map/ppermute | solution.py:64
  41.2 9.7 %collective-permute-start.16 = (bf16[4,2,64,128]{3,2,1,0:T(8,128)(2,1)S(1)}, bf16[4,2,64,128]{3,2,1,0:T(8,128)(2,1)S(1)}, u32[]{:S(2)}, u32[]{:S(2)}) collective-permute-start(bf16[4,2,64,128]{3,2,1,0:T(8,128)(2,1)S(1)} %shard_map.190.refs_0_), channel_id=1, source_target_pairs={{0,192},{8,200},{16,208},{24,216},{32,224},{40,232},{48,240},{56,2... | collective-permute-start | bytes 393224 | tf_op jit(solution)/shard_map/ppermute | solution.py:56
  41.2 9.7 %collective-permute-start.15 = (bf16[4,2,64,128]{3,2,1,0:T(8,128)(2,1)S(1)}, bf16[4,2,64,128]{3,2,1,0:T(8,128)(2,1)S(1)}, u32[]{:S(2)}, u32[]{:S(2)}) collective-permute-start(bf16[4,2,64,128]{3,2,1,0:T(8,128)(2,1)S(1)} %shard_map.190.refs_0_), channel_id=1, source_target_pairs={{0,128},{8,136},{16,144},{24,152},{32,160},{40,168},{48,176},{56,1... | collective-permute-start | bytes 393224 | tf_op jit(solution)/shard_map/ppermute | solution.py:56
  41.2 10.3 %collective-permute-start.14 = (bf16[4,2,64,128]{3,2,1,0:T(8,128)(2,1)S(1)}, bf16[4,2,64,128]{3,2,1,0:T(8,128)(2,1)S(1)}, u32[]{:S(2)}, u32[]{:S(2)}) collective-permute-start(bf16[4,2,64,128]{3,2,1,0:T(8,128)(2,1)S(1)} %shard_map.190.refs_0_), channel_id=1, source_target_pairs={{0,64},{8,72},{16,80},{24,88},{32,96},{40,104},{48,112},{56,120},{... | collective-permute-start | bytes 393224 | tf_op jit(solution)/shard_map/ppermute | solution.py:56
  51.5 2.0 %collective-permute-start.17 = (bf16[4,4,2,64,128]{4,3,2,1,0:T(8,128)(2,1)S(1)}, bf16[4,4,2,64,128]{4,3,2,1,0:T(8,128)(2,1)S(1)}, u32[]{:S(2)}, u32[]{:S(2)}) collective-permute-start(bf16[4,4,2,64,128]{4,3,2,1,0:T(8,128)(2,1)S(1)} %shard_map.193.refs_7_), channel_id=1, source_target_pairs={{0,8},{8,0},{16,24},{24,16},{32,40},{40,32},{48,56},{56,48},{64,72... | collective-permute-start | bytes 1572872 | tf_op jit(solution)/shard_map/ppermute | solution.py:64
  53.6 8.7 %copy-start.11 = (bf16[2,2,1024,128]{3,2,1,0:T(8,128)(2,1)S(1)}, bf16[2,2,1024,128]{3,2,1,0:T(8,128)(2,1)}, u32[]{:S(2)}) copy-start(bf16[2,2,1024,128]{3,2,1,0:T(8,128)(2,1)} %get-tuple-element.115) | copy-start | bytes 3145732
  53.6 10.2 %copy-start.10 = (bf16[2,2,1024,128]{3,2,1,0:T(8,128)(2,1)S(1)}, bf16[2,2,1024,128]{3,2,1,0:T(8,128)(2,1)}, u32[]{:S(2)}) copy-start(bf16[2,2,1024,128]{3,2,1,0:T(8,128)(2,1)} %get-tuple-element.116) | copy-start | bytes 3145732
  53.6 11.3 %copy-start.9 = (bf16[2,2,1024,128]{3,2,1,0:T(8,128)(2,1)S(1)}, bf16[2,2,1024,128]{3,2,1,0:T(8,128)(2,1)}, u32[]{:S(2)}) copy-start(bf16[2,2,1024,128]{3,2,1,0:T(8,128)(2,1)} %get-tuple-element.117) | copy-start | bytes 3145732
  62.1 64.0 %copy-start = (bf16[2,2,1024,128]{3,2,1,0:T(8,128)(2,1)S(1)}, bf16[2,2,1024,128]{3,2,1,0:T(8,128)(2,1)}, u32[]{:S(2)}) copy-start(bf16[2,2,1024,128]{3,2,1,0:T(8,128)(2,1)} %get-tuple-element.69.refs_4_) | copy-start | bytes 3145732
  62.1 12.6 %collective-permute-start.18 = (bf16[2064,128]{1,0:T(8,128)(2,1)S(1)}, bf16[2064,128]{1,0:T(8,128)(2,1)S(1)}, u32[]{:S(2)}, u32[]{:S(2)}) collective-permute-start(bf16[2064,128]{1,0:T(8,128)(2,1)S(1)} %get-tuple-element.93), channel_id=1, source_target_pairs={{0,8},{8,0},{16,24},{24,16},{32,40},{40,32},{48,56},{56,48},{64,72... | collective-permute-start | bytes 1585160 | tf_op jit(solution)/shard_map/ppermute | solution.py:64
  62.3 59.5 %collective-permute-start.34 = (bf16[2,2,1024,128]{3,2,1,0:T(8,128)(2,1)S(1)}, bf16[2,2,1024,128]{3,2,1,0:T(8,128)(2,1)S(1)}, u32[]{:S(2)}, u32[]{:S(2)}) collective-permute-start(bf16[2,2,1024,128]{3,2,1,0:T(8,128)(2,1)S(1)} %copy-done.11), channel_id=1, source_target_pairs={{0,1},{1,2},{2,3},{3,0},{4,5},{5,6},{6,7},{7,4},{8,9},{9,10},{10,1... | collective-permute-start | bytes 3145736 | tf_op jit(solution)/shard_map/ppermute | solution.py:69
  63.8 58.3 %collective-permute-start.35 = (bf16[2,2,1024,128]{3,2,1,0:T(8,128)(2,1)S(1)}, bf16[2,2,1024,128]{3,2,1,0:T(8,128)(2,1)S(1)}, u32[]{:S(2)}, u32[]{:S(2)}) collective-permute-start(bf16[2,2,1024,128]{3,2,1,0:T(8,128)(2,1)S(1)} %copy-done.10), channel_id=1, source_target_pairs={{0,2},{1,3},{2,0},{3,1},{4,6},{5,7},{6,4},{7,5},{8,10},{9,11},{10,... | collective-permute-start | bytes 3145736 | tf_op jit(solution)/shard_map/ppermute | solution.py:69
  64.9 57.2 %collective-permute-start.36 = (bf16[2,2,1024,128]{3,2,1,0:T(8,128)(2,1)S(1)}, bf16[2,2,1024,128]{3,2,1,0:T(8,128)(2,1)S(1)}, u32[]{:S(2)}, u32[]{:S(2)}) collective-permute-start(bf16[2,2,1024,128]{3,2,1,0:T(8,128)(2,1)S(1)} %copy-done.9), channel_id=1, source_target_pairs={{0,3},{1,0},{2,1},{3,2},{4,7},{5,4},{6,5},{7,6},{8,11},{9,8},{10,9... | collective-permute-start | bytes 3145736 | tf_op jit(solution)/shard_map/ppermute | solution.py:69
  67.0 7.7 %collective-permute-start.19 = (bf16[1024,128]{1,0:T(8,128)(2,1)S(1)}, bf16[1024,128]{1,0:T(8,128)(2,1)S(1)}, u32[]{:S(2)}, u32[]{:S(2)}) collective-permute-start(bf16[1024,128]{1,0:T(8,128)(2,1)S(1)} %get-tuple-element.96), channel_id=1, source_target_pairs={{0,64},{8,72},{16,80},{24,88},{32,96},{40,104},{48,112},{56,120},{... | collective-permute-start | bytes 786440 | tf_op jit(solution)/shard_map/ppermute | solution.py:56
  74.8 10.7 %collective-permute-start.20 = (bf16[1024,128]{1,0:T(8,128)(2,1)S(1)}, bf16[1024,128]{1,0:T(8,128)(2,1)S(1)}, u32[]{:S(2)}, u32[]{:S(2)}) collective-permute-start(bf16[1024,128]{1,0:T(8,128)(2,1)S(1)} %get-tuple-element.97), channel_id=1, source_target_pairs={{0,128},{8,136},{16,144},{24,152},{32,160},{40,168},{48,176},{56,1... | collective-permute-start | bytes 786440 | tf_op jit(solution)/shard_map/ppermute | solution.py:56
  74.8 13.7 %collective-permute-start.21 = (bf16[1024,128]{1,0:T(8,128)(2,1)S(1)}, bf16[1024,128]{1,0:T(8,128)(2,1)S(1)}, u32[]{:S(2)}, u32[]{:S(2)}) collective-permute-start(bf16[1024,128]{1,0:T(8,128)(2,1)S(1)} %get-tuple-element.98), channel_id=1, source_target_pairs={{0,192},{8,200},{16,208},{24,216},{32,224},{40,232},{48,240},{56,2... | collective-permute-start | bytes 786440 | tf_op jit(solution)/shard_map/ppermute | solution.py:56
  85.5 6.3 %collective-permute-start.22 = (bf16[528,128]{1,0:T(8,128)(2,1)S(1)}, bf16[528,128]{1,0:T(8,128)(2,1)S(1)}, u32[]{:S(2)}, u32[]{:S(2)}) collective-permute-start(bf16[528,128]{1,0:T(8,128)(2,1)S(1)} %get-tuple-element.101), channel_id=1, source_target_pairs={{0,64},{8,72},{16,80},{24,88},{32,96},{40,104},{48,112},{56,120},{... | collective-permute-start | bytes 405512 | tf_op jit(solution)/shard_map/ppermute | solution.py:56
  88.5 8.0 %collective-permute-start.23 = (bf16[528,128]{1,0:T(8,128)(2,1)S(1)}, bf16[528,128]{1,0:T(8,128)(2,1)S(1)}, u32[]{:S(2)}, u32[]{:S(2)}) collective-permute-start(bf16[528,128]{1,0:T(8,128)(2,1)S(1)} %get-tuple-element.102), channel_id=1, source_target_pairs={{0,128},{8,136},{16,144},{24,152},{32,160},{40,168},{48,176},{56,1... | collective-permute-start | bytes 405512 | tf_op jit(solution)/shard_map/ppermute | solution.py:56
  91.8 10.4 %collective-permute-start.24 = (bf16[528,128]{1,0:T(8,128)(2,1)S(1)}, bf16[528,128]{1,0:T(8,128)(2,1)S(1)}, u32[]{:S(2)}, u32[]{:S(2)}) collective-permute-start(bf16[528,128]{1,0:T(8,128)(2,1)S(1)} %get-tuple-element.103), channel_id=1, source_target_pairs={{0,192},{8,200},{16,208},{24,216},{32,224},{40,232},{48,240},{56,2... | collective-permute-start | bytes 405512 | tf_op jit(solution)/shard_map/ppermute | solution.py:56
  96.5 7.6 %collective-permute-start.28 = (bf16[256,128]{1,0:T(8,128)(2,1)S(1)}, bf16[256,128]{1,0:T(8,128)(2,1)S(1)}, u32[]{:S(2)}, u32[]{:S(2)}) collective-permute-start(bf16[256,128]{1,0:T(8,128)(2,1)S(1)} %get-tuple-element.109), channel_id=1, source_target_pairs={{0,16},{8,24},{16,32},{24,40},{32,48},{40,56},{48,0},{56,8},{64,80... | collective-permute-start | bytes 196616 | tf_op jit(solution)/shard_map/ppermute | solution.py:60
  102.3 6.3 %collective-permute-start.25 = (bf16[144,128]{1,0:T(8,128)(2,1)S(1)}, bf16[144,128]{1,0:T(8,128)(2,1)S(1)}, u32[]{:S(2)}, u32[]{:S(2)}) collective-permute-start(bf16[144,128]{1,0:T(8,128)(2,1)S(1)} %get-tuple-element.105), channel_id=1, source_target_pairs={{0,16},{8,24},{16,32},{24,40},{32,48},{40,56},{48,0},{56,8},{64,80... | collective-permute-start | bytes 110600 | tf_op jit(solution)/shard_map/ppermute | solution.py:60
  104.1 6.4 %collective-permute-start.26 = (bf16[144,128]{1,0:T(8,128)(2,1)S(1)}, bf16[144,128]{1,0:T(8,128)(2,1)S(1)}, u32[]{:S(2)}, u32[]{:S(2)}) collective-permute-start(bf16[144,128]{1,0:T(8,128)(2,1)S(1)} %get-tuple-element.106), channel_id=1, source_target_pairs={{0,32},{8,40},{16,48},{24,56},{32,0},{40,8},{48,16},{56,24},{64,96... | collective-permute-start | bytes 110600 | tf_op jit(solution)/shard_map/ppermute | solution.py:60
  108.5 4.9 %collective-permute-start.27 = (bf16[144,128]{1,0:T(8,128)(2,1)S(1)}, bf16[144,128]{1,0:T(8,128)(2,1)S(1)}, u32[]{:S(2)}, u32[]{:S(2)}) collective-permute-start(bf16[144,128]{1,0:T(8,128)(2,1)S(1)} %get-tuple-element.107), channel_id=1, source_target_pairs={{0,48},{8,56},{16,0},{24,8},{32,16},{40,24},{48,32},{56,40},{64,11... | collective-permute-start | bytes 110600 | tf_op jit(solution)/shard_map/ppermute | solution.py:60
  110.5 5.9 %collective-permute-start.29 = (bf16[256,128]{1,0:T(8,128)(2,1)S(1)}, bf16[256,128]{1,0:T(8,128)(2,1)S(1)}, u32[]{:S(2)}, u32[]{:S(2)}) collective-permute-start(bf16[256,128]{1,0:T(8,128)(2,1)S(1)} %get-tuple-element.110), channel_id=1, source_target_pairs={{0,32},{8,40},{16,48},{24,56},{32,0},{40,8},{48,16},{56,24},{64,96... | collective-permute-start | bytes 196616 | tf_op jit(solution)/shard_map/ppermute | solution.py:60
  113.4 4.3 %collective-permute-start.30 = (bf16[256,128]{1,0:T(8,128)(2,1)S(1)}, bf16[256,128]{1,0:T(8,128)(2,1)S(1)}, u32[]{:S(2)}, u32[]{:S(2)}) collective-permute-start(bf16[256,128]{1,0:T(8,128)(2,1)S(1)} %get-tuple-element.111), channel_id=1, source_target_pairs={{0,48},{8,56},{16,0},{24,8},{32,16},{40,24},{48,32},{56,40},{64,11... | collective-permute-start | bytes 196616 | tf_op jit(solution)/shard_map/ppermute | solution.py:60
  118.3 4.3 %collective-permute-start.31 = (bf16[272,128]{1,0:T(8,128)(2,1)S(1)}, bf16[272,128]{1,0:T(8,128)(2,1)S(1)}, u32[]{:S(2)}, u32[]{:S(2)}) collective-permute-start(bf16[272,128]{1,0:T(8,128)(2,1)S(1)} %get-tuple-element.118.refs_0_), channel_id=1, source_target_pairs={{0,1},{1,2},{2,3},{3,0},{4,5},{5,6},{6,7},{7,4},{8,9},{9,10},{10,1... | collective-permute-start | bytes 208904 | tf_op jit(solution)/shard_map/ppermute | solution.py:69
  118.3 5.8 %collective-permute-start.32 = (bf16[272,128]{1,0:T(8,128)(2,1)S(1)}, bf16[272,128]{1,0:T(8,128)(2,1)S(1)}, u32[]{:S(2)}, u32[]{:S(2)}) collective-permute-start(bf16[272,128]{1,0:T(8,128)(2,1)S(1)} %get-tuple-element.118.refs_0_), channel_id=1, source_target_pairs={{0,2},{1,3},{2,0},{3,1},{4,6},{5,7},{6,4},{7,5},{8,10},{9,11},{10,... | collective-permute-start | bytes 208904 | tf_op jit(solution)/shard_map/ppermute | solution.py:69
  121.8 4.3 %collective-permute-start.33 = (bf16[272,128]{1,0:T(8,128)(2,1)S(1)}, bf16[272,128]{1,0:T(8,128)(2,1)S(1)}, u32[]{:S(2)}, u32[]{:S(2)}) collective-permute-start(bf16[272,128]{1,0:T(8,128)(2,1)S(1)} %get-tuple-element.118.refs_0_), channel_id=1, source_target_pairs={{0,3},{1,0},{2,1},{3,2},{4,7},{5,4},{6,5},{7,6},{8,11},{9,8},{10,9... | collective-permute-start | bytes 208904 | tf_op jit(solution)/shard_map/ppermute | solution.py:69
  126.8 14.9 %collective-permute-start.37 = (bf16[1040,128]{1,0:T(8,128)(2,1)S(1)}, bf16[1040,128]{1,0:T(8,128)(2,1)S(1)}, u32[]{:S(2)}, u32[]{:S(2)}) collective-permute-start(bf16[1040,128]{1,0:T(8,128)(2,1)S(1)} %shard_map.200.near_ref), channel_id=1, source_target_pairs={{0,4},{1,5},{2,6},{3,7},{4,0},{5,1},{6,2},{7,3},{8,12},{9,13},{10,... | collective-permute-start | bytes 798728 | tf_op jit(solution)/shard_map/ppermute | solution.py:73
  (2 other events, 12.1 us)
